TPU v7x, 128 devices: a whole 4x4x4 slice. The times are simulated.
128 devices in a mesh: gx: 16 (over y_lo, z, core), gy: 8 (over y_hi, x).
Axes of the slice: x: 4, y: 4 (y_hi: 2, y_lo: 2; y = y_hi * 2 + y_lo), z: 4, core: 2. Of those that a mesh axis runs over, the one named last changes fastest.
Arguments:
- particle_locations: float32 [3, 2097152], P(None, ('gx', 'gy')), may hold values from -3 to 3
- particle_speeds: float32 [3, 2097152], P(None, ('gx', 'gy')), may hold values from -3 to 3
- particle_bulk: float32 [2097152], P(('gx', 'gy')), may hold values from 0.5 to 2
- receiving_group_per_pair: int32 [32768], P(('gx', 'gy')), may hold values from 0 to 16383, as said below
- emitting_group_per_pair: int32 [32768], P(('gx', 'gy')), may hold values from 0 to 16383, as said below
- active_pair_slots: int32 [128], P(('gx', 'gy')), may hold values from 2 to 256, as said below
- landing_site_triple: int32 [3, 2097152], P(None, ('gx', 'gy')), may hold values from 0 to 4095, as said below
- landing_weight_octants: int32 [2097152], P(('gx', 'gy')), may hold values from 1 to 8
- thermal_excess: float32 [64, 512, 4096], P(None, 'gx', 'gy'), may hold values from -6 to 6
- molten_strip_midlines: int32 [2], replicated, may hold values from 0 to 511
Outputs:
- advanced_locations: float32 [3, 2097152], P(None, ('gx', 'gy'))
- advanced_speeds: float32 [3, 2097152], P(None, ('gx', 'gy'))
- packing_share_per_site: float32 [64, 512, 4096], P(None, 'gx', 'gy')
- advanced_thermal_excess: float32 [64, 512, 4096], P(None, 'gx', 'gy')
Inputs may be any that keep to these rules, and one draw needn't show every extreme that they name: `receiving_group_per_pair`: slots t of device k = t div 256 have a target block among that device's blocks k * 128 to (k + 1) * 128 - 1. For every slot, emitting_group_per_pair differs from receiving_group_per_pair by at most 2; the difference 2 is reached in both directions. `active_pair_slots`: slots at or past a device's count are not live and hold arbitrary blocks that still satisfy the other promises; some device has all 256 slots live. `landing_site_triple`: particle p of device k = p div 16384 (device row r = p div 131072, column c = k mod 8) deposits into grid rows r * 32 - 16 to (r + 1) * 32 + 15 and columns c * 512 to (c + 1) * 512 - 1; both row limits are reached. At most 4096 of one device's particles lie below its own rows and at most 4096 above them, and both counts 4096 are reached.
All inputs are finite; a program needn't handle non-finite values.
Results may differ from a plain program's by a relative error of at most 0.0003.
Values sent between devices are 32-bit elements; how exact they have to be, the bound alone decides.
No kernel may reach another device: no remote copies, remote signals or barrier semaphores. Data moves between devices by JAX's collectives and lax.ppermute only.
A program may use at most 128 MiB of HBM per device.

v0:
```python
import math

import jax
import jax.numpy as jnp
from jax import lax
from jax.sharding import PartitionSpec as P

G = 16
HB = 2
BAND = 64


stiffness = 0.0078125
damping = 0.00390625
time_step = 0.5
depth_scale = 12.0
conduct = 0.1
laser_power = 0.5


def padded(cells, sides, width):
    for axis, dim in sides:
        count = lax.axis_size(axis)
        ends = count - 1
        head = lax.slice_in_dim(cells, 0, width, axis=dim)
        tail = lax.slice_in_dim(cells, cells.shape[dim] - width, cells.shape[dim], axis=dim)
        cells = jnp.concatenate(
            [
                lax.ppermute(tail, axis, [(i, (i + 1) % count) for i in range(ends)]),
                cells,
                lax.ppermute(head, axis, [((i + 1) % count, i) for i in range(ends)]),
            ],
            axis=dim,
        )
    return cells


def from_behind(value, axis, steps):
    count = lax.axis_size(axis)
    first, last = (max(0, -steps), min(count, count - steps))
    return lax.ppermute(value, axis, [(source, source + steps) for source in range(first, last)])


def tile_force(target, source):
    offset = target[:, 0:3, :, None] - source[:, 0:3, None, :]
    weight = jnp.exp(-0.5 * jnp.sum(offset * offset, axis=1))
    relative = target[:, 3:6, :, None] - source[:, 3:6, None, :]
    repulse = jnp.sum(weight[:, None] * offset, axis=3)
    friction = jnp.sum(weight[:, None] * relative, axis=3)
    return stiffness * repulse - damping * friction


def neighbours(array):
    return (
        array[2:, 1:-1, 1:-1],
        array[:-2, 1:-1, 1:-1],
        array[1:-1, 2:, 1:-1],
        array[1:-1, :-2, 1:-1],
        array[1:-1, 1:-1, 2:],
        array[1:-1, 1:-1, :-2],
    )


def thermal_advance(field_now, granular_share, mesh_line_number, band_row):
    conductance = conduct * (1.0 + 0.5 * jnp.tanh(field_now)) / (1.0 + granular_share)
    centre = field_now[1:-1, 1:-1, 1:-1]
    centre_cond = conductance[1:-1, 1:-1, 1:-1]
    change = jnp.zeros_like(centre)
    for near_field, near_cond in zip(neighbours(field_now), neighbours(conductance)):
        change = change + 0.5 * (centre_cond + near_cond) * (near_field - centre)
    beam_row = laser_power * jnp.exp(-jnp.square((mesh_line_number - band_row) / BAND))
    heating = beam_row[None, :, None] * granular_share[1:-1, 1:-1, 1:-1]
    return centre + change + heating


def body(
    particle_locations,
    particle_speeds,
    particle_bulk,
    receiving_group_per_pair,
    emitting_group_per_pair,
    active_pair_slots,
    landing_site_triple,
    landing_weight_octants,
    thermal_excess,
    molten_strip_midlines,
):
    blocks = particle_locations.shape[1] // 128
    first_block = lax.axis_index(("gx", "gy")) * blocks
    states = jnp.concatenate([particle_locations, particle_speeds], axis=0)
    rimmed = padded(states, ((("gx", "gy"), 1),), HB * 128)
    ext_blocks = rimmed.reshape(6, blocks + 2 * HB, 128).transpose(1, 0, 2)
    listed = receiving_group_per_pair.shape[0]
    group_size = math.gcd(listed, 16)
    target_local = (receiving_group_per_pair - first_block).reshape(-1, group_size)
    source_local = (emitting_group_per_pair - first_block + HB).reshape(-1, group_size)
    live_count = active_pair_slots[0]
    block_ids = jnp.arange(blocks, dtype=jnp.int32)

    def add_group(group, running):
        targets = target_local[group]
        sources = source_local[group]
        slot_ids = group * group_size + jnp.arange(group_size, dtype=jnp.int32)
        live_mask = (slot_ids < live_count).astype(jnp.float32)
        pushed = tile_force(ext_blocks[targets + HB], ext_blocks[sources])
        owners = (targets[:, None] == block_ids[None, :]).astype(jnp.float32) * live_mask[:, None]
        return running + jnp.einsum("tb,tcp->bcp", owners, pushed, precision=lax.Precision.HIGHEST)

    empty = jnp.zeros((blocks, 3, 128), jnp.float32)
    summed = lax.fori_loop(0, listed // group_size, add_group, empty)
    forces_all = summed.transpose(1, 0, 2).reshape(3, blocks * 128)
    advanced_speeds = particle_speeds + time_step * forces_all
    advanced_locations = particle_locations + time_step * advanced_speeds
    charge = (
        particle_bulk
        * landing_weight_octants.astype(jnp.float32)
        * 0.125
        * (1.0 + 0.5 * jnp.tanh(advanced_locations[2]))
    )
    downward_site_total = thermal_excess.shape[0]
    patch_lines_total = thermal_excess.shape[1]
    patch_across_total = thermal_excess.shape[2]
    row_start = lax.axis_index("gx") * patch_lines_total
    col_start = lax.axis_index("gy") * patch_across_total
    local_x = landing_site_triple[1] - row_start
    local_y = landing_site_triple[2] - col_start
    levels = jnp.arange(downward_site_total, dtype=jnp.float32)
    padded_rows = patch_lines_total + 2 * G
    cell_code = (local_x + G) * patch_across_total + local_y
    extended = (
        jnp.zeros((downward_site_total, padded_rows * patch_across_total), jnp.float32)
        .at[:, cell_code]
        .add(
            jnp.exp(
                -jnp.square(
                    (levels[:, None] - landing_site_triple[0][None, :].astype(jnp.float32))
                    / depth_scale
                )
            )
            * charge[None, :]
        )
    )
    extended = extended.reshape(downward_site_total, padded_rows, patch_across_total)
    from_above = from_behind(extended[:, :G], "gx", -1)
    from_below = from_behind(extended[:, G + patch_lines_total :], "gx", 1)
    granular_share = extended[:, G : G + patch_lines_total]
    granular_share = granular_share + jnp.pad(
        from_above, ((0, 0), (patch_lines_total - G, 0), (0, 0))
    )
    granular_share = granular_share + jnp.pad(
        from_below, ((0, 0), (0, patch_lines_total - G), (0, 0))
    )
    mesh_line_number = (row_start + jnp.arange(patch_lines_total, dtype=jnp.int32)).astype(
        jnp.float32
    )
    first_band = molten_strip_midlines[0].astype(jnp.float32)
    second_band = molten_strip_midlines[1].astype(jnp.float32)
    piled_sheets = jnp.stack([thermal_excess, granular_share])
    depth_pad = ((0, 0), (1, 1), (0, 0), (0, 0))
    shallow = jnp.pad(padded(piled_sheets, (("gx", 2), ("gy", 3)), 1), depth_pad)
    central_portion = thermal_advance(shallow[0], shallow[1], mesh_line_number, first_band)
    middle_rim = padded(central_portion, (("gx", 1), ("gy", 2)), 1)
    advanced_thermal_excess = thermal_advance(
        jnp.pad(middle_rim, ((1, 1), (0, 0), (0, 0))), shallow[1], mesh_line_number, second_band
    )
    return (advanced_locations, advanced_speeds, granular_share, advanced_thermal_excess)


def solution(mesh):
    placed = (
        P(None, ("gx", "gy")),
        P(None, ("gx", "gy")),
        P(("gx", "gy")),
        P(("gx", "gy")),
        P(("gx", "gy")),
        P(("gx", "gy")),
        P(None, ("gx", "gy")),
        P(("gx", "gy")),
        P(None, "gx", "gy"),
        P(),
    )
    return jax.shard_map(
        body,
        mesh=mesh,
        in_specs=placed,
        out_specs=(
            P(None, ("gx", "gy")),
            P(None, ("gx", "gy")),
            P(None, "gx", "gy"),
            P(None, "gx", "gy"),
        ),
        check_vma=False,
    )
```

profile of v0, /device:TPU:24, one launch (start us, length us, event | category | flops | bytes accessed | tf_op | source)
XLA Modules:
  0.0 453.2 jit_solution(16814781919712620310)
XLA Ops:
  1.4 3.4 collective-permute-start
  4.8 6.1 %collective-permute-start.1 = (f32[6,256]{1,0:T(8,128)S(1)}, f32[6,256]{1,0:T(8,128)S(1)}, u32[]{:S(2)}, u32[]{:S(2)}) collective-permute-start(f32[6,256]{1,0:T(8,128)S(1)} %get-tuple-element.257), channel_id=1, source_target_pairs={{1,0},{2,1},{3,2},{4,3},{5,4},{6,5},{7,6},{8,7},{9,8},{10,9},{11,1... | collective-permute-start | bytes 18440 | tf_op jit(solution)/shard_map/ppermute | solution.py:31
  15.2 119.6 %while.16 = (s32[]{:T(128)}, f32[128,3,128]{2,0,1:T(8,128)S(1)}, s32[16,16]{1,0:T(8,128)S(1)}, s32[]{:T(128)}, f32[132,6,128]{2,1,0:T(8,128)S(1)}, /*index=5*/s3...) while((s32[]{:T(128)}, f32[128,3,128]{2,0,1:T(8,128)S(1)}, s32[16,16]{1,0:T(8,128)S(1)}, ...), condition=%wide.region_4.0_spmd.clone, body=%wide.region_0.0_spmd.clone.sunk | while | flops 16625828 | bytes 5235659 | solution.py:110
  18.4 3.8 fusion.97
  25.8 3.8 fusion.97
  33.3 3.8 fusion.97
  40.8 3.8 fusion.97
  48.3 3.8 fusion.97
  55.7 3.8 fusion.97
  63.2 3.8 fusion.97
  70.7 3.8 fusion.97
  78.1 3.8 fusion.97
  85.6 3.8 fusion.97
  93.1 3.8 fusion.97
  100.6 3.8 fusion.97
  108.0 3.8 fusion.97
  115.5 3.8 fusion.97
  123.0 3.8 fusion.97
  130.5 3.8 fusion.97
  135.9 104.9 %scatter_custom_fusion = f32[64,32768]{0,1:T(8,128)} fusion(s32[16384]{0:T(1024)S(1)} %bitcast.71, f32[]{:T(128)} %constant.130.clone.1, f32[16384]{0:T(1024)S(1)} %multiply_multiply_fusion, f32[]{:T(128)} %constant.142.clone.1, f32[16384]{0:T(1024)S(1)} %bitcast.69), kind=kCustom, calls=%fused_computation.44 | custom fusion | flops 6291456 | bytes 8519688 | tf_op jit(solution)/shard_map/scatter-add | solution.py:133
  240.9 7.8 %fusion.80 = (f32[64,16,512]{0,2,1:T(8,128)}, f32[64,16,512]{0,2,1:T(8,128)}) fusion(f32[64,64,512]{0,2,1:T(8,128)} %bitcast.64), kind=kLoop, calls=%fused_computation.166 | loop fusion | bytes 8388608 | tf_op jit(solution)/shard_map/slice | solution.py:144
  248.6 2.8 copy.88
  251.5 3.8 copy.89
  257.2 6.2 %collective-permute-start.2 = (f32[64,16,512]{2,0,1:T(8,128)S(1)}, f32[64,16,512]{2,0,1:T(8,128)}, u32[]{:S(2)}, u32[]{:S(2)}) collective-permute-start(f32[64,16,512]{2,0,1:T(8,128)S(1)} %copy.88), channel_id=1, source_target_pairs={{8,0},{16,8},{24,16},{32,24},{40,32},{48,40},{56,48},{64,56},{72,6... | collective-permute-start | bytes 6291464 | tf_op jit(solution)/shard_map/ppermute | solution.py:41
  263.4 6.6 %copy.102 = f32[64,32,512]{2,0,1:T(8,128)} copy(f32[64,32,512]{2,1,0:T(8,128)} %param.20) | data formatting | bytes 8388608 | tf_op args[8]
  270.0 7.6 %slice.264 = f32[64,32,512]{0,2,1:T(8,128)} slice(f32[64,64,512]{0,2,1:T(8,128)} %bitcast.65), slice={[0:64], [16:48], [0:512]} | slice | bytes 8388608 | tf_op jit(solution)/shard_map/slice | solution.py:146
  277.6 6.8 %copy.87 = f32[64,32,512]{2,0,1:T(8,128)} copy(f32[64,32,512]{0,2,1:T(8,128)} %slice.264) | data formatting | bytes 8388608
  286.5 4.8 %pad_add_fusion = f32[64,32,512]{2,0,1:T(8,128)S(1)} fusion(f32[64,16,512]{2,0,1:T(8,128)} %collective-permute-done.3, f32[64,32,512]{2,0,1:T(8,128)} %copy.87, f32[64,16,512]{2,0,1:T(8,128)} %collective-permute-done.2), kind=kLoop, calls=%fused_computation.134 | loop fusion | flops 2097152 | bytes 12582912 | tf_op jit(solution)/shard_map/add | solution.py:150
  291.3 2.1 collective-permute-start.4
  293.4 5.9 %collective-permute-start.5 = (f32[2,64,1,512]{3,1,2,0:T(8,128)S(1)}, f32[2,64,1,512]{3,1,2,0:T(8,128)S(1)}, u32[]{:S(2)}, u32[]{:S(2)}) collective-permute-start(f32[2,64,1,512]{3,1,2,0:T(8,128)S(1)} %get-tuple-element.251), channel_id=1, source_target_pairs={{8,0},{16,8},{24,16},{32,24},{40,32},{48,40},{56,48},{64,56},{72,6... | collective-permute-start | bytes 786440 | tf_op jit(solution)/shard_map/ppermute | solution.py:31
  303.2 2.2 pad_maximum_fusion.11
  305.4 2.4 copy.75
  308.5 6.0 %collective-permute-start.7 = (f32[2,64,34,1]{1,0,3,2:T(2,128)S(1)}, f32[2,64,34,1]{1,0,3,2:T(2,128)S(1)}, u32[]{:S(2)}, u32[]{:S(2)}) collective-permute-start(f32[2,64,34,1]{1,0,3,2:T(2,128)S(1)} %copy.76), channel_id=1, source_target_pairs={{1,0},{2,1},{3,2},{4,3},{5,4},{6,5},{7,6},{9,8},{10,9},{11,10},{12... | collective-permute-start | bytes 52232 | tf_op jit(solution)/shard_map/ppermute | solution.py:31
  314.6 2.1 collective-permute-start.6
  316.7 7.3 %collective-permute-done.6 = f32[2,64,34,1]{1,0,3,2:T(2,128)S(1)} collective-permute-done((f32[2,64,34,1]{1,0,3,2:T(2,128)S(1)}, f32[2,64,34,1]{1,0,3,2:T(2,128)S(1)}, u32[]{:S(2)}, u32[]{:S(2)}) %collective-permute-start.6) | collective-permute-done | bytes 17440 | tf_op jit(solution)/shard_map/ppermute | solution.py:29
  324.7 2.1 copy.78
  326.9 14.0 %select_maximum_fusion = f32[2,66,34,514]{3,1,2,0:T(8,128)S(1)} fusion(f32[2,64,34,1]{3,1,2,0:T(8,128)} %copy.78, f32[2,64,34,1]{3,1,2,0:T(8,128)S(1)} %copy.77, f32[2,64,1,512]{3,1,2,0:T(8,128)S(1)} %collective-permute-done.5, f32[2,64,1,512]{3,1,2,0:T(8,128)S(1)} %collective-permute-done.4, f32[1,64,32,512]{3,1,2,0:T(8,128)} %bitcast.63, ...), kind=kLoop, calls=%fused_computation.36 | loop fusion | flops 32295648 | bytes 18175040 | tf_op jit(solution)/shard_map/concatenate | solution.py:27
  340.8 4.5 copy-done
  345.3 2.1 multiply_divide_fusion.1
  347.4 9.9 %slice_bitcast_fusion = (f32[66,34,514]{2,0,1:T(8,128)}, f32[66,34,514]{2,0,1:T(8,128)}) fusion(f32[2,66,34,514]{3,1,2,0:T(8,128)} %copy-done), kind=kLoop, calls=%fused_computation.58 | loop fusion | bytes 18454656 | tf_op jit(solution)/shard_map/squeeze | solution.py:161
  357.3 26.5 %fusion.57 = f32[64,32,512]{2,0,1:T(8,128)S(1)} fusion(f32[66,34,514]{2,0,1:T(8,128)} %get-tuple-element.247, f32[66,34,514]{2,0,1:T(8,128)S(1)} %multiply_divide_fusion.1, f32[66,34,514]{2,0,1:T(8,128)} %get-tuple-element.246, f32[32]{0:T(128)S(1)} %exponential_multiply_fusion.1), kind=kLoop, calls=%fused_computation.106 | loop fusion | flops 33554432 | bytes 67108992 | tf_op jit(solution)/shard_map/add | solution.py:73
  385.8 5.8 %collective-permute-start.9 = (f32[64,1,512]{2,0,1:T(8,128)S(1)}, f32[64,1,512]{2,0,1:T(8,128)S(1)}, u32[]{:S(2)}, u32[]{:S(2)}) collective-permute-start(f32[64,1,512]{2,0,1:T(8,128)S(1)} %get-tuple-element.255), channel_id=1, source_target_pairs={{8,0},{16,8},{24,16},{32,24},{40,32},{48,40},{56,48},{64,56},{72,6... | collective-permute-start | bytes 393224 | tf_op jit(solution)/shard_map/ppermute | solution.py:31
  395.4 1.9 collective-permute-start.10
  397.3 7.7 %collective-permute-start.11 = (f32[64,34,1]{0,1,2:T(8,128)S(1)}, f32[64,34,1]{0,1,2:T(8,128)S(1)}, u32[]{:S(2)}, u32[]{:S(2)}) collective-permute-start(f32[64,34,1]{0,1,2:T(8,128)S(1)} %copy.80), channel_id=1, source_target_pairs={{1,0},{2,1},{3,2},{4,3},{5,4},{6,5},{7,6},{9,8},{10,9},{11,10},{12... | collective-permute-start | bytes 26120 | tf_op jit(solution)/shard_map/ppermute | solution.py:31
  405.1 6.6 %copy.85 = f32[64,32,512]{2,1,0:T(8,128)} copy(f32[64,32,512]{2,0,1:T(8,128)} %copy-done.1) | data formatting | bytes 8388608
  412.6 11.3 %multiply_divide_fusion = (f32[66,34,514]{2,0,1:T(8,128)S(1)}, f32[66,34,514]{2,0,1:T(8,128)}) fusion(f32[2,66,34,514]{3,1,2,0:T(8,128)} %copy-done, f32[64,34,1]{2,0,1:T(8,128)S(1)} %copy.82, f32[64,1,512]{2,0,1:T(8,128)S(1)} %collective-permute-done.9, f32[64,32,512]{2,0,1:T(8,128)} %copy-done.2, f32[64,1,512]{2,0,1:T(8,128)S(1)} %collective-permute-done.8, ...), kind=kLoop, calls=%fused_computation.60 | loop fusion | flops 19608072 | bytes 18314848 | tf_op jit(solution)/shard_map/div | solution.py:65
  423.9 22.5 %fusion.35 = f32[64,32,512]{2,0,1:T(8,128)} fusion(f32[64,32,512]{2,0,1:T(8,128)S(1)} %copy-done.3, f32[64,34,1]{2,0,1:T(8,128)S(1)} %copy.81, f32[64,1,512]{2,0,1:T(8,128)S(1)} %collective-permute-done.9, f32[64,1,512]{2,0,1:T(8,128)S(1)} %collective-permute-done.8, f32[66,34,514]{2,0,1:T(8,128)S(1)} %get-tuple-element.234, f32[64,34,1]{2,0,1:T(8,128)S(1)} %copy.82, ...), kind=kLoop, calls=%fused_computation.68 | loop fusion | flops 41943040 | bytes 50611328 | tf_op jit(solution)/shard_map/add | solution.py:73
  446.3 6.6 %copy.86 = f32[64,32,512]{2,1,0:T(8,128)} copy(f32[64,32,512]{2,0,1:T(8,128)} %fusion.35) | data formatting | bytes 8388608
  (250 shorter events, 77.2 us)
Async XLA Ops:
  1.4 12.6 %collective-permute-start = (f32[6,256]{1,0:T(8,128)S(1)}, f32[6,256]{1,0:T(8,128)S(1)}, u32[]{:S(2)}, u32[]{:S(2)}) collective-permute-start(f32[6,256]{1,0:T(8,128)S(1)} %get-tuple-element.256), channel_id=1, source_target_pairs={{0,1},{1,2},{2,3},{3,4},{4,5},{5,6},{6,7},{7,8},{8,9},{9,10},{10,1... | collective-permute-start | bytes 18440 | tf_op jit(solution)/shard_map/ppermute | solution.py:29
  4.8 9.2 %collective-permute-start.1 = (f32[6,256]{1,0:T(8,128)S(1)}, f32[6,256]{1,0:T(8,128)S(1)}, u32[]{:S(2)}, u32[]{:S(2)}) collective-permute-start(f32[6,256]{1,0:T(8,128)S(1)} %get-tuple-element.257), channel_id=1, source_target_pairs={{1,0},{2,1},{3,2},{4,3},{5,4},{6,5},{7,6},{8,7},{9,8},{10,9},{11,1... | collective-permute-start | bytes 18440 | tf_op jit(solution)/shard_map/ppermute | solution.py:31
  15.1 119.7 %copy-start.5 = (f32[3,16384]{1,0:T(4,128)S(1)}, f32[3,16384]{1,0:T(4,128)}, u32[]{:S(2)}) copy-start(f32[3,16384]{1,0:T(4,128)} %param.12) | copy-start | bytes 589828
  15.1 119.7 %copy-start.6 = (f32[3,16384]{1,0:T(4,128)S(1)}, f32[3,16384]{1,0:T(4,128)}, u32[]{:S(2)}) copy-start(f32[3,16384]{1,0:T(4,128)} %param.13) | copy-start | bytes 589828
  15.1 120.7 %copy-start.8 = (f32[16384]{0:T(1024)S(1)}, f32[16384]{0:T(1024)}, u32[]{:S(2)}) copy-start(f32[16384]{0:T(1024)} %param.14) | copy-start | bytes 196612
  15.2 120.7 %copy-start.9 = (s32[16384]{0:T(1024)S(1)}, s32[16384]{0:T(1024)}, u32[]{:S(2)}) copy-start(s32[16384]{0:T(1024)} %param.19) | copy-start | bytes 196612
  135.8 105.1 %copy-start.7 = (f32[3,16384]{1,0:T(4,128)}, f32[3,16384]{1,0:T(4,128)S(1)}, u32[]{:S(2)}) copy-start(f32[3,16384]{1,0:T(4,128)S(1)} %get-tuple-element.236) | copy-start | bytes 589828
  255.3 29.8 %collective-permute-start.3 = (f32[64,16,512]{2,0,1:T(8,128)}, f32[64,16,512]{2,0,1:T(8,128)}, u32[]{:S(2)}, u32[]{:S(2)}) collective-permute-start(f32[64,16,512]{2,0,1:T(8,128)} %copy.89), channel_id=1, source_target_pairs={{0,8},{8,16},{16,24},{24,32},{32,40},{40,48},{48,56},{56,64},{64,7... | collective-permute-start | bytes 6291464 | tf_op jit(solution)/shard_map/ppermute | solution.py:41
  257.2 29.3 %collective-permute-start.2 = (f32[64,16,512]{2,0,1:T(8,128)S(1)}, f32[64,16,512]{2,0,1:T(8,128)}, u32[]{:S(2)}, u32[]{:S(2)}) collective-permute-start(f32[64,16,512]{2,0,1:T(8,128)S(1)} %copy.88), channel_id=1, source_target_pairs={{8,0},{16,8},{24,16},{32,24},{40,32},{48,40},{56,48},{64,56},{72,6... | collective-permute-start | bytes 6291464 | tf_op jit(solution)/shard_map/ppermute | solution.py:41
  284.4 6.9 %copy-start.4 = (f32[64,32,512]{2,0,1:T(8,128)S(1)}, f32[64,32,512]{2,0,1:T(8,128)}, u32[]{:S(2)}) copy-start(f32[64,32,512]{2,0,1:T(8,128)} %copy.102) | copy-start | bytes 12582916
  291.3 11.9 %copy-start.1 = (f32[64,32,512]{2,0,1:T(8,128)}, f32[64,32,512]{2,0,1:T(8,128)S(1)}, u32[]{:S(2)}) copy-start(f32[64,32,512]{2,0,1:T(8,128)S(1)} %pad_add_fusion) | copy-start | bytes 12582916
  291.3 8.0 %copy-start.10 = (s32[2]{0:T(128)S(1)}, s32[2]{0:T(128)}, u32[]{:S(2)}) copy-start(s32[2]{0:T(128)} %param.21) | copy-start | bytes 28
  291.3 10.1 %collective-permute-start.4 = (f32[2,64,1,512]{3,1,2,0:T(8,128)S(1)}, f32[2,64,1,512]{3,1,2,0:T(8,128)S(1)}, u32[]{:S(2)}, u32[]{:S(2)}) collective-permute-start(f32[2,64,1,512]{3,1,2,0:T(8,128)S(1)} %get-tuple-element.250), channel_id=1, source_target_pairs={{0,8},{8,16},{16,24},{24,32},{32,40},{40,48},{48,56},{56,64},{64,7... | collective-permute-start | bytes 786440 | tf_op jit(solution)/shard_map/ppermute | solution.py:29
  293.4 9.7 %collective-permute-start.5 = (f32[2,64,1,512]{3,1,2,0:T(8,128)S(1)}, f32[2,64,1,512]{3,1,2,0:T(8,128)S(1)}, u32[]{:S(2)}, u32[]{:S(2)}) collective-permute-start(f32[2,64,1,512]{3,1,2,0:T(8,128)S(1)} %get-tuple-element.251), channel_id=1, source_target_pairs={{8,0},{16,8},{24,16},{32,24},{40,32},{48,40},{56,48},{64,56},{72,6... | collective-permute-start | bytes 786440 | tf_op jit(solution)/shard_map/ppermute | solution.py:31
  308.5 16.2 %collective-permute-start.7 = (f32[2,64,34,1]{1,0,3,2:T(2,128)S(1)}, f32[2,64,34,1]{1,0,3,2:T(2,128)S(1)}, u32[]{:S(2)}, u32[]{:S(2)}) collective-permute-start(f32[2,64,34,1]{1,0,3,2:T(2,128)S(1)} %copy.76), channel_id=1, source_target_pairs={{1,0},{2,1},{3,2},{4,3},{5,4},{6,5},{7,6},{9,8},{10,9},{11,10},{12... | collective-permute-start | bytes 52232 | tf_op jit(solution)/shard_map/ppermute | solution.py:31
  314.6 9.4 %collective-permute-start.6 = (f32[2,64,34,1]{1,0,3,2:T(2,128)S(1)}, f32[2,64,34,1]{1,0,3,2:T(2,128)S(1)}, u32[]{:S(2)}, u32[]{:S(2)}) collective-permute-start(f32[2,64,34,1]{1,0,3,2:T(2,128)S(1)} %copy.75), channel_id=1, source_target_pairs={{0,1},{1,2},{2,3},{3,4},{4,5},{5,6},{6,7},{8,9},{9,10},{10,11},{11... | collective-permute-start | bytes 52232 | tf_op jit(solution)/shard_map/ppermute | solution.py:29
  340.8 4.5 copy-start
  383.8 10.2 %copy-start.2 = (f32[64,32,512]{2,0,1:T(8,128)}, f32[64,32,512]{2,0,1:T(8,128)S(1)}, u32[]{:S(2)}) copy-start(f32[64,32,512]{2,0,1:T(8,128)S(1)} %fusion.57) | copy-start | bytes 12582916
  383.8 8.4 %collective-permute-start.8 = (f32[64,1,512]{2,0,1:T(8,128)S(1)}, f32[64,1,512]{2,0,1:T(8,128)S(1)}, u32[]{:S(2)}, u32[]{:S(2)}) collective-permute-start(f32[64,1,512]{2,0,1:T(8,128)S(1)} %get-tuple-element.254), channel_id=1, source_target_pairs={{0,8},{8,16},{16,24},{24,32},{32,40},{40,48},{48,56},{56,64},{64,7... | collective-permute-start | bytes 393224 | tf_op jit(solution)/shard_map/ppermute | solution.py:29
  385.8 8.3 %collective-permute-start.9 = (f32[64,1,512]{2,0,1:T(8,128)S(1)}, f32[64,1,512]{2,0,1:T(8,128)S(1)}, u32[]{:S(2)}, u32[]{:S(2)}) collective-permute-start(f32[64,1,512]{2,0,1:T(8,128)S(1)} %get-tuple-element.255), channel_id=1, source_target_pairs={{8,0},{16,8},{24,16},{32,24},{40,32},{48,40},{56,48},{64,56},{72,6... | collective-permute-start | bytes 393224 | tf_op jit(solution)/shard_map/ppermute | solution.py:31
  395.4 16.8 %collective-permute-start.10 = (f32[64,34,1]{0,1,2:T(8,128)S(1)}, f32[64,34,1]{0,1,2:T(8,128)S(1)}, u32[]{:S(2)}, u32[]{:S(2)}) collective-permute-start(f32[64,34,1]{0,1,2:T(8,128)S(1)} %copy.79), channel_id=1, source_target_pairs={{0,1},{1,2},{2,3},{3,4},{4,5},{5,6},{6,7},{8,9},{9,10},{10,11},{11... | collective-permute-start | bytes 26120 | tf_op jit(solution)/shard_map/ppermute | solution.py:29
  397.3 14.4 %collective-permute-start.11 = (f32[64,34,1]{0,1,2:T(8,128)S(1)}, f32[64,34,1]{0,1,2:T(8,128)S(1)}, u32[]{:S(2)}, u32[]{:S(2)}) collective-permute-start(f32[64,34,1]{0,1,2:T(8,128)S(1)} %copy.80), channel_id=1, source_target_pairs={{1,0},{2,1},{3,2},{4,3},{5,4},{6,5},{7,6},{9,8},{10,9},{11,10},{12... | collective-permute-start | bytes 26120 | tf_op jit(solution)/shard_map/ppermute | solution.py:31
  412.6 11.3 %copy-start.3 = (f32[64,32,512]{2,0,1:T(8,128)S(1)}, f32[64,32,512]{2,0,1:T(8,128)}, u32[]{:S(2)}) copy-start(f32[64,32,512]{2,0,1:T(8,128)} %copy-done.2) | copy-start | bytes 12582916
where the time goes:
time: 461 us; the launch traced here: 453 us
  other arithmetic  286 us (62%)
  local copies, waits for them, and re-layouts  90.3 us (20%)
  starting transfers between devices  51 us (11%)
  waiting for transfers between devices  13.9 us (3%)
  matrix products  7.77 us (2%)
    scatter-add x1, other arithmetic, body(): extended = jnp.zeros((downward_site_total, padded_rows * patch_across_tot...  105 us
    reduce_sum x16, other arithmetic, tile_force(): repulse = jnp.sum(weight[:, None] * offset, axis=3)  61.4 us
    add x2, other arithmetic, thermal_advance(): return centre + change + heating  48.9 us
    unnamed x28, local copies, waits for them, and re-layouts  37.9 us
    ppermute x5, starting transfers between devices, padded(): lax.ppermute(head, axis, [((i + 1) % count, i) for i in range(ends)])  31.4 us
    gather x32, local copies, waits for them, and re-layouts, add_group(): pushed = tile_force(ext_blocks[targets + HB], ext_blocks[sources])  18.1 us
    reduce_sum x16, other arithmetic, tile_force(): weight = jnp.exp(-0.5 * jnp.sum(offset * offset, axis=1))  16.6 us
    concatenate x2, other arithmetic, padded(): jnp.concatenate([lax.ppermute(tail, axis, [(i, (i + 1) % count) for i in...  14.4 us
  transfers between devices with their start and end apart: 12, of which 7 were waited for; matrix products, arithmetic and copies ran while one was open for 7% of the time, Pallas kernels for 0%

commit v1 on v0

v1 whole, which is shorter than its diff:
```python
import math

import jax
import jax.numpy as jnp
from jax import lax
from jax.experimental import pallas as pl
from jax.experimental.pallas import tpu as pltpu
from jax.sharding import PartitionSpec as P

F32 = jnp.float32
BF16 = jnp.bfloat16
I32 = jnp.int32

DEPTH = 64
CX = 32
CY = 512
NPART = 16384
G = 16
HB = 2
NB = 128
NEXT = NB + 2 * HB
SLOTS = 256
BAND = 64.0
BIN = 256
LOG2E = 1.4426950408889634
VMEM_LIMIT = 56 * 1024 * 1024
UNROLL = 4

VSPEC = pl.BlockSpec(memory_space=pltpu.VMEM)
SSPEC = pl.BlockSpec(memory_space=pltpu.SMEM)


def iota(shape, dim):
    return lax.broadcasted_iota(I32, shape, dim)


def partner(a, step, axis, low):
    size = a.shape[axis]
    return jnp.where(low, pltpu.roll(a, size - step, axis), pltpu.roll(a, step, axis))


def cross_stage(ks, cs, step, axis, low):
    nk, nc = [], []
    for k, c in zip(ks, cs):
        pk = partner(k, step, axis, low)
        pc = partner(c, step, axis, low)
        m = jnp.where(low, jnp.minimum(k, pk), jnp.maximum(k, pk))
        nk.append(m)
        nc.append(jnp.where(m != k, pc, c))
    return nk, nc


def vreg_stage(ks, cs, j, descending):
    ks, cs = list(ks), list(cs)
    for r in range(16):
        if r & (1 << j):
            continue
        a, b = r, r | (1 << j)
        if descending(r):
            a, b = b, a
        less = ks[b] < ks[a]
        ks[a], ks[b] = jnp.minimum(ks[a], ks[b]), jnp.maximum(ks[a], ks[b])
        cs[a], cs[b] = jnp.where(less, cs[b], cs[a]), jnp.where(less, cs[a], cs[b])
    return ks, cs


def bitonic(ks, cs):
    sub = iota((8, 128), 0)
    lane = iota((8, 128), 1)
    up = lambda r: False

    def low_stages(ks, cs, top):
        for j in range(top, 3, -1):
            step = 1 << (j - 4)
            ks, cs = cross_stage(ks, cs, step, 0, (sub & step) == 0)
        for j in range(min(top, 3), -1, -1):
            ks, cs = vreg_stage(ks, cs, j, up)
        return ks, cs

    for k in range(1, 4):
        for j in range(k - 1, -1, -1):
            ks, cs = vreg_stage(ks, cs, j, lambda r: bool(r & (1 << k)))
    for k in range(4, 7):
        flip = -((sub >> (k - 4)) & 1)
        ks = [a ^ flip for a in ks]
        ks, cs = low_stages(ks, cs, k - 1)
        ks = [a ^ flip for a in ks]

    def phase(k, carry):
        ks, cs = list(carry[:16]), list(carry[16:])
        flip = -((lane >> (k - 7)) & 1)
        ks = [a ^ flip for a in ks]

        def lane_step(t, inner):
            step = jnp.left_shift(jnp.int32(1), k - 8 - t)
            low = (lane & step) == 0
            nk, nc = cross_stage(list(inner[:16]), list(inner[16:]), step, 1, low)
            return tuple(nk) + tuple(nc)

        out = lax.fori_loop(0, k - 7, lane_step, tuple(ks) + tuple(cs))
        ks, cs = low_stages(list(out[:16]), list(out[16:]), 6)
        ks = [a ^ flip for a in ks]
        return tuple(ks) + tuple(cs)

    out = lax.fori_loop(7, 15, phase, tuple(ks) + tuple(cs))
    return list(out[:16]), list(out[16:])


def split3(a):
    h1 = a.astype(BF16)
    r = a - h1.astype(F32)
    h2 = r.astype(BF16)
    h3 = (r - h2.astype(F32)).astype(BF16)
    return h1, h2, h3


def particle_kernel(
    tgt, src, cnt, loc, vel, halo_lo, halo_hi, key, wb,
    nloc, nvel, skey, schg, last, send_lo, send_hi,
    left, right, stat, acc, zrow,
):
    wide = 4 * 128

    def prepare(x3, v3, at, width):
        pad = jnp.zeros((5, width), F32)
        x = jnp.concatenate([x3, pad], axis=0)
        v = jnp.concatenate([v3, pad], axis=0)
        row = iota((8, width), 0)
        xs = x * math.sqrt(LOG2E)
        q = 0.5 * jnp.sum(xs * xs, axis=0, keepdims=True)
        full = jnp.where(row < 3, xs, jnp.where(row < 5, q, 0.0))
        h = [p.astype(F32) for p in split3(full)]

        def mix(a, b, is_target):
            base = h[a]
            if b is None:
                return jnp.where(row < 3, base, 0.0)
            if is_target:
                return jnp.where(row < 3, base, jnp.where(row == 3, h[b], jnp.where(row == 4, 1.0, 0.0)))
            return jnp.where(row < 3, base, jnp.where(row == 3, -1.0, jnp.where(row == 4, -h[b], 0.0)))

        extra = [0, 1, 2, None, None, None]
        ta = [0, 0, 1, 1, 0, 2]
        sa = [0, 1, 0, 1, 2, 0]
        for p in range(0, 6, 2):
            lt = jnp.concatenate([mix(ta[p], extra[p], True), mix(ta[p + 1], extra[p + 1], True)], axis=0)
            rt = jnp.concatenate([mix(sa[p], extra[p], False), mix(sa[p + 1], extra[p + 1], False)], axis=0)
            left[pl.ds(8 * p, 16), pl.ds(at, width)] = lt.astype(BF16)
            right[pl.ds(8 * p, 16), pl.ds(at, width)] = rt.astype(BF16)
        w = (2.0 * x - v) * (1.0 / 256.0)
        wh = w.astype(BF16).astype(F32)
        wl = w - wh
        w2 = jnp.concatenate([jnp.where(row == 3, 1.0, wh), wl], axis=0)
        stat[:, pl.ds(at, width)] = w2.astype(BF16)

    prepare(halo_lo[0:3, :], halo_lo[3:6, :], 0, HB * 128)
    prepare(halo_hi[0:3, :], halo_hi[3:6, :], (NB + HB) * 128, HB * 128)

    def prep(i, carry):
        at = pl.multiple_of(i * wide, wide)
        prepare(loc[:, pl.ds(at, wide)], vel[:, pl.ds(at, wide)], pl.multiple_of(at + HB * 128, 128), wide)
        return carry

    lax.fori_loop(0, NPART // wide, prep, 0)
    acc[...] = jnp.zeros_like(acc)
    live = cnt[0]

    def tiles(g, carry):
        outs = []
        for u in range(UNROLL):
            t = g * UNROLL + u
            a = tgt[t] & (NB - 1)
            b = a + (src[t] - tgt[t]) + HB
            lm = left[:, pl.ds(pl.multiple_of((a + HB) * 128, 128), 128)]
            rm = right[:, pl.ds(pl.multiple_of(b * 128, 128), 128)]
            arg = lax.dot_general(rm, lm, (((0,), (0,)), ((), ())), preferred_element_type=F32)
            g_mn = jnp.exp2(arg)
            gh = g_mn.astype(BF16)
            gl = (g_mn - gh.astype(F32)).astype(BF16)
            s = stat[:, pl.ds(pl.multiple_of(b * 128, 128), 128)]
            out = jnp.dot(
                jnp.concatenate([s, s], axis=1),
                jnp.concatenate([gh, gl], axis=0),
                preferred_element_type=F32,
            )
            home = jnp.where(t < live, a, NB)
            outs.append((home, out[0:8] + out[8:16]))
        for home, out in outs:
            at = pl.multiple_of(home * 8, 8)
            acc[pl.ds(at, 8), :] = acc[pl.ds(at, 8), :] + out
        return carry

    lax.fori_loop(0, (live + UNROLL - 1) // UNROLL, tiles, 0)

    def advance(i, carry):
        for u in range(8):
            b = i * 8 + u
            at = pl.multiple_of(b * 128, 128)
            x = loc[:, pl.ds(at, 128)]
            v = vel[:, pl.ds(at, 128)]
            f = acc[pl.ds(pl.multiple_of(b * 8, 8), 8), :]
            w = (2.0 * x - v) * (1.0 / 256.0)
            force = w * f[3:4] - f[0:3]
            nv = v + 0.5 * force
            nx = x + 0.5 * nv
            nvel[:, pl.ds(at, 128)] = nv
            nloc[:, pl.ds(at, 128)] = nx
            zrow[pl.ds(b, 1), :] = nx[2:3]
        return carry

    lax.fori_loop(0, NB // 8, advance, 0)

    charge = wb[...] * (1.0 + 0.5 * jnp.tanh(zrow[...]))
    keys = key[...]
    ks = [keys[8 * r : 8 * r + 8] for r in range(16)]
    cs = [charge[8 * r : 8 * r + 8] for r in range(16)]
    ks, cs = bitonic(ks, cs)
    last[...] = ks[15][7:8]
    kt = jnp.concatenate(ks, axis=0)
    ct = jnp.concatenate(cs, axis=0)
    kt = jnp.transpose(kt)
    ct = jnp.transpose(ct)
    skey[...] = kt
    schg[...] = ct
    for ref, at in ((send_lo, 0), (send_hi, 96)):
        kk = kt[at : at + 32]
        ref[0:32] = (kk >> 15).astype(F32)
        ref[32:64] = ((kk >> 6) & 511).astype(F32)
        ref[64:96] = (kk & 63).astype(F32)
        ref[96:128] = ct[at : at + 32]


def particles(tgt, src, cnt, loc, vel, halo_lo, halo_hi, key, wb):
    sd = jax.ShapeDtypeStruct
    return pl.pallas_call(
        particle_kernel,
        out_shape=(
            sd((3, NPART), F32), sd((3, NPART), F32),
            sd((128, 128), I32), sd((128, 128), F32), sd((1, 128), I32),
            sd((128, 128), F32), sd((128, 128), F32),
        ),
        in_specs=[SSPEC] * 3 + [VSPEC] * 6,
        out_specs=(VSPEC,) * 7,
        scratch_shapes=[
            pltpu.VMEM((48, NEXT * 128), BF16),
            pltpu.VMEM((48, NEXT * 128), BF16),
            pltpu.VMEM((16, NEXT * 128), BF16),
            pltpu.VMEM(((NB + 1) * 8, 128), F32),
            pltpu.VMEM((NB, 128), F32),
        ],
        compiler_params=pltpu.CompilerParams(vmem_limit_bytes=VMEM_LIMIT),
        name="particle_step",
    )(tgt, src, cnt, loc, vel, halo_lo, halo_hi, key, wb)


OWN, RECV = 128, 32
BATCHES = OWN + 2 * RECV
DUMMY = BATCHES


def deposit_kernel(
    last, last_lo, last_hi, skey, schg, recv_lo, recv_hi,
    share, row_lo, row_hi, col_lo, col_hi,
    cells, prof, pile,
):
    own = skey[...]
    cells[0:OWN] = (own >> 6) - G * CY
    for ref, at, shift in ((recv_lo, OWN, -(G + CX)), (recv_hi, OWN + RECV, CX - G)):
        x = ref[0:32].astype(I32) + shift
        cells[at : at + RECV] = x * CY + ref[32:64].astype(I32)
    cells[DUMMY : DUMMY + 8] = jnp.full((8, 128), -1, I32)
    prof[DUMMY] = jnp.zeros((128, 128), BF16)
    level = iota((DEPTH, 128), 0).astype(F32)
    scale = math.sqrt(LOG2E) / 12.0

    def profile(z, charge):
        d = (level - z) * scale
        p = jnp.exp2(-(d * d)) * charge
        hi = p.astype(BF16)
        lo = (p - hi.astype(F32)).astype(BF16)
        return jnp.concatenate([hi, lo], axis=0)

    def own_profiles(i, carry):
        for u in range(4):
            b = i * 4 + u
            z = (skey[pl.ds(b, 1), :] & 63).astype(F32)
            prof[b] = profile(z, schg[pl.ds(b, 1), :])
        return carry

    lax.fori_loop(0, OWN // 4, own_profiles, 0)

    def recv_profiles(i, carry):
        for ref, at in ((recv_lo, OWN), (recv_hi, OWN + RECV)):
            for u in range(2):
                b = i * 2 + u
                prof[at + b] = profile(ref[pl.ds(64 + b, 1), :], ref[pl.ds(96 + b, 1), :])
        return carry

    lax.fori_loop(0, RECV // 2, recv_profiles, 0)

    def clear(i, carry):
        pile[i] = jnp.zeros((DEPTH, BIN), F32)
        return carry

    lax.fori_loop(0, 2 * CX, clear, 0)
    spot = iota((BIN, 128), 0)

    def walk(base, count, last_bin, first_bin):
        def seek(i, s):
            b = last_bin(i)
            return s[0] + (b < first_bin).astype(I32), s[1] + (b < 2 * CX).astype(I32)

        start, stop = lax.fori_loop(0, count, seek, (jnp.int32(0), jnp.int32(0)))
        stop = jnp.minimum(stop, count - 1)
        steps = stop - start + 1 + (2 * CX - 1 - first_bin)

        def step(g, state):
            i, j = state
            work = []
            for u in range(UNROLL):
                ii = jnp.where(i <= stop, base + i, DUMMY)
                work.append((ii, j))
                more = jnp.logical_and(last_bin(jnp.minimum(i, count - 1)) > j, j < 2 * CX - 1)
                j = jnp.where(more, j + 1, j)
                i = jnp.where(more, i, jnp.minimum(i + 1, count))
            outs = []
            for ii, jj in work:
                row = cells[pl.ds(ii, 1), :] - jj * BIN
                hot = jnp.where(spot == row, 1.0, 0.0).astype(BF16)
                out = lax.dot_general(prof[ii], hot, (((1,), (1,)), ((), ())), preferred_element_type=F32)
                outs.append(out[:DEPTH] + out[DEPTH:])
            for (ii, jj), out in zip(work, outs):
                pile[jj] = pile[jj] + out
            return i, j

        @pl.when(start <= stop)
        def _():
            lax.fori_loop(0, (steps + UNROLL - 1) // UNROLL, step, (start, jnp.int32(first_bin)))

    walk(0, OWN, lambda i: (last[i] >> 14) - 2 * G, 0)
    walk(OWN, RECV, lambda i: last_lo[i], 0)
    walk(OWN + RECV, RECV, lambda i: last_hi[i], 2 * G)

    row_lo[:, :BIN] = pile[0]
    row_lo[:, BIN:] = pile[1]
    row_hi[:, :BIN] = pile[2 * CX - 2]
    row_hi[:, BIN:] = pile[2 * CX - 1]
    lane = iota((8, 128), 1)
    sub = iota((8, 512), 0)

    def flip(t, carry):
        xg = t // 8
        zg = lax.rem(t, 8)
        z0 = pl.multiple_of(zg * 8, 8)
        x0 = pl.multiple_of(xg * 8, 8)
        a = []
        for i in range(8):
            bin0 = (x0 + i) * 2
            a.append(jnp.concatenate([pile[bin0, pl.ds(z0, 8), :], pile[bin0 + 1, pl.ds(z0, 8), :]], axis=1))
        for d in (1, 2, 4):
            b = list(a)
            low = (sub & d) == 0
            for i in range(8):
                if i & d:
                    continue
                p, q = a[i], a[i | d]
                b[i] = jnp.where(low, p, pltpu.roll(q, d, 0))
                b[i | d] = jnp.where(low, pltpu.roll(p, 8 - d, 0), q)
            a = b
        c0 = jnp.where(zg == 0, jnp.zeros((8, 128), F32), col_lo[pl.ds(x0, 8), :])
        c1 = jnp.where(zg == 0, jnp.zeros((8, 128), F32), col_hi[pl.ds(x0, 8), :])
        for k in range(8):
            share[z0 + k, pl.ds(x0, 8), :] = a[k]
            z = z0 + k
            c0 = jnp.where(lane == z, pltpu.roll(a[k][:, :128], z, 1), c0)
            c1 = jnp.where(lane == z, pltpu.roll(a[k][:, 384:], z + 1, 1), c1)
        col_lo[pl.ds(x0, 8), :] = c0
        col_hi[pl.ds(x0, 8), :] = c1
        return carry

    lax.fori_loop(0, 32, flip, 0)


def deposit(last, last_lo, last_hi, skey, schg, recv_lo, recv_hi):
    sd = jax.ShapeDtypeStruct
    return pl.pallas_call(
        deposit_kernel,
        out_shape=(
            sd((DEPTH, CX, CY), F32),
            sd((DEPTH, CY), F32), sd((DEPTH, CY), F32),
            sd((CX, 128), F32), sd((CX, 128), F32),
        ),
        in_specs=[SSPEC] * 3 + [VSPEC] * 4,
        out_specs=(VSPEC,) * 5,
        scratch_shapes=[
            pltpu.VMEM((BATCHES + 8, 128), I32),
            pltpu.VMEM((BATCHES + 1, 128, 128), BF16),
            pltpu.VMEM((2 * CX, DEPTH, BIN), F32),
        ],
        compiler_params=pltpu.CompilerParams(vmem_limit_bytes=VMEM_LIMIT),
        name="deposit",
    )(last, last_lo, last_hi, skey, schg, recv_lo, recv_hi)


def edges_kernel(left, right, top, bottom, row_lo, row_hi, col_lo, col_hi):
    row_lo[...] = top[:, 0, :]
    row_hi[...] = bottom[:, 7, :]
    lane = iota((CX, 128), 1)
    c0 = jnp.zeros((CX, 128), F32)
    c1 = jnp.zeros((CX, 128), F32)
    for z in range(DEPTH):
        a = left[z] if z == 0 else pltpu.roll(left[z], z, 1)
        c0 = jnp.where(lane == z, a, c0)
        c1 = jnp.where(lane == z, pltpu.roll(right[z], z + 1, 1), c1)
    col_lo[...] = c0
    col_hi[...] = c1


def edges(cells):
    sd = jax.ShapeDtypeStruct
    return pl.pallas_call(
        edges_kernel,
        grid=(1,),
        out_shape=(
            sd((DEPTH, CY), F32), sd((DEPTH, CY), F32),
            sd((CX, 128), F32), sd((CX, 128), F32),
        ),
        in_specs=[
            pl.BlockSpec((DEPTH, CX, 128), lambda i: (0, 0, 0)),
            pl.BlockSpec((DEPTH, CX, 128), lambda i: (0, 0, CY // 128 - 1)),
            pl.BlockSpec((DEPTH, 8, CY), lambda i: (0, 0, 0)),
            pl.BlockSpec((DEPTH, 8, CY), lambda i: (0, CX // 8 - 1, 0)),
        ],
        out_specs=(
            pl.BlockSpec((DEPTH, CY), lambda i: (0, 0)), pl.BlockSpec((DEPTH, CY), lambda i: (0, 0)),
            pl.BlockSpec((CX, 128), lambda i: (0, 0)), pl.BlockSpec((CX, 128), lambda i: (0, 0)),
        ),
        compiler_params=pltpu.CompilerParams(vmem_limit_bytes=VMEM_LIMIT),
        name="temperature_edges",
    )(cells, cells, cells, cells)


def half_kappa(u, v):
    return 0.05 * (1.0 + 0.5 * jnp.tanh(u)) / (1.0 + v)


def heat_kernel(
    with_edges, beam, u_ref, v_ref, ur_lo, ur_hi, uc_lo, uc_hi, vr_lo, vr_hi, vc_lo, vc_hi, out, *rest
):
    if with_edges:
        row_lo, row_hi, col_lo, col_hi = rest[:4]
        rest = rest[4:]
    kr_lo, kr_hi, kc_lo, kc_hi, kz, fz = rest
    kr_lo[...] = half_kappa(ur_lo[...], vr_lo[...])
    kr_hi[...] = half_kappa(ur_hi[...], vr_hi[...])
    kc_lo[...] = half_kappa(uc_lo[...], vc_lo[...])
    kc_hi[...] = half_kappa(uc_hi[...], vc_hi[...])
    if with_edges:
        col_lo[...] = jnp.zeros_like(col_lo)
        col_hi[...] = jnp.zeros_like(col_hi)
    lane = iota((CX, 128), 1)
    row = iota((CX, CY), 0)
    rows = (iota((CX, 128), 0).astype(F32) + beam[0]) * (1.0 / BAND)
    glow = 0.5 * jnp.exp(-(rows * rows))
    glow = jnp.concatenate([glow] * (CY // 128), axis=1)
    k0 = half_kappa(u_ref[0], v_ref[0])
    kz[0] = k0
    fz[...] = (k0 + 0.05) * u_ref[0]

    def plane(z, is_last):
        u = u_ref[z]
        k = kz[z & 1]
        if is_last:
            up = (k + 0.05) * (0.0 - u)
        else:
            un = u_ref[z + 1]
            kn = half_kappa(un, v_ref[z + 1])
            kz[(z + 1) & 1] = kn
            up = (k + kn) * (un - u)
        total = up - fz[...]
        fz[...] = up
        at = pl.ds(z, 1)
        below_u = jnp.where(row == 0, ur_lo[at, :], pltpu.roll(u, 1, 0))
        below_k = jnp.where(row == 0, kr_lo[at, :], pltpu.roll(k, 1, 0))
        f = (k + below_k) * (u - below_u)
        top = (k[24:32] + kr_hi[at, :]) * (ur_hi[at, :] - u[24:32])
        shifted = pltpu.roll(f, CX - 1, 0)
        above = jnp.concatenate([shifted[:24], jnp.where(row[24:32] == CX - 1, top, shifted[24:32])], axis=0)
        total = total + (above - f)

        def put(wide, tile, first):
            if first:
                return jnp.concatenate([jnp.where(lane == 0, tile, wide[:, :128]), wide[:, 128:]], axis=1)
            return jnp.concatenate([wide[:, :384], jnp.where(lane == 127, tile, wide[:, 384:])], axis=1)

        back = (128 - z) & 127
        left_u = put(pltpu.roll(u, 1, 1), pltpu.roll(uc_lo[...], back, 1), True)
        left_k = put(pltpu.roll(k, 1, 1), pltpu.roll(kc_lo[...], back, 1), True)
        f = (k + left_k) * (u - left_u)
        end_u = pltpu.roll(uc_hi[...], 127 - z, 1)
        end_k = pltpu.roll(kc_hi[...], 127 - z, 1)
        end = (k[:, 384:] + end_k) * (end_u - u[:, 384:])
        total = total + (put(pltpu.roll(f, CY - 1, 1), end, False) - f)
        new = u + total + glow * v_ref[z]
        out[z] = new
        if with_edges:
            row_lo[at, :] = new[0:1]
            row_hi[at, :] = new[CX - 1 : CX]
            col_lo[...] = jnp.where(lane == z, pltpu.roll(new[:, :128], z, 1), col_lo[...])
            col_hi[...] = jnp.where(lane == z, pltpu.roll(new[:, 384:], z + 1, 1), col_hi[...])

    def body(z, carry):
        plane(z, False)
        return carry

    lax.fori_loop(0, DEPTH - 1, body, 0)
    plane(DEPTH - 1, True)


def heat(beam, u, v, u_halo, v_halo, with_edges):
    sd = jax.ShapeDtypeStruct
    outs = [sd((DEPTH, CX, CY), F32)]
    if with_edges:
        outs += [sd((DEPTH, CY), F32)] * 2 + [sd((CX, 128), F32)] * 2
    return pl.pallas_call(
        lambda *refs: heat_kernel(with_edges, *refs),
        out_shape=tuple(outs),
        in_specs=[SSPEC] + [VSPEC] * 10,
        out_specs=(VSPEC,) * len(outs),
        scratch_shapes=[
            pltpu.VMEM((DEPTH, CY), F32), pltpu.VMEM((DEPTH, CY), F32),
            pltpu.VMEM((CX, 128), F32), pltpu.VMEM((CX, 128), F32),
            pltpu.VMEM((2, CX, CY), F32), pltpu.VMEM((CX, CY), F32),
        ],
        compiler_params=pltpu.CompilerParams(vmem_limit_bytes=VMEM_LIMIT),
        name="heat_step_one" if with_edges else "heat_step_two",
    )(beam, u, v, *u_halo, *v_halo)


def shift(value, axis, steps):
    count = lax.axis_size(axis)
    first, stop = max(0, -steps), min(count, count - steps)
    return lax.ppermute(value, axis, [(i, i + steps) for i in range(first, stop)])


def exchange(edge):
    row_lo, row_hi, col_lo, col_hi = edge
    return (
        shift(row_hi, "gx", 1),
        shift(row_lo, "gx", -1),
        shift(col_hi, "gy", 1),
        shift(col_lo, "gy", -1),
    )


def body(
    particle_locations,
    particle_speeds,
    particle_bulk,
    receiving_group_per_pair,
    emitting_group_per_pair,
    active_pair_slots,
    landing_site_triple,
    landing_weight_octants,
    thermal_excess,
    molten_strip_midlines,
):
    states = jnp.concatenate([particle_locations, particle_speeds], axis=0)
    width = HB * 128
    halo_lo = shift(states[:, NPART - width :], ("gx", "gy"), 1)
    halo_hi = shift(states[:, :width], ("gx", "gy"), -1)
    u_halo = exchange(edges(thermal_excess))

    row_start = lax.axis_index("gx") * CX
    col_start = lax.axis_index("gy") * CY
    px = landing_site_triple[1] - row_start + G
    py = landing_site_triple[2] - col_start
    key = ((px * CY + py) * DEPTH + landing_site_triple[0]).reshape(128, 128)
    wb = (particle_bulk * landing_weight_octants.astype(F32) * 0.125).reshape(128, 128)

    nloc, nvel, skey, schg, last, send_lo, send_hi = particles(
        receiving_group_per_pair, emitting_group_per_pair, active_pair_slots,
        particle_locations, particle_speeds, halo_lo, halo_hi, key, wb,
    )
    from_lo = shift(send_hi, "gx", 1)
    from_hi = shift(send_lo, "gx", -1)

    def last_bins(got, by):
        cell = (got[0:32, 127].astype(I32) + by) * CY + got[32:64, 127].astype(I32)
        return cell >> 8

    v, *v_edge = deposit(
        last.reshape(128), last_bins(from_lo, -(G + CX)), last_bins(from_hi, CX - G),
        skey, schg, from_lo, from_hi,
    )
    v_halo = exchange(v_edge)
    beam = (row_start - molten_strip_midlines).astype(F32)
    mid, *mid_edge = heat(beam[0:1], thermal_excess, v, u_halo, v_halo, True)
    (final,) = heat(beam[1:2], mid, v, exchange(mid_edge), v_halo, False)
    return nloc, nvel, v, final


def solution(mesh):
    placed = (
        P(None, ("gx", "gy")),
        P(None, ("gx", "gy")),
        P(("gx", "gy")),
        P(("gx", "gy")),
        P(("gx", "gy")),
        P(("gx", "gy")),
        P(None, ("gx", "gy")),
        P(("gx", "gy")),
        P(None, "gx", "gy"),
        P(),
    )
    return jax.shard_map(
        body,
        mesh=mesh,
        in_specs=placed,
        out_specs=(
            P(None, ("gx", "gy")),
            P(None, ("gx", "gy")),
            P(None, "gx", "gy"),
            P(None, "gx", "gy"),
        ),
        check_vma=False,
    )
```

time: 461 us -> 176 us (0.38); the launches traced: 453 us -> 174 us
  other arithmetic: 286 us -> 5.84 us
  Pallas kernels: 0 us -> 94.6 us
  local copies, waits for them, and re-layouts: 90.3 us -> 2.7 us
  starting transfers between devices: 51 us -> 63 us
  matrix products: 7.77 us -> 0 us
  waiting for transfers between devices: 13.9 us -> 6.71 us
    scatter-add x1 -> x0, other arithmetic: 105 us -> none  [body(): extended = jnp.zeros((downward_site_total, padded_rows * patch_across_tot...]
    pallas_call x0 -> x5, Pallas kernels: none -> 94.6 us  [the longest x2 42.5 us: heat(): pl.pallas_call(lambda *refs: heat_kernel(with_edges, *refs), out_shape=tu...]
    reduce_sum x32 -> x0, other arithmetic: 78 us -> none  [the longest x16 61.4 us: tile_force(): repulse = jnp.sum(weight[:, None] * offset, axis=3)]
    add x6 -> x1, other arithmetic: 55.5 us -> 2.06 us  [body(): key = ((px * CY + py) * DEPTH + landing_site_triple[0]).reshape(128, 128)]
    unnamed x28 -> x36, local copies, waits for them, and re-layouts: 37.9 us -> 2.05 us
    slice x40 -> x1, local copies, waits for them, and re-layouts: 20.4 us -> 0.65 us  [body(): mid, *mid_edge = heat(beam[0:1], thermal_excess, v, u_halo, v_halo, True)]
    gather x32 -> x0, local copies, waits for them, and re-layouts: 18.1 us -> none  [add_group(): pushed = tile_force(ext_blocks[targets + HB], ext_blocks[sources])]
    concatenate x2 -> x1, other arithmetic: 14.4 us -> 0.75 us  [body(): states = jnp.concatenate([particle_locations, particle_speeds], axis=0)]
  transfers between devices with their start and end apart: 12 -> 16, of which waited for: 7 -> 4; matrix products, arithmetic and copies ran while one was open for 7% -> 3% of each run, Pallas kernels for 0% -> 18%
where the time goes in v1:
time: 176 us; the launch traced here: 174 us
  Pallas kernels  94.6 us (54%)
  starting transfers between devices  63 us (36%)
  waiting for transfers between devices  6.71 us (4%)
  other arithmetic  5.84 us (3%)
  local copies, waits for them, and re-layouts  2.7 us (2%)
    ppermute x16, starting transfers between devices, shift(): lax.ppermute(value, axis, [(i, i + steps) for i in range(first, stop)])  63 us
    pallas_call x2, Pallas kernels, heat(): pl.pallas_call(lambda *refs: heat_kernel(with_edges, *refs), out_shape=tu...  42.5 us
    pallas_call x1, Pallas kernels, deposit(): pl.pallas_call(deposit_kernel, out_shape=(sd((DEPTH, CX, CY), F32), sd((D...  28.3 us
    pallas_call x1, Pallas kernels, particles(): pl.pallas_call(particle_kernel, out_shape=(sd((3, NPART), F32), sd((3, NP...  20.3 us
    ppermute x16, waiting for transfers between devices, shift(): lax.ppermute(value, axis, [(i, i + steps) for i in range(first, stop)])  6.71 us
    pallas_call x1, Pallas kernels, edges(): pl.pallas_call(edges_kernel, grid=(1,), out_shape=(sd((DEPTH, CY), F32),...  3.52 us
  transfers between devices with their start and end apart: 16, of which 4 were waited for; matrix products, arithmetic and copies ran while one was open for 3% of the time, Pallas kernels for 18%

profile of v1, /device:TPU:24, one launch (start us, length us, event | category | flops | bytes accessed | tf_op | source)
XLA Modules:
  0.0 174.5 jit_solution(10695513741358065650)
XLA Ops:
  0.6 0.7 pad_maximum_fusion
  1.4 5.3 %collective-permute-start.1 = (f32[6,256]{1,0:T(8,128)S(1)}, f32[6,256]{1,0:T(8,128)S(1)}, u32[]{:S(2)}, u32[]{:S(2)}) collective-permute-start(f32[6,256]{1,0:T(8,128)S(1)} %get-tuple-element.46), channel_id=1, source_target_pairs={{1,0},{2,1},{3,2},{4,3},{5,4},{6,5},{7,6},{8,7},{9,8},{10,9},{11,1... | collective-permute-start | bytes 18440 | tf_op jit(solution)/shard_map/ppermute | solution.py:543
  6.7 1.9 %collective-permute-start = (f32[6,256]{1,0:T(8,128)S(1)}, f32[6,256]{1,0:T(8,128)S(1)}, u32[]{:S(2)}, u32[]{:S(2)}) collective-permute-start(f32[6,256]{1,0:T(8,128)S(1)} %get-tuple-element.47), channel_id=1, source_target_pairs={{0,1},{1,2},{2,3},{3,4},{4,5},{5,6},{6,7},{7,8},{8,9},{9,10},{10,1... | collective-permute-start | bytes 18440 | tf_op jit(solution)/shard_map/ppermute | solution.py:543
  8.7 2.1 %multiply_add_fusion = s32[1,16384]{1,0:T(1,128)} fusion(s32[3,16384]{1,0:T(4,128)} %param.16, s32[]{:T(128)S(6)} %mul.41, s32[]{:T(128)S(6)} %mul.38), kind=kLoop, calls=%fused_computation | loop fusion | flops 114688 | bytes 262152 | tf_op jit(solution)/shard_map/add | solution.py:578
  10.7 1.5 multiply_bitcast_fusion.wb
  12.9 0.0 collective-permute-done.1.halo_hi
  12.9 3.0 %collective-permute-done.halo_lo = f32[6,256]{1,0:T(8,128)S(1)} collective-permute-done((f32[6,256]{1,0:T(8,128)S(1)}, f32[6,256]{1,0:T(8,128)S(1)}, u32[]{:S(2)}, u32[]{:S(2)}) %collective-permute-start) | collective-permute-done | bytes 6176 | tf_op jit(solution)/shard_map/ppermute | solution.py:543
  15.9 0.6 copy-done.15
  16.5 20.3 %particle_step.1 = (f32[3,16384]{1,0:T(4,128)}, f32[3,16384]{1,0:T(4,128)}, s32[128,128]{1,0:T(8,128)}, f32[128,128]{1,0:T(8,128)}, s32[1,128]{1,0:T(1,128)}, /*index=5*/f32[128,128]{1,0:T(8,128)}, f32[128,128]{1,0:T(8,128)}) custom-call(s32[256]{0:T(256)} %tgt.1, s32[256]{0:T(256)} %src.1, s32[1]{0:T(128)S(6)} %copy.14.cnt, f32[3,16384]{1,0:T(4,128)} %loc.1, ...), custom_call_target="tpu_custom_call" | custom-call | tf_op jit(solution)/shard_map/particle_step/pallas_call | solution.py:235
  36.8 2.1 %collective-permute-start.2 = (f32[128,128]{1,0:T(8,128)}, f32[128,128]{1,0:T(8,128)S(1)}, u32[]{:S(2)}, u32[]{:S(2)}) collective-permute-start(f32[128,128]{1,0:T(8,128)} %get-tuple-element.28), channel_id=1, source_target_pairs={{0,8},{8,16},{16,24},{24,32},{32,40},{40,48},{48,56},{56,64},{64,7... | collective-permute-start | bytes 196616 | tf_op jit(solution)/shard_map/ppermute | solution.py:543
  38.8 3.5 %temperature_edges.1 = (f32[64,512]{1,0:T(8,128)}, f32[64,512]{1,0:T(8,128)}, f32[32,128]{1,0:T(8,128)}, f32[32,128]{1,0:T(8,128)}) custom-call(f32[64,32,512]{2,1,0:T(8,128)} %refs_1_.1, f32[64,32,512]{2,1,0:T(8,128)} %refs_1_.1, f32[64,32,512]{2,1,0:T(8,128)} %refs_1_.1, f32[64,32,512]{2,1,0:T(8,128)} %refs_1_.1), custom_call_target="tpu_custom_call" | custom-call | tf_op jit(solution)/shard_map/temperature_edges/pallas_call | solution.py:421
  42.3 1.9 %collective-permute-start.6 = (f32[32,128]{1,0:T(8,128)}, f32[32,128]{1,0:T(8,128)S(1)}, u32[]{:S(2)}, u32[]{:S(2)}) collective-permute-start(f32[32,128]{1,0:T(8,128)} %get-tuple-element.35), channel_id=1, source_target_pairs={{0,1},{1,2},{2,3},{3,4},{4,5},{5,6},{6,7},{8,9},{9,10},{10,11},{11... | collective-permute-start | bytes 49160 | tf_op jit(solution)/shard_map/ppermute | solution.py:543
  44.3 7.5 %collective-permute-start.7 = (f32[32,128]{1,0:T(8,128)}, f32[32,128]{1,0:T(8,128)S(1)}, u32[]{:S(2)}, u32[]{:S(2)}) collective-permute-start(f32[32,128]{1,0:T(8,128)} %get-tuple-element.36), channel_id=1, source_target_pairs={{1,0},{2,1},{3,2},{4,3},{5,4},{6,5},{7,6},{9,8},{10,9},{11,10},{12... | collective-permute-start | bytes 49160 | tf_op jit(solution)/shard_map/ppermute | solution.py:543
  51.8 1.9 %collective-permute-start.4 = (f32[64,512]{1,0:T(8,128)}, f32[64,512]{1,0:T(8,128)S(1)}, u32[]{:S(2)}, u32[]{:S(2)}) collective-permute-start(f32[64,512]{1,0:T(8,128)} %get-tuple-element.33), channel_id=1, source_target_pairs={{0,8},{8,16},{16,24},{24,32},{32,40},{40,48},{48,56},{56,64},{64,7... | collective-permute-start | bytes 393224 | tf_op jit(solution)/shard_map/ppermute | solution.py:543
  53.7 5.8 %collective-permute-start.5 = (f32[64,512]{1,0:T(8,128)}, f32[64,512]{1,0:T(8,128)S(1)}, u32[]{:S(2)}, u32[]{:S(2)}) collective-permute-start(f32[64,512]{1,0:T(8,128)} %get-tuple-element.34), channel_id=1, source_target_pairs={{8,0},{16,8},{24,16},{32,24},{40,32},{48,40},{56,48},{64,56},{72,6... | collective-permute-start | bytes 393224 | tf_op jit(solution)/shard_map/ppermute | solution.py:543
  59.5 0.0 collective-permute-done.2.recv_lo
  59.5 1.9 %collective-permute-start.3 = (f32[128,128]{1,0:T(8,128)S(1)}, f32[128,128]{1,0:T(8,128)S(1)}, u32[]{:S(2)}, u32[]{:S(2)}) collective-permute-start(f32[128,128]{1,0:T(8,128)S(1)} %copy-done.16), channel_id=1, source_target_pairs={{8,0},{16,8},{24,16},{32,24},{40,32},{48,40},{56,48},{64,56},{72,6... | collective-permute-start | bytes 196616 | tf_op jit(solution)/shard_map/ppermute | solution.py:543
  61.4 0.8 fusion.7.last_lo
  62.2 1.1 collective-permute-done.3.recv_hi
  63.3 0.7 fusion.2.last_hi
  64.1 28.3 %deposit.1 = (f32[64,32,512]{2,1,0:T(8,128)}, f32[64,512]{1,0:T(8,128)}, f32[64,512]{1,0:T(8,128)}, f32[32,128]{1,0:T(8,128)}, f32[32,128]{1,0:T(8,128)}) custom-call(s32[128]{0:T(128)} %bitcast.5, s32[32]{0:T(128)} %fusion.7.last_lo, s32[32]{0:T(128)} %fusion.2.last_hi, s32[128,128]{1,0:T(8,128)} %get-tuple-element.30.skey, ...), custom_call_target="tpu_custom_call" | custom-call | tf_op jit(solution)/shard_map/deposit/pallas_call | solution.py:386
  92.4 1.9 %collective-permute-start.10 = (f32[32,128]{1,0:T(8,128)}, f32[32,128]{1,0:T(8,128)S(1)}, u32[]{:S(2)}, u32[]{:S(2)}) collective-permute-start(f32[32,128]{1,0:T(8,128)} %get-tuple-element.39), channel_id=1, source_target_pairs={{0,1},{1,2},{2,3},{3,4},{4,5},{5,6},{6,7},{8,9},{9,10},{10,11},{11... | collective-permute-start | bytes 49160 | tf_op jit(solution)/shard_map/ppermute | solution.py:543
  94.3 0.0 collective-permute-done.6.refs_5_
  94.3 1.9 %collective-permute-start.8 = (f32[64,512]{1,0:T(8,128)}, f32[64,512]{1,0:T(8,128)S(1)}, u32[]{:S(2)}, u32[]{:S(2)}) collective-permute-start(f32[64,512]{1,0:T(8,128)} %get-tuple-element.37), channel_id=1, source_target_pairs={{0,8},{8,16},{16,24},{24,32},{32,40},{40,48},{48,56},{56,64},{64,7... | collective-permute-start | bytes 393224 | tf_op jit(solution)/shard_map/ppermute | solution.py:543
  96.3 0.0 collective-permute-done.7.refs_6_
  96.3 5.8 %collective-permute-start.9 = (f32[64,512]{1,0:T(8,128)}, f32[64,512]{1,0:T(8,128)S(1)}, u32[]{:S(2)}, u32[]{:S(2)}) collective-permute-start(f32[64,512]{1,0:T(8,128)} %get-tuple-element.38), channel_id=1, source_target_pairs={{8,0},{16,8},{24,16},{32,24},{40,32},{48,40},{56,48},{64,56},{72,6... | collective-permute-start | bytes 393224 | tf_op jit(solution)/shard_map/ppermute | solution.py:543
  102.1 0.0 collective-permute-done.10.refs_9_
  102.1 7.7 %collective-permute-start.11 = (f32[32,128]{1,0:T(8,128)}, f32[32,128]{1,0:T(8,128)S(1)}, u32[]{:S(2)}, u32[]{:S(2)}) collective-permute-start(f32[32,128]{1,0:T(8,128)} %get-tuple-element.40), channel_id=1, source_target_pairs={{1,0},{2,1},{3,2},{4,3},{5,4},{6,5},{7,6},{9,8},{10,9},{11,10},{12... | collective-permute-start | bytes 49160 | tf_op jit(solution)/shard_map/ppermute | solution.py:543
  109.8 0.6 fusion.10
  110.4 1.0 collective-permute-done.11.refs_10_
  111.4 0.0 collective-permute-done.4.refs_3_
  111.4 0.0 collective-permute-done.5.refs_4_
  111.4 0.0 collective-permute-done.8.refs_7_
  111.5 0.5 copy-done.9
  112.0 0.1 copy-done.4
  112.1 0.0 copy-done.5
  112.1 0.0 copy-done
  112.2 0.1 copy-done.1
  112.2 23.5 %heat_step_one.1 = (f32[64,32,512]{2,1,0:T(8,128)}, f32[64,512]{1,0:T(8,128)}, f32[64,512]{1,0:T(8,128)}, f32[32,128]{1,0:T(8,128)}, f32[32,128]{1,0:T(8,128)}) custom-call(f32[1]{0:T(128)} %get-tuple-element.48.refs_0_, f32[64,32,512]{2,1,0:T(8,128)} %refs_1_.1, f32[64,32,512]{2,1,0:T(8,128)} %get-tuple-element.23.refs_2_, f32[64,512]{1,0:T(8,128)} %copy-done.4, ...), custom_call_target="tpu_custom_call" | custom-call | tf_op jit(solution)/shard_map/heat_step_one/pallas_call | solution.py:525
  135.8 1.9 %collective-permute-start.12 = (f32[64,512]{1,0:T(8,128)}, f32[64,512]{1,0:T(8,128)S(1)}, u32[]{:S(2)}, u32[]{:S(2)}) collective-permute-start(f32[64,512]{1,0:T(8,128)} %get-tuple-element.42), channel_id=1, source_target_pairs={{0,8},{8,16},{16,24},{24,32},{32,40},{40,48},{48,56},{56,64},{64,7... | collective-permute-start | bytes 393224 | tf_op jit(solution)/shard_map/ppermute | solution.py:543
  137.7 5.8 %collective-permute-start.13 = (f32[64,512]{1,0:T(8,128)}, f32[64,512]{1,0:T(8,128)S(1)}, u32[]{:S(2)}, u32[]{:S(2)}) collective-permute-start(f32[64,512]{1,0:T(8,128)} %get-tuple-element.43), channel_id=1, source_target_pairs={{8,0},{16,8},{24,16},{32,24},{40,32},{48,40},{56,48},{64,56},{72,6... | collective-permute-start | bytes 393224 | tf_op jit(solution)/shard_map/ppermute | solution.py:543
  143.4 1.9 %collective-permute-start.14 = (f32[32,128]{1,0:T(8,128)}, f32[32,128]{1,0:T(8,128)S(1)}, u32[]{:S(2)}, u32[]{:S(2)}) collective-permute-start(f32[32,128]{1,0:T(8,128)} %get-tuple-element.44), channel_id=1, source_target_pairs={{0,1},{1,2},{2,3},{3,4},{4,5},{5,6},{6,7},{8,9},{9,10},{10,11},{11... | collective-permute-start | bytes 49160 | tf_op jit(solution)/shard_map/ppermute | solution.py:543
  145.4 7.8 %collective-permute-start.15 = (f32[32,128]{1,0:T(8,128)}, f32[32,128]{1,0:T(8,128)S(1)}, u32[]{:S(2)}, u32[]{:S(2)}) collective-permute-start(f32[32,128]{1,0:T(8,128)} %get-tuple-element.45), channel_id=1, source_target_pairs={{1,0},{2,1},{3,2},{4,3},{5,4},{6,5},{7,6},{9,8},{10,9},{11,10},{12... | collective-permute-start | bytes 49160 | tf_op jit(solution)/shard_map/ppermute | solution.py:543
  153.2 1.6 collective-permute-done.15.refs_6_
  154.9 0.6 copy-done.13
  155.4 0.1 copy-done.6
  155.5 0.1 copy-done.7
  155.5 18.9 %heat_step_two.1 = f32[64,32,512]{2,1,0:T(8,128)} custom-call(f32[1]{0:T(128)} %get-tuple-element.49.refs_0_, f32[64,32,512]{2,1,0:T(8,128)} %get-tuple-element.41.refs_1_, f32[64,32,512]{2,1,0:T(8,128)} %get-tuple-element.23.refs_2_, f32[64,512]{1,0:T(8,128)} %copy-done.6, f32[64,512]{1,0:T(8,128)} %copy-done.7, f32[32,128]{1,0:T(8,128)} %copy-done.12, ...), custom_call_target="tpu_custom_call" | custom-call | tf_op jit(solution)/shard_map/heat_step_two/pallas_call | solution.py:525
  (32 shorter events, 0.1 us)
Async XLA Ops:
  1.4 11.5 %collective-permute-start.1 = (f32[6,256]{1,0:T(8,128)S(1)}, f32[6,256]{1,0:T(8,128)S(1)}, u32[]{:S(2)}, u32[]{:S(2)}) collective-permute-start(f32[6,256]{1,0:T(8,128)S(1)} %get-tuple-element.46), channel_id=1, source_target_pairs={{1,0},{2,1},{3,2},{4,3},{5,4},{6,5},{7,6},{8,7},{9,8},{10,9},{11,1... | collective-permute-start | bytes 18440 | tf_op jit(solution)/shard_map/ppermute | solution.py:543
  6.7 9.2 %collective-permute-start = (f32[6,256]{1,0:T(8,128)S(1)}, f32[6,256]{1,0:T(8,128)S(1)}, u32[]{:S(2)}, u32[]{:S(2)}) collective-permute-start(f32[6,256]{1,0:T(8,128)S(1)} %get-tuple-element.47), channel_id=1, source_target_pairs={{0,1},{1,2},{2,3},{3,4},{4,5},{5,6},{6,7},{7,8},{8,9},{9,10},{10,1... | collective-permute-start | bytes 18440 | tf_op jit(solution)/shard_map/ppermute | solution.py:543
  12.9 3.0 %copy-start.14 = (f32[6,256]{1,0:T(8,128)}, f32[6,256]{1,0:T(8,128)S(1)}, u32[]{:S(2)}) copy-start(f32[6,256]{1,0:T(8,128)S(1)} %collective-permute-done.1.halo_hi) | copy-start | bytes 18436
  15.9 0.6 copy-start.15
  36.7 22.8 %copy-start.16 = (f32[128,128]{1,0:T(8,128)S(1)}, f32[128,128]{1,0:T(8,128)}, u32[]{:S(2)}) copy-start(f32[128,128]{1,0:T(8,128)} %get-tuple-element.29) | copy-start | bytes 196612
  36.7 65.3 %copy-start.17 = (s32[2]{0:T(128)S(1)}, s32[2]{0:T(128)}, u32[]{:S(2)}) copy-start(s32[2]{0:T(128)} %param.19) | copy-start | bytes 28
  36.8 22.7 %collective-permute-start.2 = (f32[128,128]{1,0:T(8,128)}, f32[128,128]{1,0:T(8,128)S(1)}, u32[]{:S(2)}, u32[]{:S(2)}) collective-permute-start(f32[128,128]{1,0:T(8,128)} %get-tuple-element.28), channel_id=1, source_target_pairs={{0,8},{8,16},{16,24},{24,32},{32,40},{40,48},{48,56},{56,64},{64,7... | collective-permute-start | bytes 196616 | tf_op jit(solution)/shard_map/ppermute | solution.py:543
  42.3 52.0 %collective-permute-start.6 = (f32[32,128]{1,0:T(8,128)}, f32[32,128]{1,0:T(8,128)S(1)}, u32[]{:S(2)}, u32[]{:S(2)}) collective-permute-start(f32[32,128]{1,0:T(8,128)} %get-tuple-element.35), channel_id=1, source_target_pairs={{0,1},{1,2},{2,3},{3,4},{4,5},{5,6},{6,7},{8,9},{9,10},{10,11},{11... | collective-permute-start | bytes 49160 | tf_op jit(solution)/shard_map/ppermute | solution.py:543
  44.3 52.0 %collective-permute-start.7 = (f32[32,128]{1,0:T(8,128)}, f32[32,128]{1,0:T(8,128)S(1)}, u32[]{:S(2)}, u32[]{:S(2)}) collective-permute-start(f32[32,128]{1,0:T(8,128)} %get-tuple-element.36), channel_id=1, source_target_pairs={{1,0},{2,1},{3,2},{4,3},{5,4},{6,5},{7,6},{9,8},{10,9},{11,10},{12... | collective-permute-start | bytes 49160 | tf_op jit(solution)/shard_map/ppermute | solution.py:543
  51.8 59.6 %collective-permute-start.4 = (f32[64,512]{1,0:T(8,128)}, f32[64,512]{1,0:T(8,128)S(1)}, u32[]{:S(2)}, u32[]{:S(2)}) collective-permute-start(f32[64,512]{1,0:T(8,128)} %get-tuple-element.33), channel_id=1, source_target_pairs={{0,8},{8,16},{16,24},{24,32},{32,40},{40,48},{48,56},{56,64},{64,7... | collective-permute-start | bytes 393224 | tf_op jit(solution)/shard_map/ppermute | solution.py:543
  53.7 57.7 %collective-permute-start.5 = (f32[64,512]{1,0:T(8,128)}, f32[64,512]{1,0:T(8,128)S(1)}, u32[]{:S(2)}, u32[]{:S(2)}) collective-permute-start(f32[64,512]{1,0:T(8,128)} %get-tuple-element.34), channel_id=1, source_target_pairs={{8,0},{16,8},{24,16},{32,24},{40,32},{48,40},{56,48},{64,56},{72,6... | collective-permute-start | bytes 393224 | tf_op jit(solution)/shard_map/ppermute | solution.py:543
  59.5 4.6 %copy-start.2 = (f32[128,128]{1,0:T(8,128)}, f32[128,128]{1,0:T(8,128)S(1)}, u32[]{:S(2)}) copy-start(f32[128,128]{1,0:T(8,128)S(1)} %collective-permute-done.2.recv_lo) | copy-start | bytes 196612
  59.5 3.8 %collective-permute-start.3 = (f32[128,128]{1,0:T(8,128)S(1)}, f32[128,128]{1,0:T(8,128)S(1)}, u32[]{:S(2)}, u32[]{:S(2)}) collective-permute-start(f32[128,128]{1,0:T(8,128)S(1)} %copy-done.16), channel_id=1, source_target_pairs={{8,0},{16,8},{24,16},{32,24},{40,32},{48,40},{56,48},{64,56},{72,6... | collective-permute-start | bytes 196616 | tf_op jit(solution)/shard_map/ppermute | solution.py:543
  63.3 0.7 copy-start.3
  92.4 9.7 %collective-permute-start.10 = (f32[32,128]{1,0:T(8,128)}, f32[32,128]{1,0:T(8,128)S(1)}, u32[]{:S(2)}, u32[]{:S(2)}) collective-permute-start(f32[32,128]{1,0:T(8,128)} %get-tuple-element.39), channel_id=1, source_target_pairs={{0,1},{1,2},{2,3},{3,4},{4,5},{5,6},{6,7},{8,9},{9,10},{10,11},{11... | collective-permute-start | bytes 49160 | tf_op jit(solution)/shard_map/ppermute | solution.py:543
  94.3 17.1 %copy-start.10 = (f32[32,128]{1,0:T(8,128)}, f32[32,128]{1,0:T(8,128)S(1)}, u32[]{:S(2)}) copy-start(f32[32,128]{1,0:T(8,128)S(1)} %collective-permute-done.6.refs_5_) | copy-start | bytes 49156
  94.3 17.1 %collective-permute-start.8 = (f32[64,512]{1,0:T(8,128)}, f32[64,512]{1,0:T(8,128)S(1)}, u32[]{:S(2)}, u32[]{:S(2)}) collective-permute-start(f32[64,512]{1,0:T(8,128)} %get-tuple-element.37), channel_id=1, source_target_pairs={{0,8},{8,16},{16,24},{24,32},{32,40},{40,48},{48,56},{56,64},{64,7... | collective-permute-start | bytes 393224 | tf_op jit(solution)/shard_map/ppermute | solution.py:543
  96.3 15.2 %copy-start.11 = (f32[32,128]{1,0:T(8,128)}, f32[32,128]{1,0:T(8,128)S(1)}, u32[]{:S(2)}) copy-start(f32[32,128]{1,0:T(8,128)S(1)} %collective-permute-done.7.refs_6_) | copy-start | bytes 49156
  96.3 15.2 %collective-permute-start.9 = (f32[64,512]{1,0:T(8,128)}, f32[64,512]{1,0:T(8,128)S(1)}, u32[]{:S(2)}, u32[]{:S(2)}) collective-permute-start(f32[64,512]{1,0:T(8,128)} %get-tuple-element.38), channel_id=1, source_target_pairs={{8,0},{16,8},{24,16},{32,24},{40,32},{48,40},{56,48},{64,56},{72,6... | collective-permute-start | bytes 393224 | tf_op jit(solution)/shard_map/ppermute | solution.py:543
  102.1 9.4 %copy-start.8 = (f32[32,128]{1,0:T(8,128)}, f32[32,128]{1,0:T(8,128)S(1)}, u32[]{:S(2)}) copy-start(f32[32,128]{1,0:T(8,128)S(1)} %collective-permute-done.10.refs_9_) | copy-start | bytes 49156
  102.1 9.3 %collective-permute-start.11 = (f32[32,128]{1,0:T(8,128)}, f32[32,128]{1,0:T(8,128)S(1)}, u32[]{:S(2)}, u32[]{:S(2)}) collective-permute-start(f32[32,128]{1,0:T(8,128)} %get-tuple-element.40), channel_id=1, source_target_pairs={{1,0},{2,1},{3,2},{4,3},{5,4},{6,5},{7,6},{9,8},{10,9},{11,10},{12... | collective-permute-start | bytes 49160 | tf_op jit(solution)/shard_map/ppermute | solution.py:543
  111.4 0.6 copy-start.9
  111.4 0.7 copy-start.4
  111.4 0.7 copy-start.5
  111.4 0.7 copy-start
  111.4 0.8 copy-start.1
  135.8 19.1 %collective-permute-start.12 = (f32[64,512]{1,0:T(8,128)}, f32[64,512]{1,0:T(8,128)S(1)}, u32[]{:S(2)}, u32[]{:S(2)}) collective-permute-start(f32[64,512]{1,0:T(8,128)} %get-tuple-element.42), channel_id=1, source_target_pairs={{0,8},{8,16},{16,24},{24,32},{32,40},{40,48},{48,56},{56,64},{64,7... | collective-permute-start | bytes 393224 | tf_op jit(solution)/shard_map/ppermute | solution.py:543
  137.7 17.2 %collective-permute-start.13 = (f32[64,512]{1,0:T(8,128)}, f32[64,512]{1,0:T(8,128)S(1)}, u32[]{:S(2)}, u32[]{:S(2)}) collective-permute-start(f32[64,512]{1,0:T(8,128)} %get-tuple-element.43), channel_id=1, source_target_pairs={{8,0},{16,8},{24,16},{32,24},{40,32},{48,40},{56,48},{64,56},{72,6... | collective-permute-start | bytes 393224 | tf_op jit(solution)/shard_map/ppermute | solution.py:543
  143.4 9.8 %collective-permute-start.14 = (f32[32,128]{1,0:T(8,128)}, f32[32,128]{1,0:T(8,128)S(1)}, u32[]{:S(2)}, u32[]{:S(2)}) collective-permute-start(f32[32,128]{1,0:T(8,128)} %get-tuple-element.44), channel_id=1, source_target_pairs={{0,1},{1,2},{2,3},{3,4},{4,5},{5,6},{6,7},{8,9},{9,10},{10,11},{11... | collective-permute-start | bytes 49160 | tf_op jit(solution)/shard_map/ppermute | solution.py:543
  145.4 9.5 %collective-permute-start.15 = (f32[32,128]{1,0:T(8,128)}, f32[32,128]{1,0:T(8,128)S(1)}, u32[]{:S(2)}, u32[]{:S(2)}) collective-permute-start(f32[32,128]{1,0:T(8,128)} %get-tuple-element.45), channel_id=1, source_target_pairs={{1,0},{2,1},{3,2},{4,3},{5,4},{6,5},{7,6},{9,8},{10,9},{11,10},{12... | collective-permute-start | bytes 49160 | tf_op jit(solution)/shard_map/ppermute | solution.py:543
  153.2 1.6 copy-start.12
  154.8 0.6 copy-start.13
  154.8 0.7 copy-start.6
  154.8 0.7 copy-start.7

commit v2 on v1

v2 whole, which is shorter than its diff:
```python
import math

import jax
import jax.numpy as jnp
from jax import lax
from jax.experimental import pallas as pl
from jax.experimental.pallas import tpu as pltpu
from jax.sharding import PartitionSpec as P

F32 = jnp.float32
BF16 = jnp.bfloat16
I32 = jnp.int32

DEPTH = 64
CX = 32
CY = 512
NPART = 16384
G = 16
HB = 2
NB = 128
NEXT = NB + 2 * HB
SLOTS = 256
BAND = 64.0
BIN = 256
LOG2E = 1.4426950408889634
VMEM_LIMIT = 56 * 1024 * 1024
TILE_UNROLL = 32
WALK_UNROLL = 16
XW = CX + 4
BINS = 2 * XW
SEND = 128 + 8 * DEPTH

VSPEC = pl.BlockSpec(memory_space=pltpu.VMEM)
SSPEC = pl.BlockSpec(memory_space=pltpu.SMEM)
ASPEC = pl.BlockSpec(memory_space=pl.ANY)


def iota(shape, dim):
    return lax.broadcasted_iota(I32, shape, dim)


def partner(a, step, axis, low):
    size = a.shape[axis]
    return jnp.where(low, pltpu.roll(a, size - step, axis), pltpu.roll(a, step, axis))


def cross_stage(ks, cs, step, axis, low):
    nk, nc = [], []
    for k, c in zip(ks, cs):
        pk = partner(k, step, axis, low)
        pc = partner(c, step, axis, low)
        m = jnp.where(low, jnp.minimum(k, pk), jnp.maximum(k, pk))
        nk.append(m)
        nc.append(jnp.where(m != k, pc, c))
    return nk, nc


def vreg_stage(ks, cs, j, descending):
    ks, cs = list(ks), list(cs)
    for r in range(16):
        if r & (1 << j):
            continue
        a, b = r, r | (1 << j)
        if descending(r):
            a, b = b, a
        less = ks[b] < ks[a]
        ks[a], ks[b] = jnp.minimum(ks[a], ks[b]), jnp.maximum(ks[a], ks[b])
        cs[a], cs[b] = jnp.where(less, cs[b], cs[a]), jnp.where(less, cs[a], cs[b])
    return ks, cs


def bitonic(ks, cs):
    sub = iota((8, 128), 0)
    lane = iota((8, 128), 1)
    up = lambda r: False

    def low_stages(ks, cs, top):
        for j in range(top, 3, -1):
            step = 1 << (j - 4)
            ks, cs = cross_stage(ks, cs, step, 0, (sub & step) == 0)
        for j in range(min(top, 3), -1, -1):
            ks, cs = vreg_stage(ks, cs, j, up)
        return ks, cs

    for k in range(1, 4):
        for j in range(k - 1, -1, -1):
            ks, cs = vreg_stage(ks, cs, j, lambda r: bool(r & (1 << k)))
    for k in range(4, 7):
        flip = -((sub >> (k - 4)) & 1)
        ks = [a ^ flip for a in ks]
        ks, cs = low_stages(ks, cs, k - 1)
        ks = [a ^ flip for a in ks]

    def phase(k, carry):
        ks, cs = list(carry[:16]), list(carry[16:])
        flip = -((lane >> (k - 7)) & 1)
        ks = [a ^ flip for a in ks]

        def lane_step(t, inner):
            step = jnp.left_shift(jnp.int32(1), k - 8 - t)
            low = (lane & step) == 0
            nk, nc = cross_stage(list(inner[:16]), list(inner[16:]), step, 1, low)
            return tuple(nk) + tuple(nc)

        out = lax.fori_loop(0, k - 7, lane_step, tuple(ks) + tuple(cs))
        ks, cs = low_stages(list(out[:16]), list(out[16:]), 6)
        ks = [a ^ flip for a in ks]
        return tuple(ks) + tuple(cs)

    out = lax.fori_loop(7, 15, phase, tuple(ks) + tuple(cs))
    return list(out[:16]), list(out[16:])


def split3(a):
    h1 = a.astype(BF16)
    r = a - h1.astype(F32)
    h2 = r.astype(BF16)
    h3 = (r - h2.astype(F32)).astype(BF16)
    return h1, h2, h3


def particle_kernel(
    tgt, src, cnt, loc, vel, halo_lo, halo_hi, key, wb, urow,
    nloc, nvel, skey, schg, last, send_lo, send_hi,
    left, right, stat, acc, zrow,
):
    wide = 4 * 128

    def prepare(x3, v3, at, width):
        pad = jnp.zeros((5, width), F32)
        x = jnp.concatenate([x3, pad], axis=0)
        v = jnp.concatenate([v3, pad], axis=0)
        row = iota((8, width), 0)
        xs = x * math.sqrt(LOG2E)
        q = 0.5 * jnp.sum(xs * xs, axis=0, keepdims=True)
        full = jnp.where(row < 3, xs, jnp.where(row < 5, q, 0.0))
        h = [p.astype(F32) for p in split3(full)]

        def mix(a, b, is_target):
            base = h[a]
            if b is None:
                return jnp.where(row < 3, base, 0.0)
            if is_target:
                return jnp.where(row < 3, base, jnp.where(row == 3, h[b], jnp.where(row == 4, 1.0, 0.0)))
            return jnp.where(row < 3, base, jnp.where(row == 3, -1.0, jnp.where(row == 4, -h[b], 0.0)))

        extra = [0, 1, 2, None, None, None]
        ta = [0, 0, 1, 1, 0, 2]
        sa = [0, 1, 0, 1, 2, 0]
        for p in range(0, 6, 2):
            lt = jnp.concatenate([mix(ta[p], extra[p], True), mix(ta[p + 1], extra[p + 1], True)], axis=0)
            rt = jnp.concatenate([mix(sa[p], extra[p], False), mix(sa[p + 1], extra[p + 1], False)], axis=0)
            left[pl.ds(8 * p, 16), pl.ds(at, width)] = lt.astype(BF16)
            right[pl.ds(8 * p, 16), pl.ds(at, width)] = rt.astype(BF16)
        w = (2.0 * x - v) * (1.0 / 256.0)
        wh = w.astype(BF16).astype(F32)
        wl = w - wh
        w2 = jnp.concatenate([jnp.where(row == 3, 1.0, wh), wl], axis=0)
        stat[:, pl.ds(at, width)] = w2.astype(BF16)

    prepare(halo_lo[0:3, :], halo_lo[3:6, :], 0, HB * 128)
    prepare(halo_hi[0:3, :], halo_hi[3:6, :], (NB + HB) * 128, HB * 128)

    def prep(i, carry):
        at = pl.multiple_of(i * wide, wide)
        prepare(loc[:, pl.ds(at, wide)], vel[:, pl.ds(at, wide)], pl.multiple_of(at + HB * 128, 128), wide)
        return carry

    lax.fori_loop(0, NPART // wide, prep, 0)
    acc[...] = jnp.zeros_like(acc)
    live = cnt[0]

    def tiles(g, carry):
        outs = []
        for u in range(TILE_UNROLL):
            t = g * TILE_UNROLL + u
            a = tgt[t] & (NB - 1)
            b = a + (src[t] - tgt[t]) + HB
            lm = left[:, pl.ds(pl.multiple_of((a + HB) * 128, 128), 128)]
            rm = right[:, pl.ds(pl.multiple_of(b * 128, 128), 128)]
            arg = lax.dot_general(rm, lm, (((0,), (0,)), ((), ())), preferred_element_type=F32)
            g_mn = jnp.exp2(arg)
            gh = g_mn.astype(BF16)
            gl = (g_mn - gh.astype(F32)).astype(BF16)
            s = stat[:, pl.ds(pl.multiple_of(b * 128, 128), 128)]
            out = jnp.dot(
                jnp.concatenate([s, s], axis=1),
                jnp.concatenate([gh, gl], axis=0),
                preferred_element_type=F32,
            )
            home = jnp.where(t < live, a, NB)
            outs.append((home, out[0:8] + out[8:16]))
        for home, out in outs:
            at = pl.multiple_of(home * 8, 8)
            acc[pl.ds(at, 8), :] = acc[pl.ds(at, 8), :] + out
        return carry

    lax.fori_loop(0, (live + TILE_UNROLL - 1) // TILE_UNROLL, tiles, 0)

    def advance(i, carry):
        for u in range(8):
            b = i * 8 + u
            at = pl.multiple_of(b * 128, 128)
            x = loc[:, pl.ds(at, 128)]
            v = vel[:, pl.ds(at, 128)]
            f = acc[pl.ds(pl.multiple_of(b * 8, 8), 8), :]
            w = (2.0 * x - v) * (1.0 / 256.0)
            force = w * f[3:4] - f[0:3]
            nv = v + 0.5 * force
            nx = x + 0.5 * nv
            nvel[:, pl.ds(at, 128)] = nv
            nloc[:, pl.ds(at, 128)] = nx
            zrow[pl.ds(b, 1), :] = nx[2:3]
        return carry

    lax.fori_loop(0, NB // 8, advance, 0)

    charge = wb[...] * (1.0 + 0.5 * jnp.tanh(zrow[...]))
    keys = key[...]
    ks = [keys[8 * r : 8 * r + 8] for r in range(16)]
    cs = [charge[8 * r : 8 * r + 8] for r in range(16)]
    ks, cs = bitonic(ks, cs)
    last[...] = ks[15][7:8]
    kt = jnp.concatenate(ks, axis=0)
    ct = jnp.concatenate(cs, axis=0)
    kt = jnp.transpose(kt)
    ct = jnp.transpose(ct)
    skey[...] = kt
    schg[...] = ct
    for ref, at in ((send_lo, 0), (send_hi, 96)):
        kk = kt[at : at + 32]
        ref[0:32] = (kk >> 15).astype(F32)
        ref[32:64] = ((kk >> 6) & 511).astype(F32)
        ref[64:96] = (kk & 63).astype(F32)
        ref[96:128] = ct[at : at + 32]
    for r in range(4):
        ref = send_lo if r < 2 else send_hi
        for c in range(4):
            at = 128 + ((r % 2) * 4 + c) * DEPTH
            ref[at : at + DEPTH] = urow[r, :, 128 * c : 128 * c + 128]


def particles(tgt, src, cnt, loc, vel, halo_lo, halo_hi, key, wb, urow):
    sd = jax.ShapeDtypeStruct
    return pl.pallas_call(
        particle_kernel,
        out_shape=(
            sd((3, NPART), F32), sd((3, NPART), F32),
            sd((128, 128), I32), sd((128, 128), F32), sd((1, 128), I32),
            sd((SEND, 128), F32), sd((SEND, 128), F32),
        ),
        in_specs=[SSPEC] * 3 + [VSPEC] * 7,
        out_specs=(VSPEC,) * 7,
        scratch_shapes=[
            pltpu.VMEM((48, NEXT * 128), BF16),
            pltpu.VMEM((48, NEXT * 128), BF16),
            pltpu.VMEM((16, NEXT * 128), BF16),
            pltpu.VMEM(((NB + 1) * 8, 128), F32),
            pltpu.VMEM((NB, 128), F32),
        ],
        compiler_params=pltpu.CompilerParams(vmem_limit_bytes=VMEM_LIMIT),
        name="particle_step",
    )(tgt, src, cnt, loc, vel, halo_lo, halo_hi, key, wb, urow)


OWN, RECV = 128, 32


def profile(z, charge):
    level = iota((DEPTH, 128), 0).astype(F32)
    d = (level - z) * (math.sqrt(LOG2E) / 12.0)
    p = jnp.exp2(-(d * d)) * charge
    hi = p.astype(BF16)
    lo = (p - hi.astype(F32)).astype(BF16)
    return jnp.concatenate([hi, lo], axis=0)


def walk(pile, cells, prof, base, count, dummy, last_bin, first_bin, end_bin):
    spot = iota((BIN, 128), 0)

    def seek(i, s):
        b = last_bin(i)
        return s[0] + (b < first_bin).astype(I32), s[1] + (b <= end_bin).astype(I32)

    start, stop = lax.fori_loop(0, count, seek, (jnp.int32(0), jnp.int32(0)), unroll=8)
    stop = jnp.minimum(stop, count - 1)
    steps = stop - start + 1 + (end_bin - first_bin)

    def step(g, state):
        i, j = state
        work = []
        for u in range(WALK_UNROLL):
            work.append((jnp.where(i <= stop, base + i, dummy), j))
            more = jnp.logical_and(last_bin(jnp.minimum(i, count - 1)) > j, j < end_bin)
            j = jnp.where(more, j + 1, j)
            i = jnp.where(more, i, jnp.minimum(i + 1, count))
        outs = []
        for ii, jj in work:
            row = cells[pl.ds(ii, 1), :] - jj * BIN
            hot = jnp.where(spot == row, 1.0, 0.0).astype(BF16)
            out = lax.dot_general(prof[ii], hot, (((1,), (1,)), ((), ())), preferred_element_type=F32)
            outs.append(out[:DEPTH] + out[DEPTH:])
        for (ii, jj), out in zip(work, outs):
            pile[jj] = pile[jj] + out
        return i, j

    @pl.when(start <= stop)
    def _():
        lax.fori_loop(0, (steps + WALK_UNROLL - 1) // WALK_UNROLL, step, (start, jnp.int32(first_bin)))


def own_deposit_kernel(last, skey, schg, pile, row_lo, row_hi, cells, prof):
    own = skey[...]
    cells[0:OWN] = (own >> 6) - (G - HB) * CY
    cells[OWN : OWN + 8] = jnp.full((8, 128), -1, I32)
    prof[OWN] = jnp.zeros((128, 128), BF16)

    def profiles(i, carry):
        for u in range(8):
            b = i * 8 + u
            z = (skey[pl.ds(b, 1), :] & 63).astype(F32)
            prof[b] = profile(z, schg[pl.ds(b, 1), :])
        return carry

    lax.fori_loop(0, OWN // 8, profiles, 0)

    def clear(i, carry):
        pile[i] = jnp.zeros((DEPTH, BIN), F32)
        return carry

    lax.fori_loop(0, BINS, clear, 0)
    walk(pile, cells, prof, 0, OWN, OWN, lambda i: (last[i] >> 14) - 2 * (G - HB), 0, BINS - 1)
    for ref, x0 in ((row_lo, 0), (row_hi, CX - 2)):
        for r in range(2):
            for c in range(4):
                at = (r * 4 + c) * DEPTH
                ref[at : at + DEPTH] = pile[2 * (x0 + r + 2) + c // 2, :, 128 * (c % 2) : 128 * (c % 2) + 128]


def own_deposit(last, skey, schg):
    sd = jax.ShapeDtypeStruct
    return pl.pallas_call(
        own_deposit_kernel,
        out_shape=(sd((BINS, DEPTH, BIN), F32), sd((8 * DEPTH, 128), F32), sd((8 * DEPTH, 128), F32)),
        in_specs=[SSPEC, VSPEC, VSPEC],
        out_specs=(VSPEC,) * 3,
        scratch_shapes=[
            pltpu.VMEM((OWN + 8, 128), I32),
            pltpu.VMEM((OWN + 1, 128, 128), BF16),
        ],
        compiler_params=pltpu.CompilerParams(vmem_limit_bytes=VMEM_LIMIT),
        name="own_deposit",
    )(last, skey, schg)


def edge_deposit_kernel(
    last_lo, last_hi, meta, pile_in, recv_lo, recv_hi, part_lo, part_hi, ucol,
    pile_out, vrow, pay_lo, pay_hi,
    pile, cells, prof, packs, sems,
):
    load = pltpu.make_async_copy(pile_in, pile, sems.at[0])
    load.start()
    for ref, at, shift in ((recv_lo, 0, HB - G - CX), (recv_hi, RECV, HB + CX - G)):
        x = ref[0:32].astype(I32) + shift
        cells[at : at + RECV] = x * CY + ref[32:64].astype(I32)
    dummy = 2 * RECV
    cells[dummy : dummy + 8] = jnp.full((8, 128), -1, I32)
    prof[dummy] = jnp.zeros((128, 128), BF16)

    def profiles(i, carry):
        for ref, at in ((recv_lo, 0), (recv_hi, RECV)):
            for u in range(4):
                b = i * 4 + u
                prof[at + b] = profile(ref[pl.ds(64 + b, 1), :], ref[pl.ds(96 + b, 1), :])
        return carry

    lax.fori_loop(0, RECV // 4, profiles, 0)
    load.wait()
    half = 2 * (2 + G)
    walk(pile, cells, prof, 0, RECV, dummy, lambda i: last_lo[i], 4, half - 1)
    walk(pile, cells, prof, RECV, RECV, dummy, lambda i: last_hi[i], half, 2 * (2 + CX) - 1)
    for ref, x0, flag in ((part_lo, 0, meta[2]), (part_hi, CX + 2, meta[3])):
        for r in range(2):
            for c in range(4):
                at = (r * 4 + c) * DEPTH
                b = 2 * (x0 + r) + c // 2
                cols = slice(128 * (c % 2), 128 * (c % 2) + 128)
                pile[b, :, cols] = flag * (pile[b, :, cols] + ref[at : at + DEPTH])
    save = pltpu.make_async_copy(pile, pile_out, sems.at[0])
    save.start()
    for n, x in enumerate((0, 1, 2, CX + 1, CX + 2, CX + 3)):
        vrow[n, :, :BIN] = pile[2 * x]
        vrow[n, :, BIN:] = pile[2 * x + 1]
    lane = iota((DEPTH, 128), 1)
    packs[...] = jnp.zeros_like(packs)

    def pick(row, at):
        a = pile[2 * row, :, 0:128]
        b = pile[2 * row + 1, :, 128:256]
        for n, (t, by) in enumerate(((a, at), (a, at + 127), (b, at + 2), (b, at + 1))):
            packs[n] = jnp.where(lane == at, pltpu.roll(t, by & 127, 1), packs[n])

    def picks(x, carry):
        pick(x + 2, x)
        return carry

    lax.fori_loop(0, CX, picks, 0)
    pick(1, CX)
    pick(CX + 2, CX + 1)
    base = 128 + 4 * DEPTH
    for pay, recv_col, near, far in ((pay_lo, 0, 0, 1), (pay_hi, 3, 3, 2)):
        lo = recv_lo[base + recv_col * DEPTH : base + recv_col * DEPTH + DEPTH]
        hi = recv_hi[128 + recv_col * DEPTH : 128 + recv_col * DEPTH + DEPTH]
        by = 0 if recv_col == 0 else 1
        corner = jnp.where(lane == CX, pltpu.roll(lo, CX + by, 1), 0.0)
        corner = jnp.where(lane == CX + 1, pltpu.roll(hi, CX + 1 + by, 1), corner)
        t = jnp.transpose(jnp.concatenate([corner, packs[near]], axis=0))
        pay[0:CX] = t[0:CX] + ucol[near]
        pay[CX : CX + 8] = t[CX : CX + 8]
        t = jnp.transpose(jnp.concatenate([jnp.zeros((DEPTH, 128), F32), packs[far]], axis=0))
        pay[40 : 40 + CX] = t[0:CX] + ucol[far]
        pay[40 + CX : 80] = jnp.zeros((8, 128), F32)
    save.wait()


def edge_deposit(last_lo, last_hi, meta, pile, recv_lo, recv_hi, part_lo, part_hi, ucol):
    sd = jax.ShapeDtypeStruct
    return pl.pallas_call(
        edge_deposit_kernel,
        out_shape=(
            sd((BINS, DEPTH, BIN), F32), sd((6, DEPTH, CY), F32),
            sd((80, 128), F32), sd((80, 128), F32),
        ),
        in_specs=[SSPEC] * 3 + [ASPEC] + [VSPEC] * 5,
        out_specs=(ASPEC, VSPEC, VSPEC, VSPEC),
        scratch_shapes=[
            pltpu.VMEM((BINS, DEPTH, BIN), F32),
            pltpu.VMEM((2 * RECV + 8, 128), I32),
            pltpu.VMEM((2 * RECV + 1, 128, 128), BF16),
            pltpu.VMEM((4, DEPTH, 128), F32),
            pltpu.SemaphoreType.DMA((1,)),
        ],
        compiler_params=pltpu.CompilerParams(vmem_limit_bytes=VMEM_LIMIT),
        name="edge_deposit",
    )(last_lo, last_hi, meta, pile, recv_lo, recv_hi, part_lo, part_hi, ucol)


def share_kernel(pile, share):
    sub = iota((8, CY), 0)

    def turn(xg, carry):
        x0 = pl.multiple_of(xg * 8, 8)
        a = [
            jnp.concatenate([pile[2 * (x0 + i + 2)], pile[2 * (x0 + i + 2) + 1]], axis=1)
            for i in range(8)
        ]
        for d in (1, 2, 4):
            b = list(a)
            low = (sub & d) == 0
            for i in range(8):
                if i & d:
                    continue
                p, q = a[i], a[i | d]
                b[i] = jnp.where(low, p, pltpu.roll(q, d, 0))
                b[i | d] = jnp.where(low, pltpu.roll(p, 8 - d, 0), q)
            a = b
        for k in range(8):
            share[k, pl.ds(x0, 8), :] = a[k]
        return carry

    lax.fori_loop(0, CX // 8, turn, 0)


def share_layout(pile):
    return pl.pallas_call(
        share_kernel,
        grid=(DEPTH // 8,),
        out_shape=jax.ShapeDtypeStruct((DEPTH, CX, CY), F32),
        in_specs=[pl.BlockSpec((BINS, 8, BIN), lambda i: (0, i, 0))],
        out_specs=pl.BlockSpec((8, CX, CY), lambda i: (i, 0, 0)),
        compiler_params=pltpu.CompilerParams(vmem_limit_bytes=VMEM_LIMIT),
        cost_estimate=pl.CostEstimate(flops=1 << 23, bytes_accessed=1 << 23, transcendentals=0),
        name="share_layout",
    )(pile)


def edges_kernel(left, right, top, bottom, urow, ucol):
    urow[0] = top[:, 0, :]
    urow[1] = top[:, 1, :]
    urow[2] = bottom[:, 6, :]
    urow[3] = bottom[:, 7, :]
    lane = iota((CX, 128), 1)
    acc = [jnp.zeros((CX, 128), F32)] * 4
    for z in range(DEPTH):
        for n, (ref, by) in enumerate(((left, z), (left, z + 127), (right, z + 2), (right, z + 1))):
            by = by & 127
            a = ref[z] if by == 0 else pltpu.roll(ref[z], by, 1)
            acc[n] = jnp.where(lane == z, a, acc[n])
    for n in range(4):
        ucol[n] = acc[n]


def edges(cells):
    sd = jax.ShapeDtypeStruct
    return pl.pallas_call(
        edges_kernel,
        grid=(1,),
        out_shape=(sd((4, DEPTH, CY), F32), sd((4, CX, 128), F32)),
        in_specs=[
            pl.BlockSpec((DEPTH, CX, 128), lambda i: (0, 0, 0)),
            pl.BlockSpec((DEPTH, CX, 128), lambda i: (0, 0, CY // 128 - 1)),
            pl.BlockSpec((DEPTH, 8, CY), lambda i: (0, 0, 0)),
            pl.BlockSpec((DEPTH, 8, CY), lambda i: (0, CX // 8 - 1, 0)),
        ],
        out_specs=(
            pl.BlockSpec((4, DEPTH, CY), lambda i: (0, 0, 0)),
            pl.BlockSpec((4, CX, 128), lambda i: (0, 0, 0)),
        ),
        compiler_params=pltpu.CompilerParams(vmem_limit_bytes=VMEM_LIMIT),
        name="temperature_edges",
    )(cells, cells, cells, cells)


def half_kappa(u, v):
    return 0.05 * (1.0 + 0.5 * jnp.tanh(u)) / (1.0 + v)


def flux(k, kn, u, un):
    return (k + kn) * (un - u)


def heat_kernel(
    meta, u_hbm, v_hbm, urow, recv_lo, recv_hi, vrow, pay_lo, pay_hi, got_lo, got_hi, out_hbm,
    us, vs, ms, kz, fz, row1, row2, mrow, col1, col2, sems,
):
    chunks = DEPTH // 8

    def fetch(c):
        at = pl.ds(pl.multiple_of(c * 8, 8), 8)
        return (
            pltpu.make_async_copy(u_hbm.at[at], us.at[at], sems.at[0, c]),
            pltpu.make_async_copy(v_hbm.at[at], vs.at[at], sems.at[1, c]),
        )

    for c in range(chunks):
        for copy in fetch(c):
            copy.start()

    def glow_of(rows):
        d = rows * (1.0 / BAND)
        return 0.5 * jnp.exp(-(d * d))

    lane = iota((CX, 128), 1)
    sub = iota((CX, 128), 0)
    lo_half = lane < DEPTH
    side = jnp.where(lo_half, meta[4], meta[5])
    glow1 = glow_of(sub.astype(F32) + meta[0])

    def stacks(a, b, at, size):
        p, q = a[at : at + size], b[at : at + size]
        low = iota((size, 128), 1) < DEPTH
        return jnp.where(low, p, pltpu.roll(q, DEPTH, 1)), jnp.where(low, pltpu.roll(p, DEPTH, 1), q)

    def column_step(outer, here, inner, ends):
        (uo, vo), (uh, vh), (ui, vi), (ue, ve) = outer, here, inner, ends
        kh = half_kappa(uh, vh)
        ke = half_kappa(ue, ve)
        total = flux(kh, half_kappa(uo, vo), uh, uo) + flux(kh, half_kappa(ui, vi), uh, ui)

        def near(a, e, n, pad):
            below = jnp.where(sub == 0, e[0:1], pltpu.roll(a, 1, 0))
            above = jnp.where(sub == CX - 1, e[1:2], pltpu.roll(a, CX - 1, 0))
            up = jnp.where((lane & (DEPTH - 1)) == DEPTH - 1, pad, pltpu.roll(a, 127, 1))
            down = jnp.where((lane & (DEPTH - 1)) == 0, pad, pltpu.roll(a, 1, 1))
            return below, above, up, down

        for kn, un in zip(near(kh, ke, 0, 0.05), near(uh, ue, 0, 0.0)):
            total = total + flux(kh, kn, uh, un)
        return uh + total + glow1 * vh, kh

    outer = stacks(got_lo, got_hi, 40, CX)
    here = stacks(got_lo, got_hi, 0, CX)
    inner = stacks(pay_lo, pay_hi, 0, CX)
    next_in = stacks(pay_lo, pay_hi, 40, CX)
    corners = stacks(got_lo, got_hi, CX, 8)
    mid_out, k_out = column_step(outer, here, inner, corners)
    mid_in, k_in = column_step(here, inner, next_in, stacks(pay_lo, pay_hi, CX, 8))
    mid_out = mid_out * side
    sign = jnp.where(lo_half, 1.0, -1.0)
    col1[...] = sign * flux(k_out, k_in, here[0], inner[0])
    col2[...] = sign * flux(half_kappa(mid_out, here[1]), half_kappa(mid_in, inner[1]), mid_out, mid_in)

    lane_w = iota((DEPTH, CY), 1)
    sub_w = iota((DEPTH, CY), 0)
    tail = [jnp.transpose(jnp.concatenate([g[CX : CX + 8]] * 16, axis=0)) for g in (got_lo, got_hi)]
    for n in range(2):
        recv = recv_lo if n == 0 else recv_hi

        def got_row(r):
            base = 128 + r * 4 * DEPTH
            return jnp.concatenate([recv[base + c * DEPTH : base + (c + 1) * DEPTH] for c in range(4)], axis=1)

        uo, uh = (got_row(0), got_row(1)) if n == 0 else (got_row(1), got_row(0))
        ui = urow[0] if n == 0 else urow[3]
        vo, vh, vi = (vrow[0], vrow[1], vrow[2]) if n == 0 else (vrow[5], vrow[4], vrow[3])
        kh = half_kappa(uh, vh)
        ki = half_kappa(ui, vi)
        total = flux(kh, half_kappa(uo, vo), uh, uo) + flux(kh, ki, uh, ui)
        first_u = pltpu.roll(tail[0][:DEPTH], (128 - n) & 127, 1) if n else tail[0][:DEPTH]
        first_v = pltpu.roll(tail[0][DEPTH:], (128 - n) & 127, 1) if n else tail[0][DEPTH:]
        end_u = pltpu.roll(tail[1][:DEPTH], 127 - n, 1)
        end_v = pltpu.roll(tail[1][DEPTH:], 127 - n, 1)
        first_k, end_k = half_kappa(first_u, first_v), half_kappa(end_u, end_v)

        def near(a, first, end, pad):
            left = jnp.where(lane_w == 0, jnp.concatenate([first] * 4, axis=1), pltpu.roll(a, 1, 1))
            right = jnp.where(lane_w == CY - 1, jnp.concatenate([end] * 4, axis=1), pltpu.roll(a, CY - 1, 1))
            up = jnp.where(sub_w == DEPTH - 1, pad, pltpu.roll(a, DEPTH - 1, 0))
            down = jnp.where(sub_w == 0, pad, pltpu.roll(a, 1, 0))
            return left, right, up, down

        for kn, un in zip(near(kh, first_k, end_k, 0.05), near(uh, first_u, end_u, 0.0)):
            total = total + flux(kh, kn, uh, un)
        row_at = meta[0] + (-1.0 if n == 0 else float(CX))
        gl = glow_of(jnp.full((1, CY), 1.0, F32) * row_at)
        mrow[DEPTH * n : DEPTH * n + DEPTH] = (uh + total + gl * vh) * meta[2 + n]
        row1[DEPTH * n : DEPTH * n + DEPTH] = flux(kh, ki, uh, ui) if n == 0 else flux(ki, kh, ui, uh)

    glow2 = glow_of(sub.astype(F32) + meta[1])
    tiles = range(4)

    def load(ref, z):
        return [ref[z, :, 128 * c : 128 * c + 128] for c in tiles]

    def plane(src, dst, row_f, col_f, glow, z, is_last):
        u = load(src, z)
        k = load(kz, z & 1)
        v = load(vs, z)
        if is_last:
            up = [(k[c] + 0.05) * (0.0 - u[c]) for c in tiles]
        else:
            un = load(src, z + 1)
            vn = load(vs, z + 1)
            kn = [half_kappa(un[c], vn[c]) for c in tiles]
            for c in tiles:
                kz[(z + 1) & 1, :, 128 * c : 128 * c + 128] = kn[c]
            up = [flux(k[c], kn[c], u[c], un[c]) for c in tiles]
        cols = col_f[...]
        row_first = row_f[pl.ds(z, 1), :]
        row_end = row_f[pl.ds(z + DEPTH, 1), :]
        edge0 = pltpu.roll(cols, (128 - z) & 127, 1)
        edge1 = pltpu.roll(cols, 63 - z, 1)
        ru = [pltpu.roll(u[c], 1, 1) for c in tiles]
        rk = [pltpu.roll(k[c], 1, 1) for c in tiles]
        g = []
        for c in tiles:
            if c == 0:
                g.append(jnp.where(lane == 0, edge0, flux(k[0], rk[0], ru[0], u[0])))
            else:
                pu = jnp.where(lane == 0, ru[c - 1], ru[c])
                pk = jnp.where(lane == 0, rk[c - 1], rk[c])
                g.append(flux(k[c], pk, pu, u[c]))
        rg = [pltpu.roll(g[c], 127, 1) for c in tiles]
        for c in tiles:
            at = slice(128 * c, 128 * c + 128)
            gn = jnp.where(lane == 127, rg[c + 1] if c < 3 else edge1, rg[c])
            f = flux(k[c], pltpu.roll(k[c], 1, 0), pltpu.roll(u[c], 1, 0), u[c])
            f = jnp.where(sub == 0, row_first[:, at], f)
            fn = jnp.where(sub == CX - 1, row_end[:, at], pltpu.roll(f, CX - 1, 0))
            total = (up[c] - fz[:, at]) + (fn - f) + (gn - g[c])
            fz[:, at] = up[c]
            dst[z, :, at] = u[c] + total + glow * v[c]

    def begin(src):
        u = load(src, 0)
        v = load(vs, 0)
        for c in tiles:
            at = slice(128 * c, 128 * c + 128)
            k = half_kappa(u[c], v[c])
            kz[0, :, at] = k
            fz[:, at] = (k + 0.05) * u[c]

    for copy in fetch(0):
        copy.wait()
    begin(us)

    def one(z, carry):
        @pl.when((z & 7) == 7)
        def _():
            for copy in fetch((z >> 3) + 1):
                copy.wait()

        plane(us, ms, row1, col1, glow1, z, False)
        return carry

    lax.fori_loop(0, DEPTH - 1, one, 0)
    plane(us, ms, row1, col1, glow1, DEPTH - 1, True)

    for n in range(2):
        mh = mrow[DEPTH * n : DEPTH * n + DEPTH]
        kh = half_kappa(mh, vrow[1] if n == 0 else vrow[4])
        mi = ms[:, 0 if n == 0 else CX - 1, :]
        ki = half_kappa(mi, vrow[2] if n == 0 else vrow[3])
        row2[DEPTH * n : DEPTH * n + DEPTH] = flux(kh, ki, mh, mi) if n == 0 else flux(ki, kh, mi, mh)

    def store(c):
        at = pl.ds(pl.multiple_of(c * 8, 8), 8)
        return pltpu.make_async_copy(us.at[at], out_hbm.at[at], sems.at[0, c])

    begin(ms)

    def two(z, carry):
        plane(ms, us, row2, col2, glow2, z, False)

        @pl.when((z & 7) == 7)
        def _():
            store(z >> 3).start()

        return carry

    lax.fori_loop(0, DEPTH - 1, two, 0)
    plane(ms, us, row2, col2, glow2, DEPTH - 1, True)
    store(chunks - 1).start()
    for c in range(chunks):
        store(c).wait()


def heat(meta, u, v, urow, recv_lo, recv_hi, vrow, pay_lo, pay_hi, got_lo, got_hi):
    plane = pltpu.VMEM((DEPTH, CX, CY), F32)
    rows = pltpu.VMEM((2 * DEPTH, CY), F32)
    column = pltpu.VMEM((CX, 128), F32)
    return pl.pallas_call(
        heat_kernel,
        out_shape=jax.ShapeDtypeStruct((DEPTH, CX, CY), F32),
        in_specs=[SSPEC, ASPEC, ASPEC] + [VSPEC] * 8,
        out_specs=ASPEC,
        scratch_shapes=[
            plane, plane, plane,
            pltpu.VMEM((2, CX, CY), F32), pltpu.VMEM((CX, CY), F32),
            rows, rows, rows, column, column,
            pltpu.SemaphoreType.DMA((2, DEPTH // 8)),
        ],
        compiler_params=pltpu.CompilerParams(vmem_limit_bytes=VMEM_LIMIT),
        name="two_heat_steps",
    )(meta, u, v, urow, recv_lo, recv_hi, vrow, pay_lo, pay_hi, got_lo, got_hi)


def shift(value, axis, steps):
    count = lax.axis_size(axis)
    first, stop = max(0, -steps), min(count, count - steps)
    return lax.ppermute(value, axis, [(i, i + steps) for i in range(first, stop)])


def body(
    particle_locations,
    particle_speeds,
    particle_bulk,
    receiving_group_per_pair,
    emitting_group_per_pair,
    active_pair_slots,
    landing_site_triple,
    landing_weight_octants,
    thermal_excess,
    molten_strip_midlines,
):
    states = jnp.concatenate([particle_locations, particle_speeds], axis=0)
    width = HB * 128
    halo_lo = shift(states[:, NPART - width :], ("gx", "gy"), 1)
    halo_hi = shift(states[:, :width], ("gx", "gy"), -1)
    urow, ucol = edges(thermal_excess)

    gx, gy = lax.axis_index("gx"), lax.axis_index("gy")
    row_start, col_start = gx * CX, gy * CY
    beam = row_start - molten_strip_midlines
    inside = jnp.stack([gx > 0, gx < lax.axis_size("gx") - 1, gy > 0, gy < lax.axis_size("gy") - 1])
    meta = jnp.concatenate([beam.astype(F32), inside.astype(F32)])
    px = landing_site_triple[1] - row_start + G
    py = landing_site_triple[2] - col_start
    key = ((px * CY + py) * DEPTH + landing_site_triple[0]).reshape(128, 128)
    wb = (particle_bulk * landing_weight_octants.astype(F32) * 0.125).reshape(128, 128)

    nloc, nvel, skey, schg, last, send_lo, send_hi = particles(
        receiving_group_per_pair, emitting_group_per_pair, active_pair_slots,
        particle_locations, particle_speeds, halo_lo, halo_hi, key, wb, urow,
    )
    recv_lo = shift(send_hi, "gx", 1)
    recv_hi = shift(send_lo, "gx", -1)
    pile, row_lo, row_hi = own_deposit(last.reshape(128), skey, schg)
    part_lo = shift(row_hi, "gx", 1)
    part_hi = shift(row_lo, "gx", -1)

    def last_bins(got, by):
        cell = (got[0:32, 127].astype(I32) + by) * CY + got[32:64, 127].astype(I32)
        return cell >> 8

    pile, vrow, pay_lo, pay_hi = edge_deposit(
        last_bins(recv_lo, HB - G - CX), last_bins(recv_hi, HB + CX - G), meta,
        pile, recv_lo, recv_hi, part_lo, part_hi, ucol,
    )
    got_lo = shift(pay_hi, "gy", 1)
    got_hi = shift(pay_lo, "gy", -1)
    share = share_layout(pile)
    final = heat(meta, thermal_excess, share, urow, recv_lo, recv_hi, vrow, pay_lo, pay_hi, got_lo, got_hi)
    return nloc, nvel, share, final


def solution(mesh):
    placed = (
        P(None, ("gx", "gy")),
        P(None, ("gx", "gy")),
        P(("gx", "gy")),
        P(("gx", "gy")),
        P(("gx", "gy")),
        P(("gx", "gy")),
        P(None, ("gx", "gy")),
        P(("gx", "gy")),
        P(None, "gx", "gy"),
        P(),
    )
    return jax.shard_map(
        body,
        mesh=mesh,
        in_specs=placed,
        out_specs=(
            P(None, ("gx", "gy")),
            P(None, ("gx", "gy")),
            P(None, "gx", "gy"),
            P(None, "gx", "gy"),
        ),
        check_vma=False,
    )
```

time: 176 us -> 120 us (0.68)
  starting transfers between devices: 63 us -> 32.9 us
  Pallas kernels: 94.6 us -> 72.7 us
  waiting for transfers between devices: 6.71 us -> 2.87 us
    ppermute x16 -> x8, starting transfers between devices: 63 us -> 32.9 us  [shift(): lax.ppermute(value, axis, [(i, i + steps) for i in range(first, stop)])]
    pallas_call x4 -> x5, Pallas kernels: 74.3 us -> 62.2 us  [the longest x1 28.8 us: heat(): pl.pallas_call(heat_kernel, out_shape=jax.ShapeDtypeStruct((DEPTH, CX, CY...]
    pallas_call x1, Pallas kernels: 20.3 us -> 10.5 us  [particles(): pl.pallas_call(particle_kernel, out_shape=(sd((3, NPART), F32), sd((3, NP...]
    ppermute x16 -> x8, waiting for transfers between devices: 6.71 us -> 2.87 us  [shift(): lax.ppermute(value, axis, [(i, i + steps) for i in range(first, stop)])]
  transfers between devices with their start and end apart: 16 -> 8, of which waited for: 4 -> 3; matrix products, arithmetic and copies ran while one was open for 3% -> 5% of each run, Pallas kernels for 18% -> 18%
where the time goes in v2:
time: 120 us; the launch traced here: 118 us
  Pallas kernels  72.7 us (61%)
  starting transfers between devices  32.9 us (27%)
  other arithmetic  6.34 us (5%)
  waiting for transfers between devices  2.87 us (2%)
  local copies, waits for them, and re-layouts  1.91 us (2%)
  between operations  1.43 us (1%)
    ppermute x8, starting transfers between devices, shift(): lax.ppermute(value, axis, [(i, i + steps) for i in range(first, stop)])  32.9 us
    pallas_call x1, Pallas kernels, heat(): pl.pallas_call(heat_kernel, out_shape=jax.ShapeDtypeStruct((DEPTH, CX, CY...  28.8 us
    pallas_call x1, Pallas kernels, edge_deposit(): pl.pallas_call(edge_deposit_kernel, out_shape=(sd((BINS, DEPTH, BIN), F32...  11.9 us
    pallas_call x1, Pallas kernels, particles(): pl.pallas_call(particle_kernel, out_shape=(sd((3, NPART), F32), sd((3, NP...  10.5 us
    pallas_call x1, Pallas kernels, own_deposit(): pl.pallas_call(own_deposit_kernel, out_shape=(sd((BINS, DEPTH, BIN), F32)...  10.1 us
    pallas_call x1, Pallas kernels, share_layout(): pl.pallas_call(share_kernel, grid=(DEPTH // 8,), out_shape=jax.ShapeDtype...  7.1 us
    pallas_call x1, Pallas kernels, edges(): pl.pallas_call(edges_kernel, grid=(1,), out_shape=(sd((4, DEPTH, CY), F32...  4.26 us
    ppermute x8, waiting for transfers between devices, shift(): lax.ppermute(value, axis, [(i, i + steps) for i in range(first, stop)])  2.87 us
  transfers between devices with their start and end apart: 8, of which 3 were waited for; matrix products, arithmetic and copies ran while one was open for 5% of the time, Pallas kernels for 18%

profile of v2, /device:TPU:24, one launch (start us, length us, event | category | flops | bytes accessed | tf_op | source)
XLA Modules:
  0.0 118.2 jit_solution(8656013616144602256)
XLA Ops:
  0.6 0.7 pad_maximum_fusion
  1.4 5.3 %collective-permute-start.1 = (f32[6,256]{1,0:T(8,128)S(1)}, f32[6,256]{1,0:T(8,128)S(1)}, u32[]{:S(2)}, u32[]{:S(2)}) collective-permute-start(f32[6,256]{1,0:T(8,128)S(1)} %get-tuple-element.36), channel_id=1, source_target_pairs={{1,0},{2,1},{3,2},{4,3},{5,4},{6,5},{7,6},{8,7},{9,8},{10,9},{11,1... | collective-permute-start | bytes 18440 | tf_op jit(solution)/shard_map/ppermute | solution.py:751
  6.7 1.9 %collective-permute-start = (f32[6,256]{1,0:T(8,128)S(1)}, f32[6,256]{1,0:T(8,128)S(1)}, u32[]{:S(2)}, u32[]{:S(2)}) collective-permute-start(f32[6,256]{1,0:T(8,128)S(1)} %get-tuple-element.37), channel_id=1, source_target_pairs={{0,1},{1,2},{2,3},{3,4},{4,5},{5,6},{6,7},{7,8},{8,9},{9,10},{10,1... | collective-permute-start | bytes 18440 | tf_op jit(solution)/shard_map/ppermute | solution.py:751
  8.7 2.0 %multiply_add_fusion = s32[1,16384]{1,0:T(1,128)} fusion(s32[3,16384]{1,0:T(4,128)} %param.16, s32[]{:T(128)S(6)} %mul.41, s32[]{:T(128)S(6)} %mul.38), kind=kLoop, calls=%fused_computation | loop fusion | flops 114688 | bytes 262152 | tf_op jit(solution)/shard_map/add | solution.py:779
  10.7 1.5 %multiply_bitcast_fusion.wb = f32[128,128]{1,0:T(8,128)} fusion(f32[16384]{0:T(1024)} %param.12, s32[16384]{0:T(1024)} %param.17), kind=kLoop, calls=%fused_computation.1 | loop fusion | flops 49152 | bytes 196608 | tf_op jit(solution)/shard_map/reshape | solution.py:780
  12.8 0.0 copy-start.8
  12.8 4.3 %temperature_edges.1 = (f32[4,64,512]{2,1,0:T(8,128)}, f32[4,32,128]{2,1,0:T(8,128)}) custom-call(f32[64,32,512]{2,1,0:T(8,128)} %u_hbm.1, f32[64,32,512]{2,1,0:T(8,128)} %u_hbm.1, f32[64,32,512]{2,1,0:T(8,128)} %u_hbm.1, f32[64,32,512]{2,1,0:T(8,128)} %u_hbm.1), custom_call_target="tpu_custom_call" | custom-call | tf_op jit(solution)/shard_map/temperature_edges/pallas_call | solution.py:505
  17.1 0.0 collective-permute-done.1.halo_hi
  17.1 0.0 copy-start.6
  17.1 0.0 collective-permute-done.halo_lo
  17.1 0.0 copy-start.7
  17.1 0.6 copy-done.6
  17.7 0.0 copy-done.7
  17.7 10.5 %particle_step.1 = (f32[3,16384]{1,0:T(4,128)}, f32[3,16384]{1,0:T(4,128)}, s32[128,128]{1,0:T(8,128)}, f32[128,128]{1,0:T(8,128)}, s32[1,128]{1,0:T(1,128)}, /*index=5*/f32[640,128]{1,0:T(8,128)}, f32[640,128]{1,0:T(8,128)}) custom-call(s32[256]{0:T(256)} %tgt.1, s32[256]{0:T(256)} %src.1, s32[1]{0:T(128)S(6)} %copy.14.cnt, f32[3,16384]{1,0:T(4,128)} %loc.1, ...), custom_call_target="tpu_custom_call" | custom-call | tf_op jit(solution)/shard_map/particle_step/pallas_call | solution.py:245
  28.2 2.3 %collective-permute-start.2 = (f32[640,128]{1,0:T(8,128)}, f32[640,128]{1,0:T(8,128)S(1)}, u32[]{:S(2)}, u32[]{:S(2)}) collective-permute-start(f32[640,128]{1,0:T(8,128)} %get-tuple-element.23), channel_id=1, source_target_pairs={{0,8},{8,16},{16,24},{24,32},{32,40},{40,48},{48,56},{56,64},{64,7... | collective-permute-start | bytes 983048 | tf_op jit(solution)/shard_map/ppermute | solution.py:751
  30.6 0.0 copy-done.8
  30.6 5.4 %collective-permute-start.3 = (f32[640,128]{1,0:T(8,128)}, f32[640,128]{1,0:T(8,128)S(1)}, u32[]{:S(2)}, u32[]{:S(2)}) collective-permute-start(f32[640,128]{1,0:T(8,128)} %get-tuple-element.24), channel_id=1, source_target_pairs={{8,0},{16,8},{24,16},{32,24},{40,32},{48,40},{56,48},{64,56},{72,6... | collective-permute-start | bytes 983048 | tf_op jit(solution)/shard_map/ppermute | solution.py:751
  36.0 0.1 add_convert_fusion
  36.0 10.1 %own_deposit.1 = (f32[72,64,256]{2,1,0:T(8,128)}, f32[512,128]{1,0:T(8,128)}, f32[512,128]{1,0:T(8,128)}) custom-call(s32[128]{0:T(128)} %bitcast.9, s32[128,128]{1,0:T(8,128)} %get-tuple-element.26.skey, f32[128,128]{1,0:T(8,128)} %get-tuple-element.27.schg), custom_call_target="tpu_custom_call" | custom-call | tf_op jit(solution)/shard_map/own_deposit/pallas_call | solution.py:342
  46.1 1.9 %collective-permute-start.4 = (f32[512,128]{1,0:T(8,128)}, f32[512,128]{1,0:T(8,128)S(1)}, u32[]{:S(2)}, u32[]{:S(2)}) collective-permute-start(f32[512,128]{1,0:T(8,128)} %get-tuple-element.29), channel_id=1, source_target_pairs={{0,8},{8,16},{16,24},{24,32},{32,40},{40,48},{48,56},{56,64},{64,7... | collective-permute-start | bytes 786440 | tf_op jit(solution)/shard_map/ppermute | solution.py:751
  48.1 5.8 %collective-permute-start.5 = (f32[512,128]{1,0:T(8,128)}, f32[512,128]{1,0:T(8,128)S(1)}, u32[]{:S(2)}, u32[]{:S(2)}) collective-permute-start(f32[512,128]{1,0:T(8,128)} %get-tuple-element.30), channel_id=1, source_target_pairs={{8,0},{16,8},{24,16},{32,24},{40,32},{48,40},{56,48},{64,56},{72,6... | collective-permute-start | bytes 786440 | tf_op jit(solution)/shard_map/ppermute | solution.py:751
  53.8 0.6 pad_maximum_fusion.2.meta
  54.4 0.0 collective-permute-done.2.recv_lo
  54.4 0.0 copy-start
  54.4 0.7 fusion.7.last_lo
  55.1 0.0 collective-permute-done.3.recv_hi
  55.1 0.0 copy-start.1
  55.1 0.7 fusion.2.last_hi
  55.8 0.3 collective-permute-done.4.part_lo
  56.1 0.0 copy-start.2
  56.1 1.9 %collective-permute-done.5.part_hi = f32[512,128]{1,0:T(8,128)S(1)} collective-permute-done((f32[512,128]{1,0:T(8,128)}, f32[512,128]{1,0:T(8,128)S(1)}, u32[]{:S(2)}, u32[]{:S(2)}) %collective-permute-start.5) | collective-permute-done | bytes 262176 | tf_op jit(solution)/shard_map/ppermute | solution.py:751
  58.0 0.0 copy-start.3
  58.0 0.0 copy-done
  58.0 0.0 copy-done.1
  58.0 0.0 copy-done.2
  58.0 0.7 copy-done.3
  58.7 11.9 %edge_deposit.1 = (f32[72,64,256]{2,1,0:T(8,128)}, f32[6,64,512]{2,1,0:T(8,128)}, f32[80,128]{1,0:T(8,128)}, f32[80,128]{1,0:T(8,128)}) custom-call(s32[32]{0:T(128)} %fusion.7.last_lo, s32[32]{0:T(128)} %fusion.2.last_hi, f32[6]{0:T(128)} %pad_maximum_fusion.2.meta, f32[72,64,256]{2,1,0:T(8,128)} %get-tuple-element.28.pile_in, f32[640,128]{1,0:T(8,128)} %copy-done, ...), custom_call_target="tpu_custom_call" | custom-call | tf_op jit(solution)/shard_map/edge_deposit/pallas_call | solution.py:428
  70.6 8.4 %collective-permute-start.7 = (f32[80,128]{1,0:T(8,128)}, f32[80,128]{1,0:T(8,128)S(1)}, u32[]{:S(2)}, u32[]{:S(2)}) collective-permute-start(f32[80,128]{1,0:T(8,128)} %get-tuple-element.34.pay_lo), channel_id=1, source_target_pairs={{1,0},{2,1},{3,2},{4,3},{5,4},{6,5},{7,6},{9,8},{10,9},{11,10},{12... | collective-permute-start | bytes 122888 | tf_op jit(solution)/shard_map/ppermute | solution.py:751
  79.0 1.9 %collective-permute-start.6 = (f32[80,128]{1,0:T(8,128)}, f32[80,128]{1,0:T(8,128)S(1)}, u32[]{:S(2)}, u32[]{:S(2)}) collective-permute-start(f32[80,128]{1,0:T(8,128)} %get-tuple-element.35.pay_hi), channel_id=1, source_target_pairs={{0,1},{1,2},{2,3},{3,4},{4,5},{5,6},{6,7},{8,9},{9,10},{10,11},{11... | collective-permute-start | bytes 122888 | tf_op jit(solution)/shard_map/ppermute | solution.py:751
  80.9 7.1 %share_layout.1.v_hbm = f32[64,32,512]{2,1,0:T(8,128)} custom-call(f32[72,64,256]{2,1,0:T(8,128)} %get-tuple-element.32.pile), custom_call_target="tpu_custom_call" | custom-call | flops 8388608 | bytes 8388608 | tf_op jit(solution)/shard_map/share_layout/pallas_call | solution.py:475
  88.0 0.0 collective-permute-done.7.got_hi
  88.0 0.0 copy-start.4
  88.0 0.7 collective-permute-done.6.got_lo
  88.7 0.0 copy-start.5
  88.7 0.0 copy-done.4
  88.7 0.6 copy-done.5
  89.3 28.8 %two_heat_steps.1 = f32[64,32,512]{2,1,0:T(8,128)} custom-call(f32[6]{0:T(128)} %pad_maximum_fusion.2.meta, f32[64,32,512]{2,1,0:T(8,128)} %u_hbm.1, f32[64,32,512]{2,1,0:T(8,128)} %share_layout.1.v_hbm, f32[4,64,512]{2,1,0:T(8,128)} %get-tuple-element.20.urow, f32[640,128]{1,0:T(8,128)} %copy-done, f32[640,128]{1,0:T(8,128)} %copy-done.1, ...), custom_call_target="tpu_custom_call" | custom-call | tf_op jit(solution)/shard_map/two_heat_steps/pallas_call | solution.py:732
  (1 shorter events, 0.0 us)
Async XLA Ops:
  1.4 15.7 %collective-permute-start.1 = (f32[6,256]{1,0:T(8,128)S(1)}, f32[6,256]{1,0:T(8,128)S(1)}, u32[]{:S(2)}, u32[]{:S(2)}) collective-permute-start(f32[6,256]{1,0:T(8,128)S(1)} %get-tuple-element.36), channel_id=1, source_target_pairs={{1,0},{2,1},{3,2},{4,3},{5,4},{6,5},{7,6},{8,7},{9,8},{10,9},{11,1... | collective-permute-start | bytes 18440 | tf_op jit(solution)/shard_map/ppermute | solution.py:751
  6.7 10.4 %collective-permute-start = (f32[6,256]{1,0:T(8,128)S(1)}, f32[6,256]{1,0:T(8,128)S(1)}, u32[]{:S(2)}, u32[]{:S(2)}) collective-permute-start(f32[6,256]{1,0:T(8,128)S(1)} %get-tuple-element.37), channel_id=1, source_target_pairs={{0,1},{1,2},{2,3},{3,4},{4,5},{5,6},{6,7},{7,8},{8,9},{9,10},{10,1... | collective-permute-start | bytes 18440 | tf_op jit(solution)/shard_map/ppermute | solution.py:751
  12.8 17.7 %copy-start.8 = (s32[2]{0:T(128)S(1)}, s32[2]{0:T(128)}, u32[]{:S(2)}) copy-start(s32[2]{0:T(128)} %param.19) | copy-start | bytes 28
  17.1 0.6 copy-start.6
  17.1 0.6 copy-start.7
  28.2 26.2 %collective-permute-start.2 = (f32[640,128]{1,0:T(8,128)}, f32[640,128]{1,0:T(8,128)S(1)}, u32[]{:S(2)}, u32[]{:S(2)}) collective-permute-start(f32[640,128]{1,0:T(8,128)} %get-tuple-element.23), channel_id=1, source_target_pairs={{0,8},{8,16},{16,24},{24,32},{32,40},{40,48},{48,56},{56,64},{64,7... | collective-permute-start | bytes 983048 | tf_op jit(solution)/shard_map/ppermute | solution.py:751
  30.6 24.5 %collective-permute-start.3 = (f32[640,128]{1,0:T(8,128)}, f32[640,128]{1,0:T(8,128)S(1)}, u32[]{:S(2)}, u32[]{:S(2)}) collective-permute-start(f32[640,128]{1,0:T(8,128)} %get-tuple-element.24), channel_id=1, source_target_pairs={{8,0},{16,8},{24,16},{32,24},{40,32},{48,40},{56,48},{64,56},{72,6... | collective-permute-start | bytes 983048 | tf_op jit(solution)/shard_map/ppermute | solution.py:751
  46.1 10.0 %collective-permute-start.4 = (f32[512,128]{1,0:T(8,128)}, f32[512,128]{1,0:T(8,128)S(1)}, u32[]{:S(2)}, u32[]{:S(2)}) collective-permute-start(f32[512,128]{1,0:T(8,128)} %get-tuple-element.29), channel_id=1, source_target_pairs={{0,8},{8,16},{16,24},{24,32},{32,40},{40,48},{48,56},{56,64},{64,7... | collective-permute-start | bytes 786440 | tf_op jit(solution)/shard_map/ppermute | solution.py:751
  48.1 9.9 %collective-permute-start.5 = (f32[512,128]{1,0:T(8,128)}, f32[512,128]{1,0:T(8,128)S(1)}, u32[]{:S(2)}, u32[]{:S(2)}) collective-permute-start(f32[512,128]{1,0:T(8,128)} %get-tuple-element.30), channel_id=1, source_target_pairs={{8,0},{16,8},{24,16},{32,24},{40,32},{48,40},{56,48},{64,56},{72,6... | collective-permute-start | bytes 786440 | tf_op jit(solution)/shard_map/ppermute | solution.py:751
  54.4 3.6 %copy-start = (f32[640,128]{1,0:T(8,128)}, f32[640,128]{1,0:T(8,128)S(1)}, u32[]{:S(2)}) copy-start(f32[640,128]{1,0:T(8,128)S(1)} %collective-permute-done.2.recv_lo) | copy-start | bytes 983044
  55.1 2.9 %copy-start.1 = (f32[640,128]{1,0:T(8,128)}, f32[640,128]{1,0:T(8,128)S(1)}, u32[]{:S(2)}) copy-start(f32[640,128]{1,0:T(8,128)S(1)} %collective-permute-done.3.recv_hi) | copy-start | bytes 983044
  56.1 1.9 %copy-start.2 = (f32[512,128]{1,0:T(8,128)}, f32[512,128]{1,0:T(8,128)S(1)}, u32[]{:S(2)}) copy-start(f32[512,128]{1,0:T(8,128)S(1)} %collective-permute-done.4.part_lo) | copy-start | bytes 786436
  58.0 0.7 copy-start.3
  70.6 17.4 %collective-permute-start.7 = (f32[80,128]{1,0:T(8,128)}, f32[80,128]{1,0:T(8,128)S(1)}, u32[]{:S(2)}, u32[]{:S(2)}) collective-permute-start(f32[80,128]{1,0:T(8,128)} %get-tuple-element.34.pay_lo), channel_id=1, source_target_pairs={{1,0},{2,1},{3,2},{4,3},{5,4},{6,5},{7,6},{9,8},{10,9},{11,10},{12... | collective-permute-start | bytes 122888 | tf_op jit(solution)/shard_map/ppermute | solution.py:751
  79.0 9.7 %collective-permute-start.6 = (f32[80,128]{1,0:T(8,128)}, f32[80,128]{1,0:T(8,128)S(1)}, u32[]{:S(2)}, u32[]{:S(2)}) collective-permute-start(f32[80,128]{1,0:T(8,128)} %get-tuple-element.35.pay_hi), channel_id=1, source_target_pairs={{0,1},{1,2},{2,3},{3,4},{4,5},{5,6},{6,7},{8,9},{9,10},{10,11},{11... | collective-permute-start | bytes 122888 | tf_op jit(solution)/shard_map/ppermute | solution.py:751
  88.0 0.7 copy-start.4
  88.7 0.6 copy-start.5

commit v3 on v2

--- a/solution.py
+++ b/solution.py
@@ -25,10 +25,11 @@
 LOG2E = 1.4426950408889634
 VMEM_LIMIT = 56 * 1024 * 1024
 TILE_UNROLL = 32
-WALK_UNROLL = 16
+WALK_UNROLL = 32
+PLANES = 4
 XW = CX + 4
 BINS = 2 * XW
-SEND = 128 + 8 * DEPTH
+SEND = 128 + 8 * DEPTH + 8
 
 VSPEC = pl.BlockSpec(memory_space=pltpu.VMEM)
 SSPEC = pl.BlockSpec(memory_space=pltpu.SMEM)
@@ -39,16 +40,14 @@
     return lax.broadcasted_iota(I32, shape, dim)
 
 
-def partner(a, step, axis, low):
-    size = a.shape[axis]
-    return jnp.where(low, pltpu.roll(a, size - step, axis), pltpu.roll(a, step, axis))
-
-
-def cross_stage(ks, cs, step, axis, low):
+def cross_stage(ks, cs, step, axis):
+    at = iota((8, 128), axis)
+    other = at ^ step
+    low = (at & step) == 0
     nk, nc = [], []
     for k, c in zip(ks, cs):
-        pk = partner(k, step, axis, low)
-        pc = partner(c, step, axis, low)
+        pk = jnp.take_along_axis(k, other, axis=axis)
+        pc = jnp.take_along_axis(c, other, axis=axis)
         m = jnp.where(low, jnp.minimum(k, pk), jnp.maximum(k, pk))
         nk.append(m)
         nc.append(jnp.where(m != k, pc, c))
@@ -77,7 +76,7 @@
     def low_stages(ks, cs, top):
         for j in range(top, 3, -1):
             step = 1 << (j - 4)
-            ks, cs = cross_stage(ks, cs, step, 0, (sub & step) == 0)
+            ks, cs = cross_stage(ks, cs, step, 0)
         for j in range(min(top, 3), -1, -1):
             ks, cs = vreg_stage(ks, cs, j, up)
         return ks, cs
@@ -98,8 +97,7 @@
 
         def lane_step(t, inner):
             step = jnp.left_shift(jnp.int32(1), k - 8 - t)
-            low = (lane & step) == 0
-            nk, nc = cross_stage(list(inner[:16]), list(inner[16:]), step, 1, low)
+            nk, nc = cross_stage(list(inner[:16]), list(inner[16:]), step, 1)
             return tuple(nk) + tuple(nc)
 
         out = lax.fori_loop(0, k - 7, lane_step, tuple(ks) + tuple(cs))
@@ -120,9 +118,9 @@
 
 
 def particle_kernel(
-    tgt, src, cnt, loc, vel, halo_lo, halo_hi, key, wb, urow,
+    tgt, src, cnt, origin, loc, vel, halo_lo, halo_hi, site, bulk, octants, urow,
     nloc, nvel, skey, schg, last, send_lo, send_hi,
-    left, right, stat, acc, zrow,
+    left, right, stat, acc, zrow, key,
 ):
     wide = 4 * 128
 
@@ -211,11 +209,14 @@
             nvel[:, pl.ds(at, 128)] = nv
             nloc[:, pl.ds(at, 128)] = nx
             zrow[pl.ds(b, 1), :] = nx[2:3]
+            p = site[:, pl.ds(at, 128)]
+            cell = (p[1:2] - origin[0]) * CY + (p[2:3] - origin[1])
+            key[pl.ds(b, 1), :] = cell * DEPTH + p[0:1]
         return carry
 
     lax.fori_loop(0, NB // 8, advance, 0)
 
-    charge = wb[...] * (1.0 + 0.5 * jnp.tanh(zrow[...]))
+    charge = bulk[...] * octants[...].astype(F32) * 0.125 * (1.0 + 0.5 * jnp.tanh(zrow[...]))
     keys = key[...]
     ks = [keys[8 * r : 8 * r + 8] for r in range(16)]
     cs = [charge[8 * r : 8 * r + 8] for r in range(16)]
@@ -238,9 +239,11 @@
         for c in range(4):
             at = 128 + ((r % 2) * 4 + c) * DEPTH
             ref[at : at + DEPTH] = urow[r, :, 128 * c : 128 * c + 128]
-
-
-def particles(tgt, src, cnt, loc, vel, halo_lo, halo_hi, key, wb, urow):
+    for ref in (send_lo, send_hi):
+        ref[SEND - 8 : SEND] = jnp.broadcast_to(last[...].astype(F32), (8, 128))
+
+
+def particles(tgt, src, cnt, origin, loc, vel, halo_lo, halo_hi, site, bulk, octants, urow):
     sd = jax.ShapeDtypeStruct
     return pl.pallas_call(
         particle_kernel,
@@ -249,7 +252,7 @@
             sd((128, 128), I32), sd((128, 128), F32), sd((1, 128), I32),
             sd((SEND, 128), F32), sd((SEND, 128), F32),
         ),
-        in_specs=[SSPEC] * 3 + [VSPEC] * 7,
+        in_specs=[SSPEC] * 4 + [VSPEC] * 8,
         out_specs=(VSPEC,) * 7,
         scratch_shapes=[
             pltpu.VMEM((48, NEXT * 128), BF16),
@@ -257,10 +260,11 @@
             pltpu.VMEM((16, NEXT * 128), BF16),
             pltpu.VMEM(((NB + 1) * 8, 128), F32),
             pltpu.VMEM((NB, 128), F32),
+            pltpu.VMEM((NB, 128), I32),
         ],
         compiler_params=pltpu.CompilerParams(vmem_limit_bytes=VMEM_LIMIT),
         name="particle_step",
-    )(tgt, src, cnt, loc, vel, halo_lo, halo_hi, key, wb, urow)
+    )(tgt, src, cnt, origin, loc, vel, halo_lo, halo_hi, site, bulk, octants, urow)
 
 
 OWN, RECV = 128, 32
@@ -354,12 +358,16 @@
 
 
 def edge_deposit_kernel(
-    last_lo, last_hi, meta, pile_in, recv_lo, recv_hi, part_lo, part_hi, ucol,
-    pile_out, vrow, pay_lo, pay_hi,
-    pile, cells, prof, packs, sems,
+    meta, pile_in, recv_lo, recv_hi, part_lo, part_hi, ucol,
+    share, vrow, pay_lo, pay_hi,
+    pile, cells, prof, packs, last_v, last_s, sems,
 ):
     load = pltpu.make_async_copy(pile_in, pile, sems.at[0])
     load.start()
+    last_v[0:1] = recv_lo[SEND - 8 : SEND - 7].astype(I32)
+    last_v[1:2] = recv_hi[SEND - 8 : SEND - 7].astype(I32)
+    lasts = pltpu.make_async_copy(last_v, last_s, sems.at[1])
+    lasts.start()
     for ref, at, shift in ((recv_lo, 0, HB - G - CX), (recv_hi, RECV, HB + CX - G)):
         x = ref[0:32].astype(I32) + shift
         cells[at : at + RECV] = x * CY + ref[32:64].astype(I32)
@@ -375,10 +383,11 @@
         return carry
 
     lax.fori_loop(0, RECV // 4, profiles, 0)
+    lasts.wait()
     load.wait()
     half = 2 * (2 + G)
-    walk(pile, cells, prof, 0, RECV, dummy, lambda i: last_lo[i], 4, half - 1)
-    walk(pile, cells, prof, RECV, RECV, dummy, lambda i: last_hi[i], half, 2 * (2 + CX) - 1)
+    walk(pile, cells, prof, 0, RECV, dummy, lambda i: (last_s[0, OWN - RECV + i] >> 14) + 2 * (HB - G - CX), 4, half - 1)
+    walk(pile, cells, prof, RECV, RECV, dummy, lambda i: (last_s[1, i] >> 14) + 2 * (HB + CX - G), half, 2 * (2 + CX) - 1)
     for ref, x0, flag in ((part_lo, 0, meta[2]), (part_hi, CX + 2, meta[3])):
         for r in range(2):
             for c in range(4):
@@ -386,8 +395,17 @@
                 b = 2 * (x0 + r) + c // 2
                 cols = slice(128 * (c % 2), 128 * (c % 2) + 128)
                 pile[b, :, cols] = flag * (pile[b, :, cols] + ref[at : at + DEPTH])
-    save = pltpu.make_async_copy(pile, pile_out, sems.at[0])
-    save.start()
+
+    def turn(t):
+        x = t >> 1
+        cols = pl.ds(pl.multiple_of((t & 1) * BIN, BIN), BIN)
+        return pltpu.make_async_copy(pile.at[t + 2 * HB], share.at[:, x, cols], sems.at[2 + t])
+
+    def turn_start(t, carry):
+        turn(t).start()
+        return carry
+
+    lax.fori_loop(0, 2 * CX, turn_start, 0)
     for n, x in enumerate((0, 1, 2, CX + 1, CX + 2, CX + 3)):
         vrow[n, :, :BIN] = pile[2 * x]
         vrow[n, :, BIN:] = pile[2 * x + 1]
@@ -420,75 +438,51 @@
         t = jnp.transpose(jnp.concatenate([jnp.zeros((DEPTH, 128), F32), packs[far]], axis=0))
         pay[40 : 40 + CX] = t[0:CX] + ucol[far]
         pay[40 + CX : 80] = jnp.zeros((8, 128), F32)
-    save.wait()
-
-
-def edge_deposit(last_lo, last_hi, meta, pile, recv_lo, recv_hi, part_lo, part_hi, ucol):
+
+    def turn_wait(t, carry):
+        turn(t).wait()
+        return carry
+
+    lax.fori_loop(0, 2 * CX, turn_wait, 0)
+
+
+def edge_deposit(meta, pile, recv_lo, recv_hi, part_lo, part_hi, ucol):
     sd = jax.ShapeDtypeStruct
     return pl.pallas_call(
         edge_deposit_kernel,
         out_shape=(
-            sd((BINS, DEPTH, BIN), F32), sd((6, DEPTH, CY), F32),
+            sd((DEPTH, CX, CY), F32), sd((6, DEPTH, CY), F32),
             sd((80, 128), F32), sd((80, 128), F32),
         ),
-        in_specs=[SSPEC] * 3 + [ASPEC] + [VSPEC] * 5,
+        in_specs=[SSPEC, ASPEC] + [VSPEC] * 5,
         out_specs=(ASPEC, VSPEC, VSPEC, VSPEC),
         scratch_shapes=[
             pltpu.VMEM((BINS, DEPTH, BIN), F32),
             pltpu.VMEM((2 * RECV + 8, 128), I32),
             pltpu.VMEM((2 * RECV + 1, 128, 128), BF16),
             pltpu.VMEM((4, DEPTH, 128), F32),
-            pltpu.SemaphoreType.DMA((1,)),
+            pltpu.VMEM((2, 128), I32),
+            pltpu.SMEM((2, 128), I32),
+            pltpu.SemaphoreType.DMA((2 + 2 * CX,)),
         ],
         compiler_params=pltpu.CompilerParams(vmem_limit_bytes=VMEM_LIMIT),
         name="edge_deposit",
-    )(last_lo, last_hi, meta, pile, recv_lo, recv_hi, part_lo, part_hi, ucol)
-
-
-def share_kernel(pile, share):
-    sub = iota((8, CY), 0)
-
-    def turn(xg, carry):
-        x0 = pl.multiple_of(xg * 8, 8)
-        a = [
-            jnp.concatenate([pile[2 * (x0 + i + 2)], pile[2 * (x0 + i + 2) + 1]], axis=1)
-            for i in range(8)
-        ]
-        for d in (1, 2, 4):
-            b = list(a)
-            low = (sub & d) == 0
-            for i in range(8):
-                if i & d:
-                    continue
-                p, q = a[i], a[i | d]
-                b[i] = jnp.where(low, p, pltpu.roll(q, d, 0))
-                b[i | d] = jnp.where(low, pltpu.roll(p, 8 - d, 0), q)
-            a = b
-        for k in range(8):
-            share[k, pl.ds(x0, 8), :] = a[k]
-        return carry
-
-    lax.fori_loop(0, CX // 8, turn, 0)
-
-
-def share_layout(pile):
-    return pl.pallas_call(
-        share_kernel,
-        grid=(DEPTH // 8,),
-        out_shape=jax.ShapeDtypeStruct((DEPTH, CX, CY), F32),
-        in_specs=[pl.BlockSpec((BINS, 8, BIN), lambda i: (0, i, 0))],
-        out_specs=pl.BlockSpec((8, CX, CY), lambda i: (i, 0, 0)),
-        compiler_params=pltpu.CompilerParams(vmem_limit_bytes=VMEM_LIMIT),
-        cost_estimate=pl.CostEstimate(flops=1 << 23, bytes_accessed=1 << 23, transcendentals=0),
-        name="share_layout",
-    )(pile)
-
-
-def edges_kernel(left, right, top, bottom, urow, ucol):
-    urow[0] = top[:, 0, :]
-    urow[1] = top[:, 1, :]
-    urow[2] = bottom[:, 6, :]
-    urow[3] = bottom[:, 7, :]
+    )(meta, pile, recv_lo, recv_hi, part_lo, part_hi, ucol)
+
+
+def edges_kernel(cells, urow, ucol, left, right, sems):
+    rows = [
+        pltpu.make_async_copy(cells.at[:, x, :], urow.at[r], sems.at[2 + r])
+        for r, x in enumerate((0, 1, CX - 2, CX - 1))
+    ]
+    cols = [
+        pltpu.make_async_copy(cells.at[:, :, pl.ds(at, 128)], ref, sems.at[n])
+        for n, (ref, at) in enumerate(((left, 0), (right, CY - 128)))
+    ]
+    for copy in cols + rows:
+        copy.start()
+    for copy in cols:
+        copy.wait()
     lane = iota((CX, 128), 1)
     acc = [jnp.zeros((CX, 128), F32)] * 4
     for z in range(DEPTH):
@@ -498,27 +492,25 @@
             acc[n] = jnp.where(lane == z, a, acc[n])
     for n in range(4):
         ucol[n] = acc[n]
+    for copy in rows:
+        copy.wait()
 
 
 def edges(cells):
     sd = jax.ShapeDtypeStruct
     return pl.pallas_call(
         edges_kernel,
-        grid=(1,),
         out_shape=(sd((4, DEPTH, CY), F32), sd((4, CX, 128), F32)),
-        in_specs=[
-            pl.BlockSpec((DEPTH, CX, 128), lambda i: (0, 0, 0)),
-            pl.BlockSpec((DEPTH, CX, 128), lambda i: (0, 0, CY // 128 - 1)),
-            pl.BlockSpec((DEPTH, 8, CY), lambda i: (0, 0, 0)),
-            pl.BlockSpec((DEPTH, 8, CY), lambda i: (0, CX // 8 - 1, 0)),
+        in_specs=[ASPEC],
+        out_specs=(VSPEC, VSPEC),
+        scratch_shapes=[
+            pltpu.VMEM((DEPTH, CX, 128), F32),
+            pltpu.VMEM((DEPTH, CX, 128), F32),
+            pltpu.SemaphoreType.DMA((6,)),
         ],
-        out_specs=(
-            pl.BlockSpec((4, DEPTH, CY), lambda i: (0, 0, 0)),
-            pl.BlockSpec((4, CX, 128), lambda i: (0, 0, 0)),
-        ),
         compiler_params=pltpu.CompilerParams(vmem_limit_bytes=VMEM_LIMIT),
         name="temperature_edges",
-    )(cells, cells, cells, cells)
+    )(cells)
 
 
 def half_kappa(u, v):
@@ -632,44 +624,53 @@
     def load(ref, z):
         return [ref[z, :, 128 * c : 128 * c + 128] for c in tiles]
 
-    def plane(src, dst, row_f, col_f, glow, z, is_last):
-        u = load(src, z)
-        k = load(kz, z & 1)
-        v = load(vs, z)
-        if is_last:
-            up = [(k[c] + 0.05) * (0.0 - u[c]) for c in tiles]
-        else:
-            un = load(src, z + 1)
-            vn = load(vs, z + 1)
-            kn = [half_kappa(un[c], vn[c]) for c in tiles]
+    def planes(src, dst, row_f, col_f, glow, z0, is_last):
+        k = load2(kz)
+        down = load2(fz)
+        cols = col_f[...]
+        for p in range(PLANES):
+            z = z0 + p
+            u = load(src, z)
+            v = load(vs, z)
+            if is_last and p == PLANES - 1:
+                kn = k
+                up = [(k[c] + 0.05) * (0.0 - u[c]) for c in tiles]
+            else:
+                un = load(src, z + 1)
+                vn = load(vs, z + 1)
+                kn = [half_kappa(un[c], vn[c]) for c in tiles]
+                up = [flux(k[c], kn[c], u[c], un[c]) for c in tiles]
+            row_first = row_f[pl.ds(z, 1), :]
+            row_end = row_f[pl.ds(z + DEPTH, 1), :]
+            edge0 = pltpu.roll(cols, (128 - z) & 127, 1)
+            edge1 = pltpu.roll(cols, 63 - z, 1)
+            ru = [pltpu.roll(u[c], 1, 1) for c in tiles]
+            rk = [pltpu.roll(k[c], 1, 1) for c in tiles]
+            g = []
             for c in tiles:
-                kz[(z + 1) & 1, :, 128 * c : 128 * c + 128] = kn[c]
-            up = [flux(k[c], kn[c], u[c], un[c]) for c in tiles]
-        cols = col_f[...]
-        row_first = row_f[pl.ds(z, 1), :]
-        row_end = row_f[pl.ds(z + DEPTH, 1), :]
-        edge0 = pltpu.roll(cols, (128 - z) & 127, 1)
-        edge1 = pltpu.roll(cols, 63 - z, 1)
-        ru = [pltpu.roll(u[c], 1, 1) for c in tiles]
-        rk = [pltpu.roll(k[c], 1, 1) for c in tiles]
-        g = []
-        for c in tiles:
-            if c == 0:
-                g.append(jnp.where(lane == 0, edge0, flux(k[0], rk[0], ru[0], u[0])))
-            else:
-                pu = jnp.where(lane == 0, ru[c - 1], ru[c])
-                pk = jnp.where(lane == 0, rk[c - 1], rk[c])
-                g.append(flux(k[c], pk, pu, u[c]))
-        rg = [pltpu.roll(g[c], 127, 1) for c in tiles]
+                if c == 0:
+                    g.append(jnp.where(lane == 0, edge0, flux(k[0], rk[0], ru[0], u[0])))
+                else:
+                    pu = jnp.where(lane == 0, ru[c - 1], ru[c])
+                    pk = jnp.where(lane == 0, rk[c - 1], rk[c])
+                    g.append(flux(k[c], pk, pu, u[c]))
+            rg = [pltpu.roll(g[c], 127, 1) for c in tiles]
+            for c in tiles:
+                at = slice(128 * c, 128 * c + 128)
+                gn = jnp.where(lane == 127, rg[c + 1] if c < 3 else edge1, rg[c])
+                f = flux(k[c], pltpu.roll(k[c], 1, 0), pltpu.roll(u[c], 1, 0), u[c])
+                f = jnp.where(sub == 0, row_first[:, at], f)
+                fn = jnp.where(sub == CX - 1, row_end[:, at], pltpu.roll(f, CX - 1, 0))
+                total = (up[c] - down[c]) + (fn - f) + (gn - g[c])
+                dst[z, :, at] = u[c] + total + glow * v[c]
+            k, down = kn, up
         for c in tiles:
             at = slice(128 * c, 128 * c + 128)
-            gn = jnp.where(lane == 127, rg[c + 1] if c < 3 else edge1, rg[c])
-            f = flux(k[c], pltpu.roll(k[c], 1, 0), pltpu.roll(u[c], 1, 0), u[c])
-            f = jnp.where(sub == 0, row_first[:, at], f)
-            fn = jnp.where(sub == CX - 1, row_end[:, at], pltpu.roll(f, CX - 1, 0))
-            total = (up[c] - fz[:, at]) + (fn - f) + (gn - g[c])
-            fz[:, at] = up[c]
-            dst[z, :, at] = u[c] + total + glow * v[c]
+            kz[:, at] = k[c]
+            fz[:, at] = down[c]
+
+    def load2(ref):
+        return [ref[:, 128 * c : 128 * c + 128] for c in tiles]
 
     def begin(src):
         u = load(src, 0)
@@ -677,24 +678,26 @@
         for c in tiles:
             at = slice(128 * c, 128 * c + 128)
             k = half_kappa(u[c], v[c])
-            kz[0, :, at] = k
+            kz[:, at] = k
             fz[:, at] = (k + 0.05) * u[c]
 
+    groups = DEPTH // PLANES
+    per = 8 // PLANES
     for copy in fetch(0):
         copy.wait()
     begin(us)
 
-    def one(z, carry):
-        @pl.when((z & 7) == 7)
+    def one(g, carry):
+        @pl.when(lax.rem(g, per) == per - 1)
         def _():
-            for copy in fetch((z >> 3) + 1):
+            for copy in fetch((g + 1) // per):
                 copy.wait()
 
-        plane(us, ms, row1, col1, glow1, z, False)
-        return carry
-
-    lax.fori_loop(0, DEPTH - 1, one, 0)
-    plane(us, ms, row1, col1, glow1, DEPTH - 1, True)
+        planes(us, ms, row1, col1, glow1, g * PLANES, False)
+        return carry
+
+    lax.fori_loop(0, groups - 1, one, 0)
+    planes(us, ms, row1, col1, glow1, DEPTH - PLANES, True)
 
     for n in range(2):
         mh = mrow[DEPTH * n : DEPTH * n + DEPTH]
@@ -709,17 +712,17 @@
 
     begin(ms)
 
-    def two(z, carry):
-        plane(ms, us, row2, col2, glow2, z, False)
-
-        @pl.when((z & 7) == 7)
+    def two(g, carry):
+        planes(ms, us, row2, col2, glow2, g * PLANES, False)
+
+        @pl.when(lax.rem(g, per) == per - 1)
         def _():
-            store(z >> 3).start()
-
-        return carry
-
-    lax.fori_loop(0, DEPTH - 1, two, 0)
-    plane(ms, us, row2, col2, glow2, DEPTH - 1, True)
+            store(g // per).start()
+
+        return carry
+
+    lax.fori_loop(0, groups - 1, two, 0)
+    planes(ms, us, row2, col2, glow2, DEPTH - PLANES, True)
     store(chunks - 1).start()
     for c in range(chunks):
         store(c).wait()
@@ -736,7 +739,7 @@
         out_specs=ASPEC,
         scratch_shapes=[
             plane, plane, plane,
-            pltpu.VMEM((2, CX, CY), F32), pltpu.VMEM((CX, CY), F32),
+            pltpu.VMEM((CX, CY), F32), pltpu.VMEM((CX, CY), F32),
             rows, rows, rows, column, column,
             pltpu.SemaphoreType.DMA((2, DEPTH // 8)),
         ],
@@ -774,14 +777,12 @@
     beam = row_start - molten_strip_midlines
     inside = jnp.stack([gx > 0, gx < lax.axis_size("gx") - 1, gy > 0, gy < lax.axis_size("gy") - 1])
     meta = jnp.concatenate([beam.astype(F32), inside.astype(F32)])
-    px = landing_site_triple[1] - row_start + G
-    py = landing_site_triple[2] - col_start
-    key = ((px * CY + py) * DEPTH + landing_site_triple[0]).reshape(128, 128)
-    wb = (particle_bulk * landing_weight_octants.astype(F32) * 0.125).reshape(128, 128)
+    origin = jnp.stack([row_start - G, col_start])
 
     nloc, nvel, skey, schg, last, send_lo, send_hi = particles(
-        receiving_group_per_pair, emitting_group_per_pair, active_pair_slots,
-        particle_locations, particle_speeds, halo_lo, halo_hi, key, wb, urow,
+        receiving_group_per_pair, emitting_group_per_pair, active_pair_slots, origin,
+        particle_locations, particle_speeds, halo_lo, halo_hi, landing_site_triple,
+        particle_bulk.reshape(128, 128), landing_weight_octants.reshape(128, 128), urow,
     )
     recv_lo = shift(send_hi, "gx", 1)
     recv_hi = shift(send_lo, "gx", -1)
@@ -789,17 +790,11 @@
     part_lo = shift(row_hi, "gx", 1)
     part_hi = shift(row_lo, "gx", -1)
 
-    def last_bins(got, by):
-        cell = (got[0:32, 127].astype(I32) + by) * CY + got[32:64, 127].astype(I32)
-        return cell >> 8
-
-    pile, vrow, pay_lo, pay_hi = edge_deposit(
-        last_bins(recv_lo, HB - G - CX), last_bins(recv_hi, HB + CX - G), meta,
-        pile, recv_lo, recv_hi, part_lo, part_hi, ucol,
+    share, vrow, pay_lo, pay_hi = edge_deposit(
+        meta, pile, recv_lo, recv_hi, part_lo, part_hi, ucol,
     )
     got_lo = shift(pay_hi, "gy", 1)
     got_hi = shift(pay_lo, "gy", -1)
-    share = share_layout(pile)
     final = heat(meta, thermal_excess, share, urow, recv_lo, recv_hi, vrow, pay_lo, pay_hi, got_lo, got_hi)
     return nloc, nvel, share, final
 

time: 120 us -> 104 us (0.87); the launches traced: 118 us -> 104 us
  Pallas kernels: 72.7 us -> 56.9 us
  waiting for transfers between devices: 2.87 us -> 13.3 us
  starting transfers between devices: 32.9 us -> 28.4 us
  other arithmetic: 6.34 us -> 2.04 us
    ppermute x8, waiting for transfers between devices: 2.87 us -> 13.3 us  [shift(): lax.ppermute(value, axis, [(i, i + steps) for i in range(first, stop)])]
    pallas_call x1, Pallas kernels: 28.8 us -> 18.6 us  [heat(): pl.pallas_call(heat_kernel, out_shape=jax.ShapeDtypeStruct((DEPTH, CX, CY...]
    pallas_call x3 -> x2, Pallas kernels: 23.2 us -> 16.9 us  [the longest x1 13.3 us: edge_deposit(): pl.pallas_call(edge_deposit_kernel, out_shape=(sd((DEPTH, CX, CY), F32),...]
    ppermute x8, starting transfers between devices: 32.9 us -> 28.4 us  [shift(): lax.ppermute(value, axis, [(i, i + steps) for i in range(first, stop)])]
    add x1 -> x0, other arithmetic: 2.01 us -> none  [body(): key = ((px * CY + py) * DEPTH + landing_site_triple[0]).reshape(128, 128)]
    reshape x1 -> x0, other arithmetic: 1.5 us -> none  [body(): (particle_bulk * landing_weight_octants.astype(F32) * 0.125).reshape(128,...]
    shift_right_arithmetic x2 -> x0, other arithmetic: 1.41 us -> none  [last_bins(): return cell >> 8]
  transfers between devices with their start and end apart: 8 -> 8, of which waited for: 3 -> 5; matrix products, arithmetic and copies ran while one was open for 5% -> 1% of each run, Pallas kernels for 18% -> 13%
where the time goes in v3:
time: 104 us
  Pallas kernels  56.9 us (55%)
  starting transfers between devices  28.4 us (27%)
  waiting for transfers between devices  13.3 us (13%)
  local copies, waits for them, and re-layouts  2.12 us (2%)
  other arithmetic  2.04 us (2%)
  between operations  1.45 us (1%)
    ppermute x8, starting transfers between devices, shift(): lax.ppermute(value, axis, [(i, i + steps) for i in range(first, stop)])  28.4 us
    pallas_call x1, Pallas kernels, heat(): pl.pallas_call(heat_kernel, out_shape=jax.ShapeDtypeStruct((DEPTH, CX, CY...  18.6 us
    pallas_call x1, Pallas kernels, edge_deposit(): pl.pallas_call(edge_deposit_kernel, out_shape=(sd((DEPTH, CX, CY), F32),...  13.3 us
    ppermute x8, waiting for transfers between devices, shift(): lax.ppermute(value, axis, [(i, i + steps) for i in range(first, stop)])  13.3 us
    pallas_call x1, Pallas kernels, particles(): pl.pallas_call(particle_kernel, out_shape=(sd((3, NPART), F32), sd((3, NP...  11.5 us
    pallas_call x1, Pallas kernels, own_deposit(): pl.pallas_call(own_deposit_kernel, out_shape=(sd((BINS, DEPTH, BIN), F32)...  9.95 us
    pallas_call x1, Pallas kernels, edges(): pl.pallas_call(edges_kernel, out_shape=(sd((4, DEPTH, CY), F32), sd((4, C...  3.6 us
    unnamed x18, local copies, waits for them, and re-layouts  2.12 us
  transfers between devices with their start and end apart: 8, of which 5 were waited for; matrix products, arithmetic and copies ran while one was open for 1% of the time, Pallas kernels for 13%

profile of v3, /device:TPU:24, one launch (start us, length us, event | category | flops | bytes accessed | tf_op | source)
XLA Modules:
  0.0 104.2 jit_solution(2590265719706200601)
XLA Ops:
  0.6 0.0 copy-start.8
  0.6 0.8 pad_maximum_fusion
  1.4 5.3 %collective-permute-start.1 = (f32[6,256]{1,0:T(8,128)S(1)}, f32[6,256]{1,0:T(8,128)S(1)}, u32[]{:S(2)}, u32[]{:S(2)}) collective-permute-start(f32[6,256]{1,0:T(8,128)S(1)} %get-tuple-element.36), channel_id=1, source_target_pairs={{1,0},{2,1},{3,2},{4,3},{5,4},{6,5},{7,6},{8,7},{9,8},{10,9},{11,1... | collective-permute-start | bytes 18440 | tf_op jit(solution)/shard_map/ppermute | solution.py:754
  6.7 1.9 %collective-permute-start = (f32[6,256]{1,0:T(8,128)S(1)}, f32[6,256]{1,0:T(8,128)S(1)}, u32[]{:S(2)}, u32[]{:S(2)}) collective-permute-start(f32[6,256]{1,0:T(8,128)S(1)} %get-tuple-element.37), channel_id=1, source_target_pairs={{0,1},{1,2},{2,3},{3,4},{4,5},{5,6},{6,7},{7,8},{8,9},{9,10},{10,1... | collective-permute-start | bytes 18440 | tf_op jit(solution)/shard_map/ppermute | solution.py:754
  8.7 0.6 pad_add_fusion.origin
  9.9 3.6 %temperature_edges.1 = (f32[4,64,512]{2,1,0:T(8,128)}, f32[4,32,128]{2,1,0:T(8,128)}) custom-call(f32[64,32,512]{2,1,0:T(8,128)} %u_hbm.1), custom_call_target="tpu_custom_call" | custom-call | tf_op jit(solution)/shard_map/temperature_edges/pallas_call | solution.py:501
  13.5 0.0 collective-permute-done.1.halo_hi
  13.5 0.0 copy-start.6
  13.5 2.4 %collective-permute-done.halo_lo = f32[6,256]{1,0:T(8,128)S(1)} collective-permute-done((f32[6,256]{1,0:T(8,128)S(1)}, f32[6,256]{1,0:T(8,128)S(1)}, u32[]{:S(2)}, u32[]{:S(2)}) %collective-permute-start) | collective-permute-done | bytes 6176 | tf_op jit(solution)/shard_map/ppermute | solution.py:754
  15.9 0.0 copy-start.7
  15.9 0.0 copy-done.6
  15.9 0.6 copy-done.7
  16.5 11.5 %particle_step.1 = (f32[3,16384]{1,0:T(4,128)}, f32[3,16384]{1,0:T(4,128)}, s32[128,128]{1,0:T(8,128)}, f32[128,128]{1,0:T(8,128)}, s32[1,128]{1,0:T(1,128)}, /*index=5*/f32[648,128]{1,0:T(8,128)}, f32[648,128]{1,0:T(8,128)}) custom-call(s32[256]{0:T(256)} %tgt.1, s32[256]{0:T(256)} %src.1, s32[1]{0:T(128)S(6)} %copy.14.cnt, s32[2]{0:T(128)} %pad_add_fusion.origin, ...), custom_call_target="tpu_custom_call" | custom-call | tf_op jit(solution)/shard_map/particle_step/pallas_call | solution.py:248
  28.0 1.9 %collective-permute-start.2 = (f32[648,128]{1,0:T(8,128)}, f32[648,128]{1,0:T(8,128)S(1)}, u32[]{:S(2)}, u32[]{:S(2)}) collective-permute-start(f32[648,128]{1,0:T(8,128)} %get-tuple-element.27), channel_id=1, source_target_pairs={{0,8},{8,16},{16,24},{24,32},{32,40},{40,48},{48,56},{56,64},{64,7... | collective-permute-start | bytes 995336 | tf_op jit(solution)/shard_map/ppermute | solution.py:754
  29.9 5.8 %collective-permute-start.3 = (f32[648,128]{1,0:T(8,128)}, f32[648,128]{1,0:T(8,128)S(1)}, u32[]{:S(2)}, u32[]{:S(2)}) collective-permute-start(f32[648,128]{1,0:T(8,128)} %get-tuple-element.28), channel_id=1, source_target_pairs={{8,0},{16,8},{24,16},{32,24},{40,32},{48,40},{56,48},{64,56},{72,6... | collective-permute-start | bytes 995336 | tf_op jit(solution)/shard_map/ppermute | solution.py:754
  35.6 9.9 %own_deposit.1 = (f32[72,64,256]{2,1,0:T(8,128)}, f32[512,128]{1,0:T(8,128)}, f32[512,128]{1,0:T(8,128)}) custom-call(s32[128]{0:T(128)} %bitcast.11, s32[128,128]{1,0:T(8,128)} %get-tuple-element.24.skey, f32[128,128]{1,0:T(8,128)} %get-tuple-element.25.schg), custom_call_target="tpu_custom_call" | custom-call | tf_op jit(solution)/shard_map/own_deposit/pallas_call | solution.py:346
  45.6 1.9 %collective-permute-start.4 = (f32[512,128]{1,0:T(8,128)}, f32[512,128]{1,0:T(8,128)S(1)}, u32[]{:S(2)}, u32[]{:S(2)}) collective-permute-start(f32[512,128]{1,0:T(8,128)} %get-tuple-element.29), channel_id=1, source_target_pairs={{0,8},{8,16},{16,24},{24,32},{32,40},{40,48},{48,56},{56,64},{64,7... | collective-permute-start | bytes 786440 | tf_op jit(solution)/shard_map/ppermute | solution.py:754
  47.5 5.8 %collective-permute-start.5 = (f32[512,128]{1,0:T(8,128)}, f32[512,128]{1,0:T(8,128)S(1)}, u32[]{:S(2)}, u32[]{:S(2)}) collective-permute-start(f32[512,128]{1,0:T(8,128)} %get-tuple-element.30), channel_id=1, source_target_pairs={{8,0},{16,8},{24,16},{32,24},{40,32},{48,40},{56,48},{64,56},{72,6... | collective-permute-start | bytes 786440 | tf_op jit(solution)/shard_map/ppermute | solution.py:754
  53.3 0.0 copy-done.8
  53.3 0.1 add_convert_fusion
  53.4 0.6 pad_maximum_fusion.2.meta
  54.0 1.6 %collective-permute-done.4.part_lo = f32[512,128]{1,0:T(8,128)S(1)} collective-permute-done((f32[512,128]{1,0:T(8,128)}, f32[512,128]{1,0:T(8,128)S(1)}, u32[]{:S(2)}, u32[]{:S(2)}) %collective-permute-start.4) | collective-permute-done | bytes 262176 | tf_op jit(solution)/shard_map/ppermute | solution.py:754
  55.6 0.0 copy-start.2
  55.6 1.9 %collective-permute-done.5.part_hi = f32[512,128]{1,0:T(8,128)S(1)} collective-permute-done((f32[512,128]{1,0:T(8,128)}, f32[512,128]{1,0:T(8,128)S(1)}, u32[]{:S(2)}, u32[]{:S(2)}) %collective-permute-start.5) | collective-permute-done | bytes 262176 | tf_op jit(solution)/shard_map/ppermute | solution.py:754
  57.4 0.0 copy-start.3
  57.5 0.0 collective-permute-done.2.recv_lo
  57.5 0.0 copy-start
  57.5 0.0 collective-permute-done.3.recv_hi
  57.5 0.0 copy-start.1
  57.5 0.0 copy-done.2
  57.5 0.7 copy-done.3
  58.2 0.1 copy-done
  58.3 0.1 copy-done.1
  58.4 13.3 %edge_deposit.1 = (f32[64,32,512]{2,1,0:T(8,128)}, f32[6,64,512]{2,1,0:T(8,128)}, f32[80,128]{1,0:T(8,128)}, f32[80,128]{1,0:T(8,128)}) custom-call(f32[6]{0:T(128)} %pad_maximum_fusion.2.meta, f32[72,64,256]{2,1,0:T(8,128)} %get-tuple-element.26.pile_in, f32[648,128]{1,0:T(8,128)} %copy-done, f32[648,128]{1,0:T(8,128)} %copy-done.1, f32[512,128]{1,0:T(8,128)} %copy-done.2, ...), custom_call_target="tpu_custom_call" | custom-call | tf_op jit(solution)/shard_map/edge_deposit/pallas_call | solution.py:451
  71.7 3.6 %collective-permute-start.7 = (f32[80,128]{1,0:T(8,128)}, f32[80,128]{1,0:T(8,128)S(1)}, u32[]{:S(2)}, u32[]{:S(2)}) collective-permute-start(f32[80,128]{1,0:T(8,128)} %get-tuple-element.34.pay_lo), channel_id=1, source_target_pairs={{1,0},{2,1},{3,2},{4,3},{5,4},{6,5},{7,6},{9,8},{10,9},{11,10},{12... | collective-permute-start | bytes 122888 | tf_op jit(solution)/shard_map/ppermute | solution.py:754
  75.3 2.2 %collective-permute-start.6 = (f32[80,128]{1,0:T(8,128)}, f32[80,128]{1,0:T(8,128)S(1)}, u32[]{:S(2)}, u32[]{:S(2)}) collective-permute-start(f32[80,128]{1,0:T(8,128)} %get-tuple-element.35.pay_hi), channel_id=1, source_target_pairs={{0,1},{1,2},{2,3},{3,4},{4,5},{5,6},{6,7},{8,9},{9,10},{10,11},{11... | collective-permute-start | bytes 122888 | tf_op jit(solution)/shard_map/ppermute | solution.py:754
  77.6 0.2 collective-permute-done.7.got_hi
  77.8 0.0 copy-start.4
  77.8 7.2 %collective-permute-done.6.got_lo = f32[80,128]{1,0:T(8,128)S(1)} collective-permute-done((f32[80,128]{1,0:T(8,128)}, f32[80,128]{1,0:T(8,128)S(1)}, u32[]{:S(2)}, u32[]{:S(2)}) %collective-permute-start.6) | collective-permute-done | bytes 40992 | tf_op jit(solution)/shard_map/ppermute | solution.py:754
  85.0 0.0 copy-start.5
  85.0 0.0 copy-done.4
  85.0 0.6 copy-done.5
  85.6 18.6 %two_heat_steps.1 = f32[64,32,512]{2,1,0:T(8,128)} custom-call(f32[6]{0:T(128)} %pad_maximum_fusion.2.meta, f32[64,32,512]{2,1,0:T(8,128)} %u_hbm.1, f32[64,32,512]{2,1,0:T(8,128)} %get-tuple-element.18.v_hbm, f32[4,64,512]{2,1,0:T(8,128)} %get-tuple-element.20.urow, f32[648,128]{1,0:T(8,128)} %copy-done, f32[648,128]{1,0:T(8,128)} %copy-done.1, ...), custom_call_target="tpu_custom_call" | custom-call | tf_op jit(solution)/shard_map/two_heat_steps/pallas_call | solution.py:735
  (1 shorter events, 0.0 us)
Async XLA Ops:
  0.6 52.6 %copy-start.8 = (s32[2]{0:T(128)S(1)}, s32[2]{0:T(128)}, u32[]{:S(2)}) copy-start(s32[2]{0:T(128)} %param.19) | copy-start | bytes 28
  1.4 12.1 %collective-permute-start.1 = (f32[6,256]{1,0:T(8,128)S(1)}, f32[6,256]{1,0:T(8,128)S(1)}, u32[]{:S(2)}, u32[]{:S(2)}) collective-permute-start(f32[6,256]{1,0:T(8,128)S(1)} %get-tuple-element.36), channel_id=1, source_target_pairs={{1,0},{2,1},{3,2},{4,3},{5,4},{6,5},{7,6},{8,7},{9,8},{10,9},{11,1... | collective-permute-start | bytes 18440 | tf_op jit(solution)/shard_map/ppermute | solution.py:754
  6.7 9.2 %collective-permute-start = (f32[6,256]{1,0:T(8,128)S(1)}, f32[6,256]{1,0:T(8,128)S(1)}, u32[]{:S(2)}, u32[]{:S(2)}) collective-permute-start(f32[6,256]{1,0:T(8,128)S(1)} %get-tuple-element.37), channel_id=1, source_target_pairs={{0,1},{1,2},{2,3},{3,4},{4,5},{5,6},{6,7},{7,8},{8,9},{9,10},{10,1... | collective-permute-start | bytes 18440 | tf_op jit(solution)/shard_map/ppermute | solution.py:754
  13.5 2.4 %copy-start.6 = (f32[6,256]{1,0:T(8,128)}, f32[6,256]{1,0:T(8,128)S(1)}, u32[]{:S(2)}) copy-start(f32[6,256]{1,0:T(8,128)S(1)} %collective-permute-done.1.halo_hi) | copy-start | bytes 18436
  15.9 0.6 copy-start.7
  28.0 29.5 %collective-permute-start.2 = (f32[648,128]{1,0:T(8,128)}, f32[648,128]{1,0:T(8,128)S(1)}, u32[]{:S(2)}, u32[]{:S(2)}) collective-permute-start(f32[648,128]{1,0:T(8,128)} %get-tuple-element.27), channel_id=1, source_target_pairs={{0,8},{8,16},{16,24},{24,32},{32,40},{40,48},{48,56},{56,64},{64,7... | collective-permute-start | bytes 995336 | tf_op jit(solution)/shard_map/ppermute | solution.py:754
  29.9 27.6 %collective-permute-start.3 = (f32[648,128]{1,0:T(8,128)}, f32[648,128]{1,0:T(8,128)S(1)}, u32[]{:S(2)}, u32[]{:S(2)}) collective-permute-start(f32[648,128]{1,0:T(8,128)} %get-tuple-element.28), channel_id=1, source_target_pairs={{8,0},{16,8},{24,16},{32,24},{40,32},{48,40},{56,48},{64,56},{72,6... | collective-permute-start | bytes 995336 | tf_op jit(solution)/shard_map/ppermute | solution.py:754
  45.6 10.0 %collective-permute-start.4 = (f32[512,128]{1,0:T(8,128)}, f32[512,128]{1,0:T(8,128)S(1)}, u32[]{:S(2)}, u32[]{:S(2)}) collective-permute-start(f32[512,128]{1,0:T(8,128)} %get-tuple-element.29), channel_id=1, source_target_pairs={{0,8},{8,16},{16,24},{24,32},{32,40},{40,48},{48,56},{56,64},{64,7... | collective-permute-start | bytes 786440 | tf_op jit(solution)/shard_map/ppermute | solution.py:754
  47.5 9.9 %collective-permute-start.5 = (f32[512,128]{1,0:T(8,128)}, f32[512,128]{1,0:T(8,128)S(1)}, u32[]{:S(2)}, u32[]{:S(2)}) collective-permute-start(f32[512,128]{1,0:T(8,128)} %get-tuple-element.30), channel_id=1, source_target_pairs={{8,0},{16,8},{24,16},{32,24},{40,32},{48,40},{56,48},{64,56},{72,6... | collective-permute-start | bytes 786440 | tf_op jit(solution)/shard_map/ppermute | solution.py:754
  55.6 1.9 %copy-start.2 = (f32[512,128]{1,0:T(8,128)}, f32[512,128]{1,0:T(8,128)S(1)}, u32[]{:S(2)}) copy-start(f32[512,128]{1,0:T(8,128)S(1)} %collective-permute-done.4.part_lo) | copy-start | bytes 786436
  57.4 0.7 copy-start.3
  57.5 0.8 copy-start
  57.5 0.9 copy-start.1
  71.7 6.1 %collective-permute-start.7 = (f32[80,128]{1,0:T(8,128)}, f32[80,128]{1,0:T(8,128)S(1)}, u32[]{:S(2)}, u32[]{:S(2)}) collective-permute-start(f32[80,128]{1,0:T(8,128)} %get-tuple-element.34.pay_lo), channel_id=1, source_target_pairs={{1,0},{2,1},{3,2},{4,3},{5,4},{6,5},{7,6},{9,8},{10,9},{11,10},{12... | collective-permute-start | bytes 122888 | tf_op jit(solution)/shard_map/ppermute | solution.py:754
  75.3 9.7 %collective-permute-start.6 = (f32[80,128]{1,0:T(8,128)}, f32[80,128]{1,0:T(8,128)S(1)}, u32[]{:S(2)}, u32[]{:S(2)}) collective-permute-start(f32[80,128]{1,0:T(8,128)} %get-tuple-element.35.pay_hi), channel_id=1, source_target_pairs={{0,1},{1,2},{2,3},{3,4},{4,5},{5,6},{6,7},{8,9},{9,10},{10,11},{11... | collective-permute-start | bytes 122888 | tf_op jit(solution)/shard_map/ppermute | solution.py:754
  77.8 7.2 %copy-start.4 = (f32[80,128]{1,0:T(8,128)}, f32[80,128]{1,0:T(8,128)S(1)}, u32[]{:S(2)}) copy-start(f32[80,128]{1,0:T(8,128)S(1)} %collective-permute-done.7.got_hi) | copy-start | bytes 122884
  85.0 0.6 copy-start.5

commit v4 on v3

--- a/solution.py
+++ b/solution.py
@@ -23,13 +23,15 @@
 BAND = 64.0
 BIN = 256
 LOG2E = 1.4426950408889634
-VMEM_LIMIT = 56 * 1024 * 1024
+VMEM_LIMIT = 30 * 1024 * 1024
 TILE_UNROLL = 32
 WALK_UNROLL = 32
+ROW_UNROLL = 16
 PLANES = 4
 XW = CX + 4
 BINS = 2 * XW
-SEND = 128 + 8 * DEPTH + 8
+PART = 128 + 8 * DEPTH
+SEND = PART + 8 * DEPTH + 8
 
 VSPEC = pl.BlockSpec(memory_space=pltpu.VMEM)
 SSPEC = pl.BlockSpec(memory_space=pltpu.SMEM)
@@ -109,6 +111,53 @@
     return list(out[:16]), list(out[16:])
 
 
+OWN, RECV = 128, 32
+
+
+def profile(z, charge):
+    level = iota((DEPTH, 128), 0).astype(F32)
+    d = (level - z) * (math.sqrt(LOG2E) / 12.0)
+    p = jnp.exp2(-(d * d)) * charge
+    hi = p.astype(BF16)
+    lo = (p - hi.astype(F32)).astype(BF16)
+    return jnp.concatenate([hi, lo], axis=0)
+
+
+def walk(pile, cells, prof, count, last_bin, first_bin, end_bin, origin, unroll):
+    spot = iota((BIN, 128), 0)
+
+    def seek(i, s):
+        b = last_bin(i)
+        return s[0] + (b < first_bin).astype(I32), s[1] + (b <= end_bin).astype(I32)
+
+    start, stop = lax.fori_loop(0, count, seek, (jnp.int32(0), jnp.int32(0)), unroll=8)
+    stop = jnp.minimum(stop, count - 1)
+    steps = stop - start + 1 + (end_bin - first_bin)
+
+    def step(g, state):
+        i, j = state
+        work = []
+        for u in range(unroll):
+            inside = i <= stop
+            ii = jnp.minimum(i, count - 1)
+            work.append((ii, jnp.where(inside, j * BIN, -(1 << 20)), j - origin))
+            more = jnp.logical_and(last_bin(ii) > j, j < end_bin)
+            j = jnp.where(more, j + 1, j)
+            i = jnp.where(more, i, jnp.minimum(i + 1, count))
+        outs = []
+        for ii, first, home in work:
+            hot = jnp.where(spot == cells(ii) - first, 1.0, 0.0).astype(BF16)
+            out = lax.dot_general(prof(ii), hot, (((1,), (1,)), ((), ())), preferred_element_type=F32)
+            outs.append(out[:DEPTH] + out[DEPTH:])
+        for (ii, first, home), out in zip(work, outs):
+            pile[home] = pile[home] + out
+        return i, j
+
+    @pl.when(start <= stop)
+    def _():
+        lax.fori_loop(0, (steps + unroll - 1) // unroll, step, (start, jnp.int32(first_bin)))
+
+
 def split3(a):
     h1 = a.astype(BF16)
     r = a - h1.astype(F32)
@@ -120,7 +169,7 @@
 def particle_kernel(
     tgt, src, cnt, origin, loc, vel, halo_lo, halo_hi, site, bulk, octants, urow,
     nloc, nvel, skey, schg, last, send_lo, send_hi,
-    left, right, stat, acc, zrow, key,
+    left, right, stat, acc, zrow, key, last_v, last_s, rows, sem,
 ):
     wide = 4 * 128
 
@@ -222,6 +271,9 @@
     cs = [charge[8 * r : 8 * r + 8] for r in range(16)]
     ks, cs = bitonic(ks, cs)
     last[...] = ks[15][7:8]
+    last_v[...] = ks[15]
+    lasts = pltpu.make_async_copy(last_v, last_s, sem.at[0])
+    lasts.start()
     kt = jnp.concatenate(ks, axis=0)
     ct = jnp.concatenate(cs, axis=0)
     kt = jnp.transpose(kt)
@@ -239,6 +291,25 @@
         for c in range(4):
             at = 128 + ((r % 2) * 4 + c) * DEPTH
             ref[at : at + DEPTH] = urow[r, :, 128 * c : 128 * c + 128]
+    rows[...] = jnp.zeros_like(rows)
+    lasts.wait()
+
+    def cells(i):
+        return skey[pl.ds(i, 1), :] >> 6
+
+    def prof(i):
+        return profile((skey[pl.ds(i, 1), :] & 63).astype(F32), schg[pl.ds(i, 1), :])
+
+    for n, x in enumerate((G, G + CX - 2)):
+        walk(
+            rows, cells, prof, OWN, lambda i: last_s[7, i] >> 14,
+            2 * x, 2 * x + 3, 2 * x - 4 * n, ROW_UNROLL,
+        )
+    for r in range(4):
+        ref = send_lo if r < 2 else send_hi
+        for c in range(4):
+            at = PART + ((r % 2) * 4 + c) * DEPTH
+            ref[at : at + DEPTH] = rows[2 * r + c // 2, :, 128 * (c % 2) : 128 * (c % 2) + 128]
     for ref in (send_lo, send_hi):
         ref[SEND - 8 : SEND] = jnp.broadcast_to(last[...].astype(F32), (8, 128))
 
@@ -261,63 +332,19 @@
             pltpu.VMEM(((NB + 1) * 8, 128), F32),
             pltpu.VMEM((NB, 128), F32),
             pltpu.VMEM((NB, 128), I32),
+            pltpu.VMEM((8, 128), I32),
+            pltpu.SMEM((8, 128), I32),
+            pltpu.VMEM((8, DEPTH, BIN), F32),
+            pltpu.SemaphoreType.DMA((1,)),
         ],
         compiler_params=pltpu.CompilerParams(vmem_limit_bytes=VMEM_LIMIT),
         name="particle_step",
     )(tgt, src, cnt, origin, loc, vel, halo_lo, halo_hi, site, bulk, octants, urow)
 
 
-OWN, RECV = 128, 32
-
-
-def profile(z, charge):
-    level = iota((DEPTH, 128), 0).astype(F32)
-    d = (level - z) * (math.sqrt(LOG2E) / 12.0)
-    p = jnp.exp2(-(d * d)) * charge
-    hi = p.astype(BF16)
-    lo = (p - hi.astype(F32)).astype(BF16)
-    return jnp.concatenate([hi, lo], axis=0)
-
-
-def walk(pile, cells, prof, base, count, dummy, last_bin, first_bin, end_bin):
-    spot = iota((BIN, 128), 0)
-
-    def seek(i, s):
-        b = last_bin(i)
-        return s[0] + (b < first_bin).astype(I32), s[1] + (b <= end_bin).astype(I32)
-
-    start, stop = lax.fori_loop(0, count, seek, (jnp.int32(0), jnp.int32(0)), unroll=8)
-    stop = jnp.minimum(stop, count - 1)
-    steps = stop - start + 1 + (end_bin - first_bin)
-
-    def step(g, state):
-        i, j = state
-        work = []
-        for u in range(WALK_UNROLL):
-            work.append((jnp.where(i <= stop, base + i, dummy), j))
-            more = jnp.logical_and(last_bin(jnp.minimum(i, count - 1)) > j, j < end_bin)
-            j = jnp.where(more, j + 1, j)
-            i = jnp.where(more, i, jnp.minimum(i + 1, count))
-        outs = []
-        for ii, jj in work:
-            row = cells[pl.ds(ii, 1), :] - jj * BIN
-            hot = jnp.where(spot == row, 1.0, 0.0).astype(BF16)
-            out = lax.dot_general(prof[ii], hot, (((1,), (1,)), ((), ())), preferred_element_type=F32)
-            outs.append(out[:DEPTH] + out[DEPTH:])
-        for (ii, jj), out in zip(work, outs):
-            pile[jj] = pile[jj] + out
-        return i, j
-
-    @pl.when(start <= stop)
-    def _():
-        lax.fori_loop(0, (steps + WALK_UNROLL - 1) // WALK_UNROLL, step, (start, jnp.int32(first_bin)))
-
-
-def own_deposit_kernel(last, skey, schg, pile, row_lo, row_hi, cells, prof):
+def own_deposit_kernel(last, skey, schg, pile, cells, prof):
     own = skey[...]
     cells[0:OWN] = (own >> 6) - (G - HB) * CY
-    cells[OWN : OWN + 8] = jnp.full((8, 128), -1, I32)
-    prof[OWN] = jnp.zeros((128, 128), BF16)
 
     def profiles(i, carry):
         for u in range(8):
@@ -333,24 +360,22 @@
         return carry
 
     lax.fori_loop(0, BINS, clear, 0)
-    walk(pile, cells, prof, 0, OWN, OWN, lambda i: (last[i] >> 14) - 2 * (G - HB), 0, BINS - 1)
-    for ref, x0 in ((row_lo, 0), (row_hi, CX - 2)):
-        for r in range(2):
-            for c in range(4):
-                at = (r * 4 + c) * DEPTH
-                ref[at : at + DEPTH] = pile[2 * (x0 + r + 2) + c // 2, :, 128 * (c % 2) : 128 * (c % 2) + 128]
+    walk(
+        pile, lambda i: cells[pl.ds(i, 1), :], lambda i: prof[i], OWN,
+        lambda i: (last[i] >> 14) - 2 * (G - HB), 0, BINS - 1, 0, WALK_UNROLL,
+    )
 
 
 def own_deposit(last, skey, schg):
     sd = jax.ShapeDtypeStruct
     return pl.pallas_call(
         own_deposit_kernel,
-        out_shape=(sd((BINS, DEPTH, BIN), F32), sd((8 * DEPTH, 128), F32), sd((8 * DEPTH, 128), F32)),
+        out_shape=sd((BINS, DEPTH, BIN), F32),
         in_specs=[SSPEC, VSPEC, VSPEC],
-        out_specs=(VSPEC,) * 3,
+        out_specs=VSPEC,
         scratch_shapes=[
-            pltpu.VMEM((OWN + 8, 128), I32),
-            pltpu.VMEM((OWN + 1, 128, 128), BF16),
+            pltpu.VMEM((OWN, 128), I32),
+            pltpu.VMEM((OWN, 128, 128), BF16),
         ],
         compiler_params=pltpu.CompilerParams(vmem_limit_bytes=VMEM_LIMIT),
         name="own_deposit",
@@ -358,8 +383,8 @@
 
 
 def edge_deposit_kernel(
-    meta, pile_in, recv_lo, recv_hi, part_lo, part_hi, ucol,
-    share, vrow, pay_lo, pay_hi,
+    meta, pile_in, recv_lo, recv_hi, ucol,
+    share, here, vrow, pay_lo, pay_hi,
     pile, cells, prof, packs, last_v, last_s, sems,
 ):
     load = pltpu.make_async_copy(pile_in, pile, sems.at[0])
@@ -371,9 +396,6 @@
     for ref, at, shift in ((recv_lo, 0, HB - G - CX), (recv_hi, RECV, HB + CX - G)):
         x = ref[0:32].astype(I32) + shift
         cells[at : at + RECV] = x * CY + ref[32:64].astype(I32)
-    dummy = 2 * RECV
-    cells[dummy : dummy + 8] = jnp.full((8, 128), -1, I32)
-    prof[dummy] = jnp.zeros((128, 128), BF16)
 
     def profiles(i, carry):
         for ref, at in ((recv_lo, 0), (recv_hi, RECV)):
@@ -386,12 +408,17 @@
     lasts.wait()
     load.wait()
     half = 2 * (2 + G)
-    walk(pile, cells, prof, 0, RECV, dummy, lambda i: (last_s[0, OWN - RECV + i] >> 14) + 2 * (HB - G - CX), 4, half - 1)
-    walk(pile, cells, prof, RECV, RECV, dummy, lambda i: (last_s[1, i] >> 14) + 2 * (HB + CX - G), half, 2 * (2 + CX) - 1)
-    for ref, x0, flag in ((part_lo, 0, meta[2]), (part_hi, CX + 2, meta[3])):
+    for n, (at, by, first, end) in enumerate((
+        (OWN - RECV, HB - G - CX, 4, half - 1), (0, HB + CX - G, half, 2 * (2 + CX) - 1),
+    )):
+        walk(
+            pile, lambda i: cells[pl.ds(n * RECV + i, 1), :], lambda i: prof[n * RECV + i], RECV,
+            lambda i: (last_s[n, at + i] >> 14) + 2 * by, first, end, 0, WALK_UNROLL,
+        )
+    for ref, x0, flag in ((recv_lo, 0, meta[2]), (recv_hi, CX + 2, meta[3])):
         for r in range(2):
             for c in range(4):
-                at = (r * 4 + c) * DEPTH
+                at = PART + (r * 4 + c) * DEPTH
                 b = 2 * (x0 + r) + c // 2
                 cols = slice(128 * (c % 2), 128 * (c % 2) + 128)
                 pile[b, :, cols] = flag * (pile[b, :, cols] + ref[at : at + DEPTH])
@@ -399,10 +426,14 @@
     def turn(t):
         x = t >> 1
         cols = pl.ds(pl.multiple_of((t & 1) * BIN, BIN), BIN)
-        return pltpu.make_async_copy(pile.at[t + 2 * HB], share.at[:, x, cols], sems.at[2 + t])
+        return (
+            pltpu.make_async_copy(pile.at[t + 2 * HB], here.at[:, x, cols], sems.at[2 + t]),
+            pltpu.make_async_copy(pile.at[t + 2 * HB], share.at[:, x, cols], sems.at[2 + 2 * CX + t]),
+        )
 
     def turn_start(t, carry):
-        turn(t).start()
+        for copy in turn(t):
+            copy.start()
         return carry
 
     lax.fori_loop(0, 2 * CX, turn_start, 0)
@@ -422,7 +453,7 @@
         pick(x + 2, x)
         return carry
 
-    lax.fori_loop(0, CX, picks, 0)
+    lax.fori_loop(0, CX, picks, 0, unroll=4)
     pick(1, CX)
     pick(CX + 2, CX + 1)
     base = 128 + 4 * DEPTH
@@ -440,34 +471,35 @@
         pay[40 + CX : 80] = jnp.zeros((8, 128), F32)
 
     def turn_wait(t, carry):
-        turn(t).wait()
+        for copy in turn(t):
+            copy.wait()
         return carry
 
     lax.fori_loop(0, 2 * CX, turn_wait, 0)
 
 
-def edge_deposit(meta, pile, recv_lo, recv_hi, part_lo, part_hi, ucol):
+def edge_deposit(meta, pile, recv_lo, recv_hi, ucol):
     sd = jax.ShapeDtypeStruct
     return pl.pallas_call(
         edge_deposit_kernel,
         out_shape=(
-            sd((DEPTH, CX, CY), F32), sd((6, DEPTH, CY), F32),
+            sd((DEPTH, CX, CY), F32), sd((DEPTH, CX, CY), F32), sd((6, DEPTH, CY), F32),
             sd((80, 128), F32), sd((80, 128), F32),
         ),
-        in_specs=[SSPEC, ASPEC] + [VSPEC] * 5,
-        out_specs=(ASPEC, VSPEC, VSPEC, VSPEC),
+        in_specs=[SSPEC, ASPEC] + [VSPEC] * 3,
+        out_specs=(ASPEC, VSPEC, VSPEC, VSPEC, VSPEC),
         scratch_shapes=[
             pltpu.VMEM((BINS, DEPTH, BIN), F32),
-            pltpu.VMEM((2 * RECV + 8, 128), I32),
-            pltpu.VMEM((2 * RECV + 1, 128, 128), BF16),
+            pltpu.VMEM((2 * RECV, 128), I32),
+            pltpu.VMEM((2 * RECV, 128, 128), BF16),
             pltpu.VMEM((4, DEPTH, 128), F32),
             pltpu.VMEM((2, 128), I32),
             pltpu.SMEM((2, 128), I32),
-            pltpu.SemaphoreType.DMA((2 + 2 * CX,)),
+            pltpu.SemaphoreType.DMA((2 + 4 * CX,)),
         ],
         compiler_params=pltpu.CompilerParams(vmem_limit_bytes=VMEM_LIMIT),
         name="edge_deposit",
-    )(meta, pile, recv_lo, recv_hi, part_lo, part_hi, ucol)
+    )(meta, pile, recv_lo, recv_hi, ucol)
 
 
 def edges_kernel(cells, urow, ucol, left, right, sems):
@@ -522,21 +554,10 @@
 
 
 def heat_kernel(
-    meta, u_hbm, v_hbm, urow, recv_lo, recv_hi, vrow, pay_lo, pay_hi, got_lo, got_hi, out_hbm,
-    us, vs, ms, kz, fz, row1, row2, mrow, col1, col2, sems,
+    meta, us, vs, urow, recv_lo, recv_hi, vrow, pay_lo, pay_hi, got_lo, got_hi, out_hbm,
+    ms, os, kz, fz, row1, row2, mrow, col1, col2, sems,
 ):
     chunks = DEPTH // 8
-
-    def fetch(c):
-        at = pl.ds(pl.multiple_of(c * 8, 8), 8)
-        return (
-            pltpu.make_async_copy(u_hbm.at[at], us.at[at], sems.at[0, c]),
-            pltpu.make_async_copy(v_hbm.at[at], vs.at[at], sems.at[1, c]),
-        )
-
-    for c in range(chunks):
-        for copy in fetch(c):
-            copy.start()
 
     def glow_of(rows):
         d = rows * (1.0 / BAND)
@@ -683,16 +704,9 @@
 
     groups = DEPTH // PLANES
     per = 8 // PLANES
-    for copy in fetch(0):
-        copy.wait()
     begin(us)
 
     def one(g, carry):
-        @pl.when(lax.rem(g, per) == per - 1)
-        def _():
-            for copy in fetch((g + 1) // per):
-                copy.wait()
-
         planes(us, ms, row1, col1, glow1, g * PLANES, False)
         return carry
 
@@ -708,12 +722,12 @@
 
     def store(c):
         at = pl.ds(pl.multiple_of(c * 8, 8), 8)
-        return pltpu.make_async_copy(us.at[at], out_hbm.at[at], sems.at[0, c])
+        return pltpu.make_async_copy(os.at[at], out_hbm.at[at], sems.at[c])
 
     begin(ms)
 
     def two(g, carry):
-        planes(ms, us, row2, col2, glow2, g * PLANES, False)
+        planes(ms, os, row2, col2, glow2, g * PLANES, False)
 
         @pl.when(lax.rem(g, per) == per - 1)
         def _():
@@ -722,7 +736,7 @@
         return carry
 
     lax.fori_loop(0, groups - 1, two, 0)
-    planes(ms, us, row2, col2, glow2, DEPTH - PLANES, True)
+    planes(ms, os, row2, col2, glow2, DEPTH - PLANES, True)
     store(chunks - 1).start()
     for c in range(chunks):
         store(c).wait()
@@ -735,13 +749,13 @@
     return pl.pallas_call(
         heat_kernel,
         out_shape=jax.ShapeDtypeStruct((DEPTH, CX, CY), F32),
-        in_specs=[SSPEC, ASPEC, ASPEC] + [VSPEC] * 8,
+        in_specs=[SSPEC] + [VSPEC] * 10,
         out_specs=ASPEC,
         scratch_shapes=[
-            plane, plane, plane,
+            plane, plane,
             pltpu.VMEM((CX, CY), F32), pltpu.VMEM((CX, CY), F32),
             rows, rows, rows, column, column,
-            pltpu.SemaphoreType.DMA((2, DEPTH // 8)),
+            pltpu.SemaphoreType.DMA((DEPTH // 8,)),
         ],
         compiler_params=pltpu.CompilerParams(vmem_limit_bytes=VMEM_LIMIT),
         name="two_heat_steps",
@@ -786,16 +800,11 @@
     )
     recv_lo = shift(send_hi, "gx", 1)
     recv_hi = shift(send_lo, "gx", -1)
-    pile, row_lo, row_hi = own_deposit(last.reshape(128), skey, schg)
-    part_lo = shift(row_hi, "gx", 1)
-    part_hi = shift(row_lo, "gx", -1)
-
-    share, vrow, pay_lo, pay_hi = edge_deposit(
-        meta, pile, recv_lo, recv_hi, part_lo, part_hi, ucol,
-    )
+    pile = own_deposit(last.reshape(128), skey, schg)
+    share, here, vrow, pay_lo, pay_hi = edge_deposit(meta, pile, recv_lo, recv_hi, ucol)
     got_lo = shift(pay_hi, "gy", 1)
     got_hi = shift(pay_lo, "gy", -1)
-    final = heat(meta, thermal_excess, share, urow, recv_lo, recv_hi, vrow, pay_lo, pay_hi, got_lo, got_hi)
+    final = heat(meta, thermal_excess, here, urow, recv_lo, recv_hi, vrow, pay_lo, pay_hi, got_lo, got_hi)
     return nloc, nvel, share, final
 
 

time: 104 us -> 88.9 us (0.85)
  starting transfers between devices: 28.4 us -> 21.1 us
  Pallas kernels: 56.9 us -> 52 us
  waiting for transfers between devices: 13.3 us -> 10.8 us
    ppermute x8 -> x6, starting transfers between devices: 28.4 us -> 21.1 us  [shift(): lax.ppermute(value, axis, [(i, i + steps) for i in range(first, stop)])]
    pallas_call x1, Pallas kernels: 9.95 us -> 6.57 us  [own_deposit(): pl.pallas_call(own_deposit_kernel, out_shape=sd((BINS, DEPTH, BIN), F32),...]
    ppermute x8 -> x6, waiting for transfers between devices: 13.3 us -> 10.8 us  [shift(): lax.ppermute(value, axis, [(i, i + steps) for i in range(first, stop)])]
    pallas_call x1, Pallas kernels: 11.5 us -> 13.3 us  [particles(): pl.pallas_call(particle_kernel, out_shape=(sd((3, NPART), F32), sd((3, NP...]
    pallas_call x1, Pallas kernels: 3.6 us -> 1.86 us  [edges(): pl.pallas_call(edges_kernel, out_shape=(sd((4, DEPTH, CY), F32), sd((4, C...]
    unnamed x18 -> x20, local copies, waits for them, and re-layouts: 2.12 us -> 2.22 us
  transfers between devices with their start and end apart: 8 -> 6, of which waited for: 5 -> 3; matrix products, arithmetic and copies ran while one was open for 1% -> 0% of each run, Pallas kernels for 13% -> 10%
where the time goes in v4:
time: 88.9 us; the launch traced here: 88.6 us
  Pallas kernels  52 us (58%)
  starting transfers between devices  21.1 us (24%)
  waiting for transfers between devices  10.8 us (12%)
  local copies, waits for them, and re-layouts  2.22 us (2%)
  between operations  1.51 us (2%)
  other arithmetic  1.03 us (1%)
    ppermute x6, starting transfers between devices, shift(): lax.ppermute(value, axis, [(i, i + steps) for i in range(first, stop)])  21.1 us
    pallas_call x1, Pallas kernels, heat(): pl.pallas_call(heat_kernel, out_shape=jax.ShapeDtypeStruct((DEPTH, CX, CY...  17.8 us
    pallas_call x1, Pallas kernels, particles(): pl.pallas_call(particle_kernel, out_shape=(sd((3, NPART), F32), sd((3, NP...  13.3 us
    pallas_call x1, Pallas kernels, edge_deposit(): pl.pallas_call(edge_deposit_kernel, out_shape=(sd((DEPTH, CX, CY), F32),...  12.5 us
    ppermute x6, waiting for transfers between devices, shift(): lax.ppermute(value, axis, [(i, i + steps) for i in range(first, stop)])  10.8 us
    pallas_call x1, Pallas kernels, own_deposit(): pl.pallas_call(own_deposit_kernel, out_shape=sd((BINS, DEPTH, BIN), F32),...  6.57 us
    unnamed x20, local copies, waits for them, and re-layouts  2.22 us
    pallas_call x1, Pallas kernels, edges(): pl.pallas_call(edges_kernel, out_shape=(sd((4, DEPTH, CY), F32), sd((4, C...  1.86 us
  transfers between devices with their start and end apart: 6, of which 3 were waited for; matrix products, arithmetic and copies ran while one was open for 0% of the time, Pallas kernels for 10%

profile of v4, /device:TPU:24, one launch (start us, length us, event | category | flops | bytes accessed | tf_op | source)
XLA Modules:
  0.0 88.6 jit_solution(13917291486368562143)
XLA Ops:
  0.6 0.0 copy-start.3
  0.6 0.0 copy-start.2
  0.7 0.0 copy-start.8
  0.7 0.0 copy-start.7
  0.7 0.0 copy-start.9
  0.7 0.8 pad_maximum_fusion
  1.5 5.3 %collective-permute-start.1 = (f32[6,256]{1,0:T(8,128)S(1)}, f32[6,256]{1,0:T(8,128)S(1)}, u32[]{:S(2)}, u32[]{:S(2)}) collective-permute-start(f32[6,256]{1,0:T(8,128)S(1)} %get-tuple-element.32), channel_id=1, source_target_pairs={{1,0},{2,1},{3,2},{4,3},{5,4},{6,5},{7,6},{8,7},{9,8},{10,9},{11,1... | collective-permute-start | bytes 18440 | tf_op jit(solution)/shard_map/ppermute | solution.py:768
  6.8 1.9 %collective-permute-start = (f32[6,256]{1,0:T(8,128)S(1)}, f32[6,256]{1,0:T(8,128)S(1)}, u32[]{:S(2)}, u32[]{:S(2)}) collective-permute-start(f32[6,256]{1,0:T(8,128)S(1)} %get-tuple-element.33), channel_id=1, source_target_pairs={{0,1},{1,2},{2,3},{3,4},{4,5},{5,6},{6,7},{7,8},{8,9},{9,10},{10,1... | collective-permute-start | bytes 18440 | tf_op jit(solution)/shard_map/ppermute | solution.py:768
  8.7 0.1 pad_add_fusion.origin
  9.5 0.0 copy-start
  9.5 2.2 %copy-done = f32[64,32,512]{2,1,0:T(8,128)S(1)} copy-done((f32[64,32,512]{2,1,0:T(8,128)S(1)}, f32[64,32,512]{2,1,0:T(8,128)}, u32[]{:S(2)}) %copy-start) | copy-done | bytes 4194328
  11.7 0.0 copy-start.4
  11.7 0.0 copy-start.5
  11.7 0.0 copy-start.6
  11.7 1.9 %temperature_edges.1 = (f32[4,64,512]{2,1,0:T(8,128)S(1)}, f32[4,32,128]{2,1,0:T(8,128)S(1)}) custom-call(f32[64,32,512]{2,1,0:T(8,128)S(1)} %copy-done), custom_call_target="tpu_custom_call" | custom-call | tf_op jit(solution)/shard_map/temperature_edges/pallas_call | solution.py:533
  13.5 0.0 collective-permute-done.1.halo_hi
  13.6 2.4 %collective-permute-done.halo_lo = f32[6,256]{1,0:T(8,128)S(1)} collective-permute-done((f32[6,256]{1,0:T(8,128)S(1)}, f32[6,256]{1,0:T(8,128)S(1)}, u32[]{:S(2)}, u32[]{:S(2)}) %collective-permute-start) | collective-permute-done | bytes 6176 | tf_op jit(solution)/shard_map/ppermute | solution.py:768
  16.0 0.0 copy-done.3
  16.0 0.0 copy-done.2
  16.0 0.0 copy-done.8
  16.0 0.0 copy-done.7
  16.0 0.0 copy-done.4
  16.0 0.0 copy-done.5
  16.0 0.0 copy-done.6
  16.0 13.3 %particle_step.1 = (f32[3,16384]{1,0:T(4,128)}, f32[3,16384]{1,0:T(4,128)}, s32[128,128]{1,0:T(8,128)S(1)}, f32[128,128]{1,0:T(8,128)S(1)}, s32[1,128]{1,0:T(1,1...) custom-call(s32[256]{0:T(256)S(1)} %copy-done.7, s32[256]{0:T(256)S(1)} %copy-done.8, s32[1]{0:T(128)S(6)} %copy.14.cnt, ...), custom_call_target="tpu_custom_call" | custom-call | tf_op jit(solution)/shard_map/particle_step/pallas_call | solution.py:319
  29.4 1.9 %collective-permute-start.2 = (f32[1160,128]{1,0:T(8,128)S(1)}, f32[1160,128]{1,0:T(8,128)S(1)}, u32[]{:S(2)}, u32[]{:S(2)}) collective-permute-start(f32[1160,128]{1,0:T(8,128)S(1)} %get-tuple-element.24), channel_id=1, source_target_pairs={{0,8},{8,16},{16,24},{24,32},{32,40},{40,48},{48,56},{56,64},{64,7... | collective-permute-start | bytes 1781768 | tf_op jit(solution)/shard_map/ppermute | solution.py:768
  31.3 5.8 %collective-permute-start.3 = (f32[1160,128]{1,0:T(8,128)S(1)}, f32[1160,128]{1,0:T(8,128)S(1)}, u32[]{:S(2)}, u32[]{:S(2)}) collective-permute-start(f32[1160,128]{1,0:T(8,128)S(1)} %get-tuple-element.25), channel_id=1, source_target_pairs={{8,0},{16,8},{24,16},{32,24},{40,32},{48,40},{56,48},{64,56},{72,6... | collective-permute-start | bytes 1781768 | tf_op jit(solution)/shard_map/ppermute | solution.py:768
  37.1 0.1 add_convert_fusion
  37.1 0.0 copy-done.9
  37.1 0.1 pad_maximum_fusion.2.meta
  37.2 6.6 %own_deposit.1.pile_in = f32[72,64,256]{2,1,0:T(8,128)S(1)} custom-call(s32[128]{0:T(128)S(1)} %bitcast.11, s32[128,128]{1,0:T(8,128)S(1)} %get-tuple-element.22.skey, f32[128,128]{1,0:T(8,128)S(1)} %get-tuple-element.23.schg), custom_call_target="tpu_custom_call" | custom-call | tf_op jit(solution)/shard_map/own_deposit/pallas_call | solution.py:371
  43.8 0.0 copy-start.1
  43.8 0.0 collective-permute-done.2.recv_lo
  43.8 0.7 collective-permute-done.3.recv_hi
  44.5 12.5 %edge_deposit.1 = (f32[64,32,512]{2,1,0:T(8,128)}, f32[64,32,512]{2,1,0:T(8,128)S(1)}, f32[6,64,512]{2,1,0:T(8,128)S(1)}, f32[80,128]{1,0:T(8,128)S(1)}, f32[80,128]{1,0:T(8,128)S(1)}) custom-call(f32[6]{0:T(128)S(1)} %pad_maximum_fusion.2.meta, f32[72,64,256]{2,1,0:T(8,128)S(1)} %own_deposit.1.pile_in, f32[1160,128]{1,0:T(8,128)S(1)} %collective-permute-done.2.recv_lo, ...), custom_call_target="tpu_custom_call" | custom-call | tf_op jit(solution)/shard_map/edge_deposit/pallas_call | solution.py:483
  56.9 4.3 %collective-permute-start.5 = (f32[80,128]{1,0:T(8,128)S(1)}, f32[80,128]{1,0:T(8,128)S(1)}, u32[]{:S(2)}, u32[]{:S(2)}) collective-permute-start(f32[80,128]{1,0:T(8,128)S(1)} %get-tuple-element.30.pay_lo), channel_id=1, source_target_pairs={{1,0},{2,1},{3,2},{4,3},{5,4},{6,5},{7,6},{9,8},{10,9},{11,10},{12... | collective-permute-start | bytes 122888 | tf_op jit(solution)/shard_map/ppermute | solution.py:768
  61.2 1.9 %collective-permute-start.4 = (f32[80,128]{1,0:T(8,128)S(1)}, f32[80,128]{1,0:T(8,128)S(1)}, u32[]{:S(2)}, u32[]{:S(2)}) collective-permute-start(f32[80,128]{1,0:T(8,128)S(1)} %get-tuple-element.31.pay_hi), channel_id=1, source_target_pairs={{0,1},{1,2},{2,3},{3,4},{4,5},{5,6},{6,7},{8,9},{9,10},{10,11},{11... | collective-permute-start | bytes 122888 | tf_op jit(solution)/shard_map/ppermute | solution.py:768
  63.2 0.0 collective-permute-done.5.got_hi
  63.2 7.7 %collective-permute-done.4.got_lo = f32[80,128]{1,0:T(8,128)S(1)} collective-permute-done((f32[80,128]{1,0:T(8,128)S(1)}, f32[80,128]{1,0:T(8,128)S(1)}, u32[]{:S(2)}, u32[]{:S(2)}) %collective-permute-start.4) | collective-permute-done | bytes 40992 | tf_op jit(solution)/shard_map/ppermute | solution.py:768
  70.9 0.0 copy-done.1
  70.9 17.8 %two_heat_steps.1 = f32[64,32,512]{2,1,0:T(8,128)} custom-call(f32[6]{0:T(128)S(1)} %pad_maximum_fusion.2.meta, f32[64,32,512]{2,1,0:T(8,128)S(1)} %copy-done.1, f32[64,32,512]{2,1,0:T(8,128)S(1)} %get-tuple-element.28.vs, f32[4,64,512]{2,1,0:T(8,128)S(1)} %get-tuple-element.18.urow, f32[1160,128]{1,0:T(8,128)S(1)} %collective-permute-done.2.recv_lo, ...), custom_call_target="tpu_custom_call" | custom-call | tf_op jit(solution)/shard_map/two_heat_steps/pallas_call | solution.py:749
  (1 shorter events, 0.0 us)
Async XLA Ops:
  0.6 15.3 %copy-start.3 = (f32[3,16384]{1,0:T(4,128)S(1)}, f32[3,16384]{1,0:T(4,128)}, u32[]{:S(2)}) copy-start(f32[3,16384]{1,0:T(4,128)} %vel.1) | copy-start | bytes 589828
  0.6 15.3 %copy-start.2 = (f32[3,16384]{1,0:T(4,128)S(1)}, f32[3,16384]{1,0:T(4,128)}, u32[]{:S(2)}) copy-start(f32[3,16384]{1,0:T(4,128)} %loc.1) | copy-start | bytes 589828
  0.7 15.3 %copy-start.8 = (s32[256]{0:T(256)S(1)}, s32[256]{0:T(256)}, u32[]{:S(2)}) copy-start(s32[256]{0:T(256)} %src.1) | copy-start | bytes 3076
  0.7 15.3 %copy-start.7 = (s32[256]{0:T(256)S(1)}, s32[256]{0:T(256)}, u32[]{:S(2)}) copy-start(s32[256]{0:T(256)} %tgt.1) | copy-start | bytes 3076
  0.7 36.5 %copy-start.9 = (s32[2]{0:T(128)S(1)}, s32[2]{0:T(128)}, u32[]{:S(2)}) copy-start(s32[2]{0:T(128)} %param.19) | copy-start | bytes 28
  1.5 12.1 %collective-permute-start.1 = (f32[6,256]{1,0:T(8,128)S(1)}, f32[6,256]{1,0:T(8,128)S(1)}, u32[]{:S(2)}, u32[]{:S(2)}) collective-permute-start(f32[6,256]{1,0:T(8,128)S(1)} %get-tuple-element.32), channel_id=1, source_target_pairs={{1,0},{2,1},{3,2},{4,3},{5,4},{6,5},{7,6},{8,7},{9,8},{10,9},{11,1... | collective-permute-start | bytes 18440 | tf_op jit(solution)/shard_map/ppermute | solution.py:768
  6.8 9.2 %collective-permute-start = (f32[6,256]{1,0:T(8,128)S(1)}, f32[6,256]{1,0:T(8,128)S(1)}, u32[]{:S(2)}, u32[]{:S(2)}) collective-permute-start(f32[6,256]{1,0:T(8,128)S(1)} %get-tuple-element.33), channel_id=1, source_target_pairs={{0,1},{1,2},{2,3},{3,4},{4,5},{5,6},{6,7},{7,8},{8,9},{9,10},{10,1... | collective-permute-start | bytes 18440 | tf_op jit(solution)/shard_map/ppermute | solution.py:768
  9.5 2.2 %copy-start = (f32[64,32,512]{2,1,0:T(8,128)S(1)}, f32[64,32,512]{2,1,0:T(8,128)}, u32[]{:S(2)}) copy-start(f32[64,32,512]{2,1,0:T(8,128)} %us.1) | copy-start | bytes 12582916
  11.7 4.3 %copy-start.4 = (s32[3,16384]{1,0:T(4,128)S(1)}, s32[3,16384]{1,0:T(4,128)}, u32[]{:S(2)}) copy-start(s32[3,16384]{1,0:T(4,128)} %site.1) | copy-start | bytes 589828
  11.7 4.3 %copy-start.5 = (f32[16384]{0:T(1024)S(1)}, f32[16384]{0:T(1024)}, u32[]{:S(2)}) copy-start(f32[16384]{0:T(1024)} %param.12) | copy-start | bytes 196612
  11.7 4.3 %copy-start.6 = (s32[16384]{0:T(1024)S(1)}, s32[16384]{0:T(1024)}, u32[]{:S(2)}) copy-start(s32[16384]{0:T(1024)} %param.17) | copy-start | bytes 196612
  29.4 14.5 %collective-permute-start.2 = (f32[1160,128]{1,0:T(8,128)S(1)}, f32[1160,128]{1,0:T(8,128)S(1)}, u32[]{:S(2)}, u32[]{:S(2)}) collective-permute-start(f32[1160,128]{1,0:T(8,128)S(1)} %get-tuple-element.24), channel_id=1, source_target_pairs={{0,8},{8,16},{16,24},{24,32},{32,40},{40,48},{48,56},{56,64},{64,7... | collective-permute-start | bytes 1781768 | tf_op jit(solution)/shard_map/ppermute | solution.py:768
  31.3 13.2 %collective-permute-start.3 = (f32[1160,128]{1,0:T(8,128)S(1)}, f32[1160,128]{1,0:T(8,128)S(1)}, u32[]{:S(2)}, u32[]{:S(2)}) collective-permute-start(f32[1160,128]{1,0:T(8,128)S(1)} %get-tuple-element.25), channel_id=1, source_target_pairs={{8,0},{16,8},{24,16},{32,24},{40,32},{48,40},{56,48},{64,56},{72,6... | collective-permute-start | bytes 1781768 | tf_op jit(solution)/shard_map/ppermute | solution.py:768
  43.8 27.1 %copy-start.1 = (f32[64,32,512]{2,1,0:T(8,128)S(1)}, f32[64,32,512]{2,1,0:T(8,128)}, u32[]{:S(2)}) copy-start(f32[64,32,512]{2,1,0:T(8,128)} %us.1) | copy-start | bytes 12582916
  56.9 6.2 %collective-permute-start.5 = (f32[80,128]{1,0:T(8,128)S(1)}, f32[80,128]{1,0:T(8,128)S(1)}, u32[]{:S(2)}, u32[]{:S(2)}) collective-permute-start(f32[80,128]{1,0:T(8,128)S(1)} %get-tuple-element.30.pay_lo), channel_id=1, source_target_pairs={{1,0},{2,1},{3,2},{4,3},{5,4},{6,5},{7,6},{9,8},{10,9},{11,10},{12... | collective-permute-start | bytes 122888 | tf_op jit(solution)/shard_map/ppermute | solution.py:768
  61.2 9.6 %collective-permute-start.4 = (f32[80,128]{1,0:T(8,128)S(1)}, f32[80,128]{1,0:T(8,128)S(1)}, u32[]{:S(2)}, u32[]{:S(2)}) collective-permute-start(f32[80,128]{1,0:T(8,128)S(1)} %get-tuple-element.31.pay_hi), channel_id=1, source_target_pairs={{0,1},{1,2},{2,3},{3,4},{4,5},{5,6},{6,7},{8,9},{9,10},{10,11},{11... | collective-permute-start | bytes 122888 | tf_op jit(solution)/shard_map/ppermute | solution.py:768

commit v5 on v4

--- a/solution.py
+++ b/solution.py
@@ -123,15 +123,14 @@
     return jnp.concatenate([hi, lo], axis=0)
 
 
-def walk(pile, cells, prof, count, last_bin, first_bin, end_bin, origin, unroll):
+def count_below(bins, limit):
+    return jnp.sum(jnp.where(bins < limit, 1.0, 0.0)).astype(I32)
+
+
+def walk(pile, cells, prof, count, bins, last_bin, first_bin, end_bin, origin, unroll):
     spot = iota((BIN, 128), 0)
-
-    def seek(i, s):
-        b = last_bin(i)
-        return s[0] + (b < first_bin).astype(I32), s[1] + (b <= end_bin).astype(I32)
-
-    start, stop = lax.fori_loop(0, count, seek, (jnp.int32(0), jnp.int32(0)), unroll=8)
-    stop = jnp.minimum(stop, count - 1)
+    start = count_below(bins, float(first_bin))
+    stop = jnp.minimum(count_below(bins, float(end_bin + 1)), count - 1)
     steps = stop - start + 1 + (end_bin - first_bin)
 
     def step(g, state):
@@ -150,7 +149,8 @@
             out = lax.dot_general(prof(ii), hot, (((1,), (1,)), ((), ())), preferred_element_type=F32)
             outs.append(out[:DEPTH] + out[DEPTH:])
         for (ii, first, home), out in zip(work, outs):
-            pile[home] = pile[home] + out
+            x, at = home >> 1, pl.ds(pl.multiple_of((home & 1) * BIN, BIN), BIN)
+            pile[x, :, at] = pile[x, :, at] + out
         return i, j
 
     @pl.when(start <= stop)
@@ -302,14 +302,14 @@
 
     for n, x in enumerate((G, G + CX - 2)):
         walk(
-            rows, cells, prof, OWN, lambda i: last_s[7, i] >> 14,
+            rows, cells, prof, OWN, (ks[15][7:8] >> 14).astype(F32), lambda i: last_s[7, i] >> 14,
             2 * x, 2 * x + 3, 2 * x - 4 * n, ROW_UNROLL,
         )
     for r in range(4):
         ref = send_lo if r < 2 else send_hi
         for c in range(4):
             at = PART + ((r % 2) * 4 + c) * DEPTH
-            ref[at : at + DEPTH] = rows[2 * r + c // 2, :, 128 * (c % 2) : 128 * (c % 2) + 128]
+            ref[at : at + DEPTH] = rows[r, :, 128 * c : 128 * c + 128]
     for ref in (send_lo, send_hi):
         ref[SEND - 8 : SEND] = jnp.broadcast_to(last[...].astype(F32), (8, 128))
 
@@ -334,7 +334,7 @@
             pltpu.VMEM((NB, 128), I32),
             pltpu.VMEM((8, 128), I32),
             pltpu.SMEM((8, 128), I32),
-            pltpu.VMEM((8, DEPTH, BIN), F32),
+            pltpu.VMEM((4, DEPTH, CY), F32),
             pltpu.SemaphoreType.DMA((1,)),
         ],
         compiler_params=pltpu.CompilerParams(vmem_limit_bytes=VMEM_LIMIT),
@@ -342,7 +342,7 @@
     )(tgt, src, cnt, origin, loc, vel, halo_lo, halo_hi, site, bulk, octants, urow)
 
 
-def own_deposit_kernel(last, skey, schg, pile, cells, prof):
+def own_deposit_kernel(last, last_v, skey, schg, pile, cells, prof):
     own = skey[...]
     cells[0:OWN] = (own >> 6) - (G - HB) * CY
 
@@ -356,22 +356,23 @@
     lax.fori_loop(0, OWN // 8, profiles, 0)
 
     def clear(i, carry):
-        pile[i] = jnp.zeros((DEPTH, BIN), F32)
-        return carry
-
-    lax.fori_loop(0, BINS, clear, 0)
+        pile[i] = jnp.zeros((DEPTH, CY), F32)
+        return carry
+
+    lax.fori_loop(0, XW, clear, 0)
     walk(
         pile, lambda i: cells[pl.ds(i, 1), :], lambda i: prof[i], OWN,
+        ((last_v[...] >> 14) - 2 * (G - HB)).astype(F32),
         lambda i: (last[i] >> 14) - 2 * (G - HB), 0, BINS - 1, 0, WALK_UNROLL,
     )
 
 
-def own_deposit(last, skey, schg):
+def own_deposit(last, last_v, skey, schg):
     sd = jax.ShapeDtypeStruct
     return pl.pallas_call(
         own_deposit_kernel,
-        out_shape=sd((BINS, DEPTH, BIN), F32),
-        in_specs=[SSPEC, VSPEC, VSPEC],
+        out_shape=sd((XW, DEPTH, CY), F32),
+        in_specs=[SSPEC, VSPEC, VSPEC, VSPEC],
         out_specs=VSPEC,
         scratch_shapes=[
             pltpu.VMEM((OWN, 128), I32),
@@ -379,12 +380,12 @@
         ],
         compiler_params=pltpu.CompilerParams(vmem_limit_bytes=VMEM_LIMIT),
         name="own_deposit",
-    )(last, skey, schg)
+    )(last, last_v, skey, schg)
 
 
 def edge_deposit_kernel(
     meta, pile_in, recv_lo, recv_hi, ucol,
-    share, here, vrow, pay_lo, pay_hi,
+    here, vrow, pay_lo, pay_hi,
     pile, cells, prof, packs, last_v, last_s, sems,
 ):
     load = pltpu.make_async_copy(pile_in, pile, sems.at[0])
@@ -408,44 +409,39 @@
     lasts.wait()
     load.wait()
     half = 2 * (2 + G)
+    slot = iota((1, 128), 1)
     for n, (at, by, first, end) in enumerate((
         (OWN - RECV, HB - G - CX, 4, half - 1), (0, HB + CX - G, half, 2 * (2 + CX) - 1),
     )):
+        sent = jnp.logical_and(slot >= at, slot < at + RECV)
+        bins = jnp.where(sent, (last_v[n : n + 1] >> 14) + 2 * by, 4 * BINS).astype(F32)
         walk(
-            pile, lambda i: cells[pl.ds(n * RECV + i, 1), :], lambda i: prof[n * RECV + i], RECV,
+            pile, lambda i: cells[pl.ds(n * RECV + i, 1), :], lambda i: prof[n * RECV + i], RECV, bins,
             lambda i: (last_s[n, at + i] >> 14) + 2 * by, first, end, 0, WALK_UNROLL,
         )
+
+    def turn(x):
+        return pltpu.make_async_copy(pile.at[x + HB], here.at[:, x, :], sems.at[2 + x])
+
+    def turn_start(x, carry):
+        turn(x).start()
+        return carry
+
+    lax.fori_loop(0, CX, turn_start, 0)
     for ref, x0, flag in ((recv_lo, 0, meta[2]), (recv_hi, CX + 2, meta[3])):
         for r in range(2):
             for c in range(4):
                 at = PART + (r * 4 + c) * DEPTH
-                b = 2 * (x0 + r) + c // 2
-                cols = slice(128 * (c % 2), 128 * (c % 2) + 128)
-                pile[b, :, cols] = flag * (pile[b, :, cols] + ref[at : at + DEPTH])
-
-    def turn(t):
-        x = t >> 1
-        cols = pl.ds(pl.multiple_of((t & 1) * BIN, BIN), BIN)
-        return (
-            pltpu.make_async_copy(pile.at[t + 2 * HB], here.at[:, x, cols], sems.at[2 + t]),
-            pltpu.make_async_copy(pile.at[t + 2 * HB], share.at[:, x, cols], sems.at[2 + 2 * CX + t]),
-        )
-
-    def turn_start(t, carry):
-        for copy in turn(t):
-            copy.start()
-        return carry
-
-    lax.fori_loop(0, 2 * CX, turn_start, 0)
+                cols = slice(128 * c, 128 * c + 128)
+                pile[x0 + r, :, cols] = flag * (pile[x0 + r, :, cols] + ref[at : at + DEPTH])
     for n, x in enumerate((0, 1, 2, CX + 1, CX + 2, CX + 3)):
-        vrow[n, :, :BIN] = pile[2 * x]
-        vrow[n, :, BIN:] = pile[2 * x + 1]
+        vrow[n] = pile[x]
     lane = iota((DEPTH, 128), 1)
     packs[...] = jnp.zeros_like(packs)
 
     def pick(row, at):
-        a = pile[2 * row, :, 0:128]
-        b = pile[2 * row + 1, :, 128:256]
+        a = pile[row, :, 0:128]
+        b = pile[row, :, 384:512]
         for n, (t, by) in enumerate(((a, at), (a, at + 127), (b, at + 2), (b, at + 1))):
             packs[n] = jnp.where(lane == at, pltpu.roll(t, by & 127, 1), packs[n])
 
@@ -470,12 +466,11 @@
         pay[40 : 40 + CX] = t[0:CX] + ucol[far]
         pay[40 + CX : 80] = jnp.zeros((8, 128), F32)
 
-    def turn_wait(t, carry):
-        for copy in turn(t):
-            copy.wait()
-        return carry
-
-    lax.fori_loop(0, 2 * CX, turn_wait, 0)
+    def turn_wait(x, carry):
+        turn(x).wait()
+        return carry
+
+    lax.fori_loop(0, CX, turn_wait, 0)
 
 
 def edge_deposit(meta, pile, recv_lo, recv_hi, ucol):
@@ -483,19 +478,19 @@
     return pl.pallas_call(
         edge_deposit_kernel,
         out_shape=(
-            sd((DEPTH, CX, CY), F32), sd((DEPTH, CX, CY), F32), sd((6, DEPTH, CY), F32),
+            sd((DEPTH, CX, CY), F32), sd((6, DEPTH, CY), F32),
             sd((80, 128), F32), sd((80, 128), F32),
         ),
         in_specs=[SSPEC, ASPEC] + [VSPEC] * 3,
-        out_specs=(ASPEC, VSPEC, VSPEC, VSPEC, VSPEC),
+        out_specs=(VSPEC,) * 4,
         scratch_shapes=[
-            pltpu.VMEM((BINS, DEPTH, BIN), F32),
+            pltpu.VMEM((XW, DEPTH, CY), F32),
             pltpu.VMEM((2 * RECV, 128), I32),
             pltpu.VMEM((2 * RECV, 128, 128), BF16),
             pltpu.VMEM((4, DEPTH, 128), F32),
             pltpu.VMEM((2, 128), I32),
             pltpu.SMEM((2, 128), I32),
-            pltpu.SemaphoreType.DMA((2 + 4 * CX,)),
+            pltpu.SemaphoreType.DMA((2 + CX,)),
         ],
         compiler_params=pltpu.CompilerParams(vmem_limit_bytes=VMEM_LIMIT),
         name="edge_deposit",
@@ -553,59 +548,104 @@
     return (k + kn) * (un - u)
 
 
-def heat_kernel(
-    meta, us, vs, urow, recv_lo, recv_hi, vrow, pay_lo, pay_hi, got_lo, got_hi, out_hbm,
-    ms, os, kz, fz, row1, row2, mrow, col1, col2, sems,
-):
-    chunks = DEPTH // 8
-
-    def glow_of(rows):
-        d = rows * (1.0 / BAND)
-        return 0.5 * jnp.exp(-(d * d))
-
+def glow_of(rows):
+    d = rows * (1.0 / BAND)
+    return 0.5 * jnp.exp(-(d * d))
+
+
+TILES = range(CY // 128)
+
+
+def tile(c):
+    return slice(128 * c, 128 * c + 128)
+
+
+def load(ref, z):
+    return [ref[z, :, tile(c)] for c in TILES]
+
+
+def heat_planes(src, dst, vs, kz, fz, row_f, col_f, fix, glow, after):
     lane = iota((CX, 128), 1)
     sub = iota((CX, 128), 0)
-    lo_half = lane < DEPTH
-    side = jnp.where(lo_half, meta[4], meta[5])
-    glow1 = glow_of(sub.astype(F32) + meta[0])
-
-    def stacks(a, b, at, size):
-        p, q = a[at : at + size], b[at : at + size]
-        low = iota((size, 128), 1) < DEPTH
-        return jnp.where(low, p, pltpu.roll(q, DEPTH, 1)), jnp.where(low, pltpu.roll(p, DEPTH, 1), q)
-
-    def column_step(outer, here, inner, ends):
-        (uo, vo), (uh, vh), (ui, vi), (ue, ve) = outer, here, inner, ends
-        kh = half_kappa(uh, vh)
-        ke = half_kappa(ue, ve)
-        total = flux(kh, half_kappa(uo, vo), uh, uo) + flux(kh, half_kappa(ui, vi), uh, ui)
-
-        def near(a, e, n, pad):
-            below = jnp.where(sub == 0, e[0:1], pltpu.roll(a, 1, 0))
-            above = jnp.where(sub == CX - 1, e[1:2], pltpu.roll(a, CX - 1, 0))
-            up = jnp.where((lane & (DEPTH - 1)) == DEPTH - 1, pad, pltpu.roll(a, 127, 1))
-            down = jnp.where((lane & (DEPTH - 1)) == 0, pad, pltpu.roll(a, 1, 1))
-            return below, above, up, down
-
-        for kn, un in zip(near(kh, ke, 0, 0.05), near(uh, ue, 0, 0.0)):
-            total = total + flux(kh, kn, uh, un)
-        return uh + total + glow1 * vh, kh
-
-    outer = stacks(got_lo, got_hi, 40, CX)
-    here = stacks(got_lo, got_hi, 0, CX)
-    inner = stacks(pay_lo, pay_hi, 0, CX)
-    next_in = stacks(pay_lo, pay_hi, 40, CX)
-    corners = stacks(got_lo, got_hi, CX, 8)
-    mid_out, k_out = column_step(outer, here, inner, corners)
-    mid_in, k_in = column_step(here, inner, next_in, stacks(pay_lo, pay_hi, CX, 8))
-    mid_out = mid_out * side
-    sign = jnp.where(lo_half, 1.0, -1.0)
-    col1[...] = sign * flux(k_out, k_in, here[0], inner[0])
-    col2[...] = sign * flux(half_kappa(mid_out, here[1]), half_kappa(mid_in, inner[1]), mid_out, mid_in)
-
+
+    def fetch(z):
+        u = load(src, z)
+        if fix is not None:
+            u[0] = jnp.where(lane == 0, pltpu.roll(fix[...], (128 - z) & 127, 1), u[0])
+            u[3] = jnp.where(lane == 127, pltpu.roll(fix[...], 63 - z, 1), u[3])
+        return u
+
+    u0 = fetch(0)
+    v0 = load(vs, 0)
+    for c in TILES:
+        k = half_kappa(u0[c], v0[c])
+        kz[:, tile(c)] = k
+        fz[:, tile(c)] = (k + 0.05) * u0[c]
+
+    def planes(z0, is_last):
+        k = [kz[:, tile(c)] for c in TILES]
+        down = [fz[:, tile(c)] for c in TILES]
+        u = fetch(z0)
+        for p in range(PLANES):
+            z = z0 + p
+            v = load(vs, z)
+            if is_last and p == PLANES - 1:
+                un, kn = u, k
+                up = [(k[c] + 0.05) * (0.0 - u[c]) for c in TILES]
+            else:
+                un = fetch(z + 1)
+                vn = load(vs, z + 1)
+                kn = [half_kappa(un[c], vn[c]) for c in TILES]
+                up = [flux(k[c], kn[c], u[c], un[c]) for c in TILES]
+            row_first = row_f[pl.ds(z, 1), :]
+            row_end = row_f[pl.ds(z + DEPTH, 1), :]
+            ru = [pltpu.roll(u[c], 1, 1) for c in TILES]
+            rk = [pltpu.roll(k[c], 1, 1) for c in TILES]
+            g = []
+            for c in TILES:
+                if c == 0:
+                    f = flux(k[0], rk[0], ru[0], u[0])
+                    if col_f is not None:
+                        f = jnp.where(lane == 0, pltpu.roll(col_f[...], (128 - z) & 127, 1), f)
+                else:
+                    pu = jnp.where(lane == 0, ru[c - 1], ru[c])
+                    pk = jnp.where(lane == 0, rk[c - 1], rk[c])
+                    f = flux(k[c], pk, pu, u[c])
+                g.append(f)
+            rg = [pltpu.roll(g[c], 127, 1) for c in TILES]
+            for c in TILES:
+                if c < 3:
+                    gn = jnp.where(lane == 127, rg[c + 1], rg[c])
+                elif col_f is not None:
+                    gn = jnp.where(lane == 127, pltpu.roll(col_f[...], 63 - z, 1), rg[c])
+                else:
+                    gn = rg[c]
+                f = flux(k[c], pltpu.roll(k[c], 1, 0), pltpu.roll(u[c], 1, 0), u[c])
+                f = jnp.where(sub == 0, row_first[:, tile(c)], f)
+                fn = jnp.where(sub == CX - 1, row_end[:, tile(c)], pltpu.roll(f, CX - 1, 0))
+                total = (up[c] - down[c]) + (fn - f) + (gn - g[c])
+                dst[z, :, tile(c)] = u[c] + total + glow * v[c]
+            k, down, u = kn, up, un
+        for c in TILES:
+            kz[:, tile(c)] = k[c]
+            fz[:, tile(c)] = down[c]
+
+    groups = DEPTH // PLANES
+
+    def group(g, carry):
+        planes(g * PLANES, False)
+        after(g)
+        return carry
+
+    lax.fori_loop(0, groups - 1, group, 0)
+    planes(DEPTH - PLANES, True)
+
+
+def heat_one_kernel(meta, us, vs, urow, recv_lo, recv_hi, vrow, mid, mrow, share, kz, fz, row1, sem):
+    save = pltpu.make_async_copy(vs, share, sem.at[0])
+    save.start()
     lane_w = iota((DEPTH, CY), 1)
     sub_w = iota((DEPTH, CY), 0)
-    tail = [jnp.transpose(jnp.concatenate([g[CX : CX + 8]] * 16, axis=0)) for g in (got_lo, got_hi)]
     for n in range(2):
         recv = recv_lo if n == 0 else recv_hi
 
@@ -619,147 +659,146 @@
         kh = half_kappa(uh, vh)
         ki = half_kappa(ui, vi)
         total = flux(kh, half_kappa(uo, vo), uh, uo) + flux(kh, ki, uh, ui)
-        first_u = pltpu.roll(tail[0][:DEPTH], (128 - n) & 127, 1) if n else tail[0][:DEPTH]
-        first_v = pltpu.roll(tail[0][DEPTH:], (128 - n) & 127, 1) if n else tail[0][DEPTH:]
-        end_u = pltpu.roll(tail[1][:DEPTH], 127 - n, 1)
-        end_v = pltpu.roll(tail[1][DEPTH:], 127 - n, 1)
-        first_k, end_k = half_kappa(first_u, first_v), half_kappa(end_u, end_v)
-
-        def near(a, first, end, pad):
-            left = jnp.where(lane_w == 0, jnp.concatenate([first] * 4, axis=1), pltpu.roll(a, 1, 1))
-            right = jnp.where(lane_w == CY - 1, jnp.concatenate([end] * 4, axis=1), pltpu.roll(a, CY - 1, 1))
+
+        def near(a, pad):
+            left = jnp.where(lane_w == 0, a, pltpu.roll(a, 1, 1))
+            right = jnp.where(lane_w == CY - 1, a, pltpu.roll(a, CY - 1, 1))
             up = jnp.where(sub_w == DEPTH - 1, pad, pltpu.roll(a, DEPTH - 1, 0))
             down = jnp.where(sub_w == 0, pad, pltpu.roll(a, 1, 0))
             return left, right, up, down
 
-        for kn, un in zip(near(kh, first_k, end_k, 0.05), near(uh, first_u, end_u, 0.0)):
+        for kn, un in zip(near(kh, 0.05), near(uh, 0.0)):
             total = total + flux(kh, kn, uh, un)
         row_at = meta[0] + (-1.0 if n == 0 else float(CX))
         gl = glow_of(jnp.full((1, CY), 1.0, F32) * row_at)
-        mrow[DEPTH * n : DEPTH * n + DEPTH] = (uh + total + gl * vh) * meta[2 + n]
+        mrow[n] = uh + total + gl * vh
         row1[DEPTH * n : DEPTH * n + DEPTH] = flux(kh, ki, uh, ui) if n == 0 else flux(ki, kh, ui, uh)
-
-    glow2 = glow_of(sub.astype(F32) + meta[1])
-    tiles = range(4)
-
-    def load(ref, z):
-        return [ref[z, :, 128 * c : 128 * c + 128] for c in tiles]
-
-    def planes(src, dst, row_f, col_f, glow, z0, is_last):
-        k = load2(kz)
-        down = load2(fz)
-        cols = col_f[...]
-        for p in range(PLANES):
-            z = z0 + p
-            u = load(src, z)
-            v = load(vs, z)
-            if is_last and p == PLANES - 1:
-                kn = k
-                up = [(k[c] + 0.05) * (0.0 - u[c]) for c in tiles]
-            else:
-                un = load(src, z + 1)
-                vn = load(vs, z + 1)
-                kn = [half_kappa(un[c], vn[c]) for c in tiles]
-                up = [flux(k[c], kn[c], u[c], un[c]) for c in tiles]
-            row_first = row_f[pl.ds(z, 1), :]
-            row_end = row_f[pl.ds(z + DEPTH, 1), :]
-            edge0 = pltpu.roll(cols, (128 - z) & 127, 1)
-            edge1 = pltpu.roll(cols, 63 - z, 1)
-            ru = [pltpu.roll(u[c], 1, 1) for c in tiles]
-            rk = [pltpu.roll(k[c], 1, 1) for c in tiles]
-            g = []
-            for c in tiles:
-                if c == 0:
-                    g.append(jnp.where(lane == 0, edge0, flux(k[0], rk[0], ru[0], u[0])))
-                else:
-                    pu = jnp.where(lane == 0, ru[c - 1], ru[c])
-                    pk = jnp.where(lane == 0, rk[c - 1], rk[c])
-                    g.append(flux(k[c], pk, pu, u[c]))
-            rg = [pltpu.roll(g[c], 127, 1) for c in tiles]
-            for c in tiles:
-                at = slice(128 * c, 128 * c + 128)
-                gn = jnp.where(lane == 127, rg[c + 1] if c < 3 else edge1, rg[c])
-                f = flux(k[c], pltpu.roll(k[c], 1, 0), pltpu.roll(u[c], 1, 0), u[c])
-                f = jnp.where(sub == 0, row_first[:, at], f)
-                fn = jnp.where(sub == CX - 1, row_end[:, at], pltpu.roll(f, CX - 1, 0))
-                total = (up[c] - down[c]) + (fn - f) + (gn - g[c])
-                dst[z, :, at] = u[c] + total + glow * v[c]
-            k, down = kn, up
-        for c in tiles:
-            at = slice(128 * c, 128 * c + 128)
-            kz[:, at] = k[c]
-            fz[:, at] = down[c]
-
-    def load2(ref):
-        return [ref[:, 128 * c : 128 * c + 128] for c in tiles]
-
-    def begin(src):
-        u = load(src, 0)
-        v = load(vs, 0)
-        for c in tiles:
-            at = slice(128 * c, 128 * c + 128)
-            k = half_kappa(u[c], v[c])
-            kz[:, at] = k
-            fz[:, at] = (k + 0.05) * u[c]
-
-    groups = DEPTH // PLANES
+    glow = glow_of(iota((CX, 128), 0).astype(F32) + meta[0])
+    heat_planes(us, mid, vs, kz, fz, row1, None, None, glow, lambda g: None)
+    save.wait()
+
+
+def heat_one(meta, u, v, urow, recv_lo, recv_hi, vrow):
+    sd = jax.ShapeDtypeStruct
+    return pl.pallas_call(
+        heat_one_kernel,
+        out_shape=(sd((DEPTH, CX, CY), F32), sd((2, DEPTH, CY), F32), sd((DEPTH, CX, CY), F32)),
+        in_specs=[SSPEC] + [VSPEC] * 6,
+        out_specs=(VSPEC, VSPEC, ASPEC),
+        scratch_shapes=[
+            pltpu.VMEM((CX, CY), F32), pltpu.VMEM((CX, CY), F32),
+            pltpu.VMEM((2 * DEPTH, CY), F32),
+            pltpu.SemaphoreType.DMA((1,)),
+        ],
+        compiler_params=pltpu.CompilerParams(vmem_limit_bytes=VMEM_LIMIT),
+        cost_estimate=pl.CostEstimate(flops=1 << 25, bytes_accessed=1 << 24, transcendentals=1 << 21),
+        name="heat_step_one",
+    )(meta, u, v, urow, recv_lo, recv_hi, vrow)
+
+
+def heat_two_kernel(
+    meta, mid, vs, mpart, recv_lo, recv_hi, vrow, pay_lo, pay_hi, got_lo, got_hi, out_hbm,
+    os, kz, fz, row2, fix, col2, sems,
+):
+    lane = iota((CX, 128), 1)
+    sub = iota((CX, 128), 0)
+    lo_half = lane < DEPTH
+    side = jnp.where(lo_half, meta[4], meta[5])
+    glow1 = glow_of(sub.astype(F32) + meta[0])
+
+    def stacks(a, b, at, size):
+        p, q = a[at : at + size], b[at : at + size]
+        low = iota((size, 128), 1) < DEPTH
+        return jnp.where(low, p, pltpu.roll(q, DEPTH, 1)), jnp.where(low, pltpu.roll(p, DEPTH, 1), q)
+
+    def column_step(outer, here, inner, ends):
+        (uo, vo), (uh, vh), (ui, vi), (ue, ve) = outer, here, inner, ends
+        kh = half_kappa(uh, vh)
+        ke = half_kappa(ue, ve)
+        total = flux(kh, half_kappa(uo, vo), uh, uo) + flux(kh, half_kappa(ui, vi), uh, ui)
+
+        def near(a, e, pad):
+            below = jnp.where(sub == 0, e[0:1], pltpu.roll(a, 1, 0))
+            above = jnp.where(sub == CX - 1, e[1:2], pltpu.roll(a, CX - 1, 0))
+            up = jnp.where((lane & (DEPTH - 1)) == DEPTH - 1, pad, pltpu.roll(a, 127, 1))
+            down = jnp.where((lane & (DEPTH - 1)) == 0, pad, pltpu.roll(a, 1, 1))
+            return below, above, up, down
+
+        for kn, un in zip(near(kh, ke, 0.05), near(uh, ue, 0.0)):
+            total = total + flux(kh, kn, uh, un)
+        return uh + total + glow1 * vh
+
+    outer = stacks(got_lo, got_hi, 40, CX)
+    here = stacks(got_lo, got_hi, 0, CX)
+    inner = stacks(pay_lo, pay_hi, 0, CX)
+    next_in = stacks(pay_lo, pay_hi, 40, CX)
+    mid_out = column_step(outer, here, inner, stacks(got_lo, got_hi, CX, 8)) * side
+    mid_in = column_step(here, inner, next_in, stacks(pay_lo, pay_hi, CX, 8))
+    sign = jnp.where(lo_half, 1.0, -1.0)
+    fix[...] = mid_in
+    col2[...] = sign * flux(half_kappa(mid_out, here[1]), half_kappa(mid_in, inner[1]), mid_out, mid_in)
+
+    tail = [jnp.transpose(jnp.concatenate([g[CX : CX + 8]] * 16, axis=0)) for g in (got_lo, got_hi)]
+    ends = jnp.transpose(jnp.concatenate([mid_in] * 4, axis=0))
+    lane_t = iota((DEPTH, 128), 1)
+
+    def turned(a, by):
+        return pltpu.roll(a, by & 127, 1) if by & 127 else a
+
+    for n in range(2):
+        x = 0 if n == 0 else CX - 1
+        recv, r, vh = (recv_lo, 1, vrow[1]) if n == 0 else (recv_hi, 0, vrow[4])
+        mh = [mpart[n, :, tile(c)] for c in TILES]
+        mi = [mid[:, x, tile(c)] for c in TILES]
+        for c, at, half, g, e in ((0, 0, 0, 0, 0), (3, 127, DEPTH, 1, 127)):
+            base = 128 + (r * 4 + c) * DEPTH
+            uc = recv[base : base + DEPTH]
+            kc = half_kappa(uc, vh[:, tile(c)])
+            ue = turned(tail[g][:DEPTH], e - n)
+            ke = half_kappa(ue, turned(tail[g][DEPTH:], e - n))
+            mh[c] = mh[c] + jnp.where(lane_t == at, flux(kc, ke, uc, ue), 0.0)
+            mi[c] = jnp.where(lane_t == at, turned(ends[half : half + DEPTH], e - x), mi[c])
+        vi = vrow[2] if n == 0 else vrow[3]
+        for c in TILES:
+            m = mh[c] * meta[2 + n]
+            kh = half_kappa(m, vh[:, tile(c)])
+            ki = half_kappa(mi[c], vi[:, tile(c)])
+            row2[DEPTH * n : DEPTH * n + DEPTH, tile(c)] = flux(kh, ki, m, mi[c]) if n == 0 else flux(ki, kh, mi[c], m)
+
     per = 8 // PLANES
-    begin(us)
-
-    def one(g, carry):
-        planes(us, ms, row1, col1, glow1, g * PLANES, False)
-        return carry
-
-    lax.fori_loop(0, groups - 1, one, 0)
-    planes(us, ms, row1, col1, glow1, DEPTH - PLANES, True)
-
-    for n in range(2):
-        mh = mrow[DEPTH * n : DEPTH * n + DEPTH]
-        kh = half_kappa(mh, vrow[1] if n == 0 else vrow[4])
-        mi = ms[:, 0 if n == 0 else CX - 1, :]
-        ki = half_kappa(mi, vrow[2] if n == 0 else vrow[3])
-        row2[DEPTH * n : DEPTH * n + DEPTH] = flux(kh, ki, mh, mi) if n == 0 else flux(ki, kh, mi, mh)
 
     def store(c):
         at = pl.ds(pl.multiple_of(c * 8, 8), 8)
         return pltpu.make_async_copy(os.at[at], out_hbm.at[at], sems.at[c])
 
-    begin(ms)
-
-    def two(g, carry):
-        planes(ms, os, row2, col2, glow2, g * PLANES, False)
-
+    def after(g):
         @pl.when(lax.rem(g, per) == per - 1)
         def _():
             store(g // per).start()
 
-        return carry
-
-    lax.fori_loop(0, groups - 1, two, 0)
-    planes(ms, os, row2, col2, glow2, DEPTH - PLANES, True)
-    store(chunks - 1).start()
-    for c in range(chunks):
+    glow = glow_of(sub.astype(F32) + meta[1])
+    heat_planes(mid, os, vs, kz, fz, row2, col2, fix, glow, after)
+    store(DEPTH // 8 - 1).start()
+    for c in range(DEPTH // 8):
         store(c).wait()
 
 
-def heat(meta, u, v, urow, recv_lo, recv_hi, vrow, pay_lo, pay_hi, got_lo, got_hi):
-    plane = pltpu.VMEM((DEPTH, CX, CY), F32)
-    rows = pltpu.VMEM((2 * DEPTH, CY), F32)
-    column = pltpu.VMEM((CX, 128), F32)
+def heat_two(meta, mid, v, mpart, recv_lo, recv_hi, vrow, pay_lo, pay_hi, got_lo, got_hi):
     return pl.pallas_call(
-        heat_kernel,
+        heat_two_kernel,
         out_shape=jax.ShapeDtypeStruct((DEPTH, CX, CY), F32),
         in_specs=[SSPEC] + [VSPEC] * 10,
         out_specs=ASPEC,
         scratch_shapes=[
-            plane, plane,
+            pltpu.VMEM((DEPTH, CX, CY), F32),
             pltpu.VMEM((CX, CY), F32), pltpu.VMEM((CX, CY), F32),
-            rows, rows, rows, column, column,
+            pltpu.VMEM((2 * DEPTH, CY), F32),
+            pltpu.VMEM((CX, 128), F32), pltpu.VMEM((CX, 128), F32),
             pltpu.SemaphoreType.DMA((DEPTH // 8,)),
         ],
         compiler_params=pltpu.CompilerParams(vmem_limit_bytes=VMEM_LIMIT),
-        name="two_heat_steps",
-    )(meta, u, v, urow, recv_lo, recv_hi, vrow, pay_lo, pay_hi, got_lo, got_hi)
+        name="heat_step_two",
+    )(meta, mid, v, mpart, recv_lo, recv_hi, vrow, pay_lo, pay_hi, got_lo, got_hi)
 
 
 def shift(value, axis, steps):
@@ -800,11 +839,12 @@
     )
     recv_lo = shift(send_hi, "gx", 1)
     recv_hi = shift(send_lo, "gx", -1)
-    pile = own_deposit(last.reshape(128), skey, schg)
-    share, here, vrow, pay_lo, pay_hi = edge_deposit(meta, pile, recv_lo, recv_hi, ucol)
+    pile = own_deposit(last.reshape(128), last, skey, schg)
+    here, vrow, pay_lo, pay_hi = edge_deposit(meta, pile, recv_lo, recv_hi, ucol)
     got_lo = shift(pay_hi, "gy", 1)
     got_hi = shift(pay_lo, "gy", -1)
-    final = heat(meta, thermal_excess, here, urow, recv_lo, recv_hi, vrow, pay_lo, pay_hi, got_lo, got_hi)
+    mid, mpart, share = heat_one(meta, thermal_excess, here, urow, recv_lo, recv_hi, vrow)
+    final = heat_two(meta, mid, here, mpart, recv_lo, recv_hi, vrow, pay_lo, pay_hi, got_lo, got_hi)
     return nloc, nvel, share, final
 
 

time: 88.9 us -> 85.2 us (0.958)
  the two profiles are of different devices: /device:TPU:24 before, /device:TPU:17 now
where the time goes in v5:
time: 85.2 us; the launch traced here: 86.4 us
  Pallas kernels  50.9 us (60%)
  starting transfers between devices  27.8 us (33%)
  waiting for transfers between devices  2.95 us (3%)
  local copies, waits for them, and re-layouts  2.22 us (3%)
  between operations  1.55 us (2%)
  other arithmetic  1.03 us (1%)
    ppermute x6, starting transfers between devices, shift(): lax.ppermute(value, axis, [(i, i + steps) for i in range(first, stop)])  27.8 us
    pallas_call x1, Pallas kernels, particles(): pl.pallas_call(particle_kernel, out_shape=(sd((3, NPART), F32), sd((3, NP...  12.4 us
    pallas_call x1, Pallas kernels, heat_two(): pl.pallas_call(heat_two_kernel, out_shape=jax.ShapeDtypeStruct((DEPTH, CX...  11.6 us
    pallas_call x1, Pallas kernels, edge_deposit(): pl.pallas_call(edge_deposit_kernel, out_shape=(sd((DEPTH, CX, CY), F32),...  10.4 us
    pallas_call x1, Pallas kernels, heat_one(): pl.pallas_call(heat_one_kernel, out_shape=(sd((DEPTH, CX, CY), F32), sd((...  8.42 us
    pallas_call x1, Pallas kernels, own_deposit(): pl.pallas_call(own_deposit_kernel, out_shape=sd((XW, DEPTH, CY), F32), in...  6.18 us
    ppermute x6, waiting for transfers between devices, shift(): lax.ppermute(value, axis, [(i, i + steps) for i in range(first, stop)])  2.95 us
    unnamed x20, local copies, waits for them, and re-layouts  2.22 us
  transfers between devices with their start and end apart: 6, of which 1 were waited for; matrix products, arithmetic and copies ran while one was open for 0% of the time, Pallas kernels for 19%

profile of v5, /device:TPU:17, one launch (start us, length us, event | category | flops | bytes accessed | tf_op | source)
XLA Modules:
  0.0 86.4 jit_solution(16165568963942683269)
XLA Ops:
  0.6 0.0 copy-start.2
  0.6 0.0 copy-start.3
  0.7 0.0 copy-start.7
  0.7 0.0 copy-start.8
  0.7 0.0 copy-start.9
  0.7 0.8 pad_maximum_fusion
  1.5 3.1 %collective-permute-start = (f32[6,256]{1,0:T(8,128)S(1)}, f32[6,256]{1,0:T(8,128)S(1)}, u32[]{:S(2)}, u32[]{:S(2)}) collective-permute-start(f32[6,256]{1,0:T(8,128)S(1)} %get-tuple-element.37), channel_id=1, source_target_pairs={{0,1},{1,2},{2,3},{3,4},{4,5},{5,6},{6,7},{7,8},{8,9},{9,10},{10,1... | collective-permute-start | bytes 18440 | tf_op jit(solution)/shard_map/ppermute | solution.py:807
  4.6 5.8 %collective-permute-start.1 = (f32[6,256]{1,0:T(8,128)S(1)}, f32[6,256]{1,0:T(8,128)S(1)}, u32[]{:S(2)}, u32[]{:S(2)}) collective-permute-start(f32[6,256]{1,0:T(8,128)S(1)} %get-tuple-element.36), channel_id=1, source_target_pairs={{1,0},{2,1},{3,2},{4,3},{5,4},{6,5},{7,6},{8,7},{9,8},{10,9},{11,1... | collective-permute-start | bytes 18440 | tf_op jit(solution)/shard_map/ppermute | solution.py:807
  10.4 0.1 pad_add_fusion.origin
  11.1 0.0 copy-start
  11.1 2.2 %copy-done = f32[64,32,512]{2,1,0:T(8,128)S(1)} copy-done((f32[64,32,512]{2,1,0:T(8,128)S(1)}, f32[64,32,512]{2,1,0:T(8,128)}, u32[]{:S(2)}) %copy-start) | copy-done | bytes 4194328
  13.3 0.0 copy-start.4
  13.3 0.0 copy-start.5
  13.3 0.0 copy-start.6
  13.3 1.9 %temperature_edges.1 = (f32[4,64,512]{2,1,0:T(8,128)S(1)}, f32[4,32,128]{2,1,0:T(8,128)S(1)}) custom-call(f32[64,32,512]{2,1,0:T(8,128)S(1)} %copy-done), custom_call_target="tpu_custom_call" | custom-call | tf_op jit(solution)/shard_map/temperature_edges/pallas_call | solution.py:528
  15.2 0.0 collective-permute-done.halo_lo
  15.2 0.0 collective-permute-done.1.halo_hi
  15.2 0.0 copy-done.2
  15.2 0.0 copy-done.3
  15.2 0.0 copy-done.7
  15.2 0.0 copy-done.8
  15.2 0.0 copy-done.4
  15.3 0.0 copy-done.5
  15.3 0.0 copy-done.6
  15.3 12.4 %particle_step.1 = (f32[3,16384]{1,0:T(4,128)}, f32[3,16384]{1,0:T(4,128)}, s32[128,128]{1,0:T(8,128)S(1)}, f32[128,128]{1,0:T(8,128)S(1)}, s32[1,128]{1,0:T(1,1...) custom-call(s32[256]{0:T(256)S(1)} %copy-done.7, s32[256]{0:T(256)S(1)} %copy-done.8, s32[1]{0:T(128)S(6)} %copy.14.cnt, ...), custom_call_target="tpu_custom_call" | custom-call | tf_op jit(solution)/shard_map/particle_step/pallas_call | solution.py:319
  27.7 8.1 %collective-permute-start.2 = (f32[1160,128]{1,0:T(8,128)S(1)}, f32[1160,128]{1,0:T(8,128)S(1)}, u32[]{:S(2)}, u32[]{:S(2)}) collective-permute-start(f32[1160,128]{1,0:T(8,128)S(1)} %get-tuple-element.26), channel_id=1, source_target_pairs={{0,8},{8,16},{16,24},{24,32},{32,40},{40,48},{48,56},{56,64},{64,7... | collective-permute-start | bytes 1781768 | tf_op jit(solution)/shard_map/ppermute | solution.py:807
  35.8 1.9 %collective-permute-start.3 = (f32[1160,128]{1,0:T(8,128)S(1)}, f32[1160,128]{1,0:T(8,128)S(1)}, u32[]{:S(2)}, u32[]{:S(2)}) collective-permute-start(f32[1160,128]{1,0:T(8,128)S(1)} %get-tuple-element.27), channel_id=1, source_target_pairs={{8,0},{16,8},{24,16},{32,24},{40,32},{48,40},{56,48},{64,56},{72,6... | collective-permute-start | bytes 1781768 | tf_op jit(solution)/shard_map/ppermute | solution.py:807
  37.7 0.1 add_convert_fusion
  37.8 0.0 copy-done.9
  37.8 0.1 pad_maximum_fusion.2.meta
  37.9 6.2 %own_deposit.1.pile_in = f32[36,64,512]{2,1,0:T(8,128)S(1)} custom-call(s32[128]{0:T(128)S(1)} %bitcast.11, s32[1,128]{1,0:T(1,128)S(1)} %get-tuple-element.23.last_v, s32[128,128]{1,0:T(8,128)S(1)} %get-tuple-element.24.skey, f32[128,128]{1,0:T(8,128)S(1)} %get-tuple-element.25.schg), custom_call_target="tpu_custom_call" | custom-call | tf_op jit(solution)/shard_map/own_deposit/pallas_call | solution.py:372
  44.1 0.0 copy-start.1
  44.1 0.0 collective-permute-done.2.recv_lo
  44.1 2.9 %collective-permute-done.3.recv_hi = f32[1160,128]{1,0:T(8,128)S(1)} collective-permute-done((f32[1160,128]{1,0:T(8,128)S(1)}, f32[1160,128]{1,0:T(8,128)S(1)}, u32[]{:S(2)}, u32[]{:S(2)}) %collective-permute-start.3) | collective-permute-done | bytes 593952 | tf_op jit(solution)/shard_map/ppermute | solution.py:807
  47.0 10.4 %edge_deposit.1 = (f32[64,32,512]{2,1,0:T(8,128)S(1)}, f32[6,64,512]{2,1,0:T(8,128)S(1)}, f32[80,128]{1,0:T(8,128)S(1)}, f32[80,128]{1,0:T(8,128)S(1)}) custom-call(f32[6]{0:T(128)S(1)} %pad_maximum_fusion.2.meta, f32[36,64,512]{2,1,0:T(8,128)S(1)} %own_deposit.1.pile_in, f32[1160,128]{1,0:T(8,128)S(1)} %collective-permute-done.2.recv_lo, ...), custom_call_target="tpu_custom_call" | custom-call | tf_op jit(solution)/shard_map/edge_deposit/pallas_call | solution.py:478
  57.5 1.9 %collective-permute-start.4 = (f32[80,128]{1,0:T(8,128)S(1)}, f32[80,128]{1,0:T(8,128)S(1)}, u32[]{:S(2)}, u32[]{:S(2)}) collective-permute-start(f32[80,128]{1,0:T(8,128)S(1)} %get-tuple-element.35.pay_hi), channel_id=1, source_target_pairs={{0,1},{1,2},{2,3},{3,4},{4,5},{5,6},{6,7},{8,9},{9,10},{10,11},{11... | collective-permute-start | bytes 122888 | tf_op jit(solution)/shard_map/ppermute | solution.py:807
  59.4 7.0 %collective-permute-start.5 = (f32[80,128]{1,0:T(8,128)S(1)}, f32[80,128]{1,0:T(8,128)S(1)}, u32[]{:S(2)}, u32[]{:S(2)}) collective-permute-start(f32[80,128]{1,0:T(8,128)S(1)} %get-tuple-element.34.pay_lo), channel_id=1, source_target_pairs={{1,0},{2,1},{3,2},{4,3},{5,4},{6,5},{7,6},{9,8},{10,9},{11,10},{12... | collective-permute-start | bytes 122888 | tf_op jit(solution)/shard_map/ppermute | solution.py:807
  66.4 0.0 copy-done.1
  66.4 8.4 %heat_step_one.1 = (f32[64,32,512]{2,1,0:T(8,128)S(1)}, f32[2,64,512]{2,1,0:T(8,128)S(1)}, f32[64,32,512]{2,1,0:T(8,128)}) custom-call(f32[6]{0:T(128)S(1)} %pad_maximum_fusion.2.meta, f32[64,32,512]{2,1,0:T(8,128)S(1)} %copy-done.1, f32[64,32,512]{2,1,0:T(8,128)S(1)} %get-tuple-element.29.vs, f32[4,64,512]{2,1,0:T(8,128)S(1)} %get-tuple-element.20.urow, ...), custom_call_target="tpu_custom_call" | custom-call | flops 33554432 | bytes 16777216 | tf_op jit(solution)/shard_map/heat_step_one/pallas_call | solution.py:683
  74.8 0.0 collective-permute-done.4.got_lo
  74.8 0.0 collective-permute-done.5.got_hi
  74.8 11.6 %heat_step_two.1 = f32[64,32,512]{2,1,0:T(8,128)} custom-call(f32[6]{0:T(128)S(1)} %pad_maximum_fusion.2.meta, f32[64,32,512]{2,1,0:T(8,128)S(1)} %get-tuple-element.32.mid, f32[64,32,512]{2,1,0:T(8,128)S(1)} %get-tuple-element.29.vs, f32[2,64,512]{2,1,0:T(8,128)S(1)} %get-tuple-element.33.mpart, f32[1160,128]{1,0:T(8,128)S(1)} %collective-permute-done.2.recv_lo, ...), custom_call_target="tpu_custom_call" | custom-call | tf_op jit(solution)/shard_map/heat_step_two/pallas_call | solution.py:787
  (1 shorter events, 0.0 us)
Async XLA Ops:
  0.6 14.6 %copy-start.2 = (f32[3,16384]{1,0:T(4,128)S(1)}, f32[3,16384]{1,0:T(4,128)}, u32[]{:S(2)}) copy-start(f32[3,16384]{1,0:T(4,128)} %loc.1) | copy-start | bytes 589828
  0.6 14.6 %copy-start.3 = (f32[3,16384]{1,0:T(4,128)S(1)}, f32[3,16384]{1,0:T(4,128)}, u32[]{:S(2)}) copy-start(f32[3,16384]{1,0:T(4,128)} %vel.1) | copy-start | bytes 589828
  0.7 14.6 %copy-start.7 = (s32[256]{0:T(256)S(1)}, s32[256]{0:T(256)}, u32[]{:S(2)}) copy-start(s32[256]{0:T(256)} %tgt.1) | copy-start | bytes 3076
  0.7 14.6 %copy-start.8 = (s32[256]{0:T(256)S(1)}, s32[256]{0:T(256)}, u32[]{:S(2)}) copy-start(s32[256]{0:T(256)} %src.1) | copy-start | bytes 3076
  0.7 37.1 %copy-start.9 = (s32[2]{0:T(128)S(1)}, s32[2]{0:T(128)}, u32[]{:S(2)}) copy-start(s32[2]{0:T(128)} %param.19) | copy-start | bytes 28
  1.5 13.7 %collective-permute-start = (f32[6,256]{1,0:T(8,128)S(1)}, f32[6,256]{1,0:T(8,128)S(1)}, u32[]{:S(2)}, u32[]{:S(2)}) collective-permute-start(f32[6,256]{1,0:T(8,128)S(1)} %get-tuple-element.37), channel_id=1, source_target_pairs={{0,1},{1,2},{2,3},{3,4},{4,5},{5,6},{6,7},{7,8},{8,9},{9,10},{10,1... | collective-permute-start | bytes 18440 | tf_op jit(solution)/shard_map/ppermute | solution.py:807
  4.6 10.6 %collective-permute-start.1 = (f32[6,256]{1,0:T(8,128)S(1)}, f32[6,256]{1,0:T(8,128)S(1)}, u32[]{:S(2)}, u32[]{:S(2)}) collective-permute-start(f32[6,256]{1,0:T(8,128)S(1)} %get-tuple-element.36), channel_id=1, source_target_pairs={{1,0},{2,1},{3,2},{4,3},{5,4},{6,5},{7,6},{8,7},{9,8},{10,9},{11,1... | collective-permute-start | bytes 18440 | tf_op jit(solution)/shard_map/ppermute | solution.py:807
  11.1 2.2 %copy-start = (f32[64,32,512]{2,1,0:T(8,128)S(1)}, f32[64,32,512]{2,1,0:T(8,128)}, u32[]{:S(2)}) copy-start(f32[64,32,512]{2,1,0:T(8,128)} %us.1) | copy-start | bytes 12582916
  13.3 1.9 %copy-start.4 = (s32[3,16384]{1,0:T(4,128)S(1)}, s32[3,16384]{1,0:T(4,128)}, u32[]{:S(2)}) copy-start(s32[3,16384]{1,0:T(4,128)} %site.1) | copy-start | bytes 589828
  13.3 1.9 %copy-start.5 = (f32[16384]{0:T(1024)S(1)}, f32[16384]{0:T(1024)}, u32[]{:S(2)}) copy-start(f32[16384]{0:T(1024)} %param.12) | copy-start | bytes 196612
  13.3 2.0 %copy-start.6 = (s32[16384]{0:T(1024)S(1)}, s32[16384]{0:T(1024)}, u32[]{:S(2)}) copy-start(s32[16384]{0:T(1024)} %param.17) | copy-start | bytes 196612
  27.7 16.4 %collective-permute-start.2 = (f32[1160,128]{1,0:T(8,128)S(1)}, f32[1160,128]{1,0:T(8,128)S(1)}, u32[]{:S(2)}, u32[]{:S(2)}) collective-permute-start(f32[1160,128]{1,0:T(8,128)S(1)} %get-tuple-element.26), channel_id=1, source_target_pairs={{0,8},{8,16},{16,24},{24,32},{32,40},{40,48},{48,56},{56,64},{64,7... | collective-permute-start | bytes 1781768 | tf_op jit(solution)/shard_map/ppermute | solution.py:807
  35.8 11.2 %collective-permute-start.3 = (f32[1160,128]{1,0:T(8,128)S(1)}, f32[1160,128]{1,0:T(8,128)S(1)}, u32[]{:S(2)}, u32[]{:S(2)}) collective-permute-start(f32[1160,128]{1,0:T(8,128)S(1)} %get-tuple-element.27), channel_id=1, source_target_pairs={{8,0},{16,8},{24,16},{32,24},{40,32},{48,40},{56,48},{64,56},{72,6... | collective-permute-start | bytes 1781768 | tf_op jit(solution)/shard_map/ppermute | solution.py:807
  44.1 22.3 %copy-start.1 = (f32[64,32,512]{2,1,0:T(8,128)S(1)}, f32[64,32,512]{2,1,0:T(8,128)}, u32[]{:S(2)}) copy-start(f32[64,32,512]{2,1,0:T(8,128)} %us.1) | copy-start | bytes 12582916
  57.5 17.4 %collective-permute-start.4 = (f32[80,128]{1,0:T(8,128)S(1)}, f32[80,128]{1,0:T(8,128)S(1)}, u32[]{:S(2)}, u32[]{:S(2)}) collective-permute-start(f32[80,128]{1,0:T(8,128)S(1)} %get-tuple-element.35.pay_hi), channel_id=1, source_target_pairs={{0,1},{1,2},{2,3},{3,4},{4,5},{5,6},{6,7},{8,9},{9,10},{10,11},{11... | collective-permute-start | bytes 122888 | tf_op jit(solution)/shard_map/ppermute | solution.py:807
  59.4 15.4 %collective-permute-start.5 = (f32[80,128]{1,0:T(8,128)S(1)}, f32[80,128]{1,0:T(8,128)S(1)}, u32[]{:S(2)}, u32[]{:S(2)}) collective-permute-start(f32[80,128]{1,0:T(8,128)S(1)} %get-tuple-element.34.pay_lo), channel_id=1, source_target_pairs={{1,0},{2,1},{3,2},{4,3},{5,4},{6,5},{7,6},{9,8},{10,9},{11,10},{12... | collective-permute-start | bytes 122888 | tf_op jit(solution)/shard_map/ppermute | solution.py:807

commit v6 on v5

--- a/solution.py
+++ b/solution.py
@@ -27,7 +27,8 @@
 TILE_UNROLL = 32
 WALK_UNROLL = 32
 ROW_UNROLL = 16
-PLANES = 4
+PLANES = 8
+CHUNK = 8
 XW = CX + 4
 BINS = 2 * XW
 PART = 128 + 8 * DEPTH
@@ -36,6 +37,7 @@
 VSPEC = pl.BlockSpec(memory_space=pltpu.VMEM)
 SSPEC = pl.BlockSpec(memory_space=pltpu.SMEM)
 ASPEC = pl.BlockSpec(memory_space=pl.ANY)
+HSPEC = pl.BlockSpec(memory_space=pltpu.HBM)
 
 
 def iota(shape, dim):
@@ -128,7 +130,8 @@
 
 
 def walk(pile, cells, prof, count, bins, last_bin, first_bin, end_bin, origin, unroll):
-    spot = iota((BIN, 128), 0)
+    spot = iota((BIN, 128), 0).astype(F32).astype(BF16)
+    one, zero = jnp.ones((), BF16), jnp.zeros((), BF16)
     start = count_below(bins, float(first_bin))
     stop = jnp.minimum(count_below(bins, float(end_bin + 1)), count - 1)
     steps = stop - start + 1 + (end_bin - first_bin)
@@ -145,7 +148,9 @@
             i = jnp.where(more, i, jnp.minimum(i + 1, count))
         outs = []
         for ii, first, home in work:
-            hot = jnp.where(spot == cells(ii) - first, 1.0, 0.0).astype(BF16)
+            col = cells(ii) - first
+            col = jnp.where(jnp.logical_and(col >= 0, col < BIN), col, 300).astype(F32).astype(BF16)
+            hot = jnp.where(spot == col, one, zero)
             out = lax.dot_general(prof(ii), hot, (((1,), (1,)), ((), ())), preferred_element_type=F32)
             outs.append(out[:DEPTH] + out[DEPTH:])
         for (ii, first, home), out in zip(work, outs):
@@ -385,7 +390,7 @@
 
 def edge_deposit_kernel(
     meta, pile_in, recv_lo, recv_hi, ucol,
-    here, vrow, pay_lo, pay_hi,
+    share, vrow, pay_lo, pay_hi,
     pile, cells, prof, packs, last_v, last_s, sems,
 ):
     load = pltpu.make_async_copy(pile_in, pile, sems.at[0])
@@ -421,7 +426,7 @@
         )
 
     def turn(x):
-        return pltpu.make_async_copy(pile.at[x + HB], here.at[:, x, :], sems.at[2 + x])
+        return pltpu.make_async_copy(pile.at[x + HB], share.at[:, x, :], sems.at[2 + x])
 
     def turn_start(x, carry):
         turn(x).start()
@@ -482,7 +487,7 @@
             sd((80, 128), F32), sd((80, 128), F32),
         ),
         in_specs=[SSPEC, ASPEC] + [VSPEC] * 3,
-        out_specs=(VSPEC,) * 4,
+        out_specs=(HSPEC, VSPEC, VSPEC, VSPEC),
         scratch_shapes=[
             pltpu.VMEM((XW, DEPTH, CY), F32),
             pltpu.VMEM((2 * RECV, 128), I32),
@@ -564,15 +569,19 @@
     return [ref[z, :, tile(c)] for c in TILES]
 
 
-def heat_planes(src, dst, vs, kz, fz, row_f, col_f, fix, glow, after):
+def heat_planes(src, dst, vs, kz, fz, row_f, col_f, fix, glow, before, after):
     lane = iota((CX, 128), 1)
     sub = iota((CX, 128), 0)
+
+    def both(ref, z):
+        return pltpu.roll(ref[...], (128 - 2 * z) & 127, 1)
 
     def fetch(z):
         u = load(src, z)
         if fix is not None:
-            u[0] = jnp.where(lane == 0, pltpu.roll(fix[...], (128 - z) & 127, 1), u[0])
-            u[3] = jnp.where(lane == 127, pltpu.roll(fix[...], 63 - z, 1), u[3])
+            ends = both(fix, z)
+            u[0] = jnp.where(lane == 0, ends, u[0])
+            u[3] = jnp.where(lane == 127, ends, u[3])
         return u
 
     u0 = fetch(0)
@@ -601,12 +610,13 @@
             row_end = row_f[pl.ds(z + DEPTH, 1), :]
             ru = [pltpu.roll(u[c], 1, 1) for c in TILES]
             rk = [pltpu.roll(k[c], 1, 1) for c in TILES]
+            ends = None if col_f is None else both(col_f, z)
             g = []
             for c in TILES:
                 if c == 0:
                     f = flux(k[0], rk[0], ru[0], u[0])
                     if col_f is not None:
-                        f = jnp.where(lane == 0, pltpu.roll(col_f[...], (128 - z) & 127, 1), f)
+                        f = jnp.where(lane == 0, ends, f)
                 else:
                     pu = jnp.where(lane == 0, ru[c - 1], ru[c])
                     pk = jnp.where(lane == 0, rk[c - 1], rk[c])
@@ -617,7 +627,7 @@
                 if c < 3:
                     gn = jnp.where(lane == 127, rg[c + 1], rg[c])
                 elif col_f is not None:
-                    gn = jnp.where(lane == 127, pltpu.roll(col_f[...], 63 - z, 1), rg[c])
+                    gn = jnp.where(lane == 127, ends, rg[c])
                 else:
                     gn = rg[c]
                 f = flux(k[c], pltpu.roll(k[c], 1, 0), pltpu.roll(u[c], 1, 0), u[c])
@@ -633,6 +643,7 @@
     groups = DEPTH // PLANES
 
     def group(g, carry):
+        before(g)
         planes(g * PLANES, False)
         after(g)
         return carry
@@ -641,9 +652,13 @@
     planes(DEPTH - PLANES, True)
 
 
-def heat_one_kernel(meta, us, vs, urow, recv_lo, recv_hi, vrow, mid, mrow, share, kz, fz, row1, sem):
-    save = pltpu.make_async_copy(vs, share, sem.at[0])
-    save.start()
+def heat_one_kernel(meta, us, share, urow, recv_lo, recv_hi, vrow, mid, mrow, vs, kz, fz, row1, sems):
+    def bring(c):
+        at = pl.ds(pl.multiple_of(c * CHUNK, CHUNK), CHUNK)
+        return pltpu.make_async_copy(share.at[at], vs.at[at], sems.at[c])
+
+    for c in range(2):
+        bring(c).start()
     lane_w = iota((DEPTH, CY), 1)
     sub_w = iota((DEPTH, CY), 0)
     for n in range(2):
@@ -674,8 +689,21 @@
         mrow[n] = uh + total + gl * vh
         row1[DEPTH * n : DEPTH * n + DEPTH] = flux(kh, ki, uh, ui) if n == 0 else flux(ki, kh, ui, uh)
     glow = glow_of(iota((CX, 128), 0).astype(F32) + meta[0])
-    heat_planes(us, mid, vs, kz, fz, row1, None, None, glow, lambda g: None)
-    save.wait()
+
+    def before(g):
+        per = CHUNK // PLANES
+
+        @pl.when(lax.rem(g, per) == per - 1)
+        def _():
+            c = (g + 1) // per
+            bring(c).wait()
+
+            @pl.when(c + 1 < DEPTH // CHUNK)
+            def _():
+                bring(c + 1).start()
+
+    bring(0).wait()
+    heat_planes(us, mid, vs, kz, fz, row1, None, None, glow, before, lambda g: None)
 
 
 def heat_one(meta, u, v, urow, recv_lo, recv_hi, vrow):
@@ -683,12 +711,12 @@
     return pl.pallas_call(
         heat_one_kernel,
         out_shape=(sd((DEPTH, CX, CY), F32), sd((2, DEPTH, CY), F32), sd((DEPTH, CX, CY), F32)),
-        in_specs=[SSPEC] + [VSPEC] * 6,
-        out_specs=(VSPEC, VSPEC, ASPEC),
+        in_specs=[SSPEC, VSPEC, HSPEC] + [VSPEC] * 4,
+        out_specs=(VSPEC,) * 3,
         scratch_shapes=[
             pltpu.VMEM((CX, CY), F32), pltpu.VMEM((CX, CY), F32),
             pltpu.VMEM((2 * DEPTH, CY), F32),
-            pltpu.SemaphoreType.DMA((1,)),
+            pltpu.SemaphoreType.DMA((DEPTH // CHUNK,)),
         ],
         compiler_params=pltpu.CompilerParams(vmem_limit_bytes=VMEM_LIMIT),
         cost_estimate=pl.CostEstimate(flops=1 << 25, bytes_accessed=1 << 24, transcendentals=1 << 21),
@@ -735,8 +763,16 @@
     mid_out = column_step(outer, here, inner, stacks(got_lo, got_hi, CX, 8)) * side
     mid_in = column_step(here, inner, next_in, stacks(pay_lo, pay_hi, CX, 8))
     sign = jnp.where(lo_half, 1.0, -1.0)
-    fix[...] = mid_in
-    col2[...] = sign * flux(half_kappa(mid_out, here[1]), half_kappa(mid_in, inner[1]), mid_out, mid_in)
+    lane8 = iota((8, 128), 1)
+    source = ((lane8 + 1) >> 1) & (DEPTH - 1)
+    source = jnp.where((lane8 & 1) == 0, source, source + DEPTH)
+
+    def weave(ref, a):
+        for i in range(0, CX, 8):
+            ref[i : i + 8] = jnp.take_along_axis(a[i : i + 8], source, axis=1)
+
+    weave(fix, mid_in)
+    weave(col2, sign * flux(half_kappa(mid_out, here[1]), half_kappa(mid_in, inner[1]), mid_out, mid_in))
 
     tail = [jnp.transpose(jnp.concatenate([g[CX : CX + 8]] * 16, axis=0)) for g in (got_lo, got_hi)]
     ends = jnp.transpose(jnp.concatenate([mid_in] * 4, axis=0))
@@ -777,7 +813,7 @@
             store(g // per).start()
 
     glow = glow_of(sub.astype(F32) + meta[1])
-    heat_planes(mid, os, vs, kz, fz, row2, col2, fix, glow, after)
+    heat_planes(mid, os, vs, kz, fz, row2, col2, fix, glow, lambda g: None, after)
     store(DEPTH // 8 - 1).start()
     for c in range(DEPTH // 8):
         store(c).wait()
@@ -840,10 +876,10 @@
     recv_lo = shift(send_hi, "gx", 1)
     recv_hi = shift(send_lo, "gx", -1)
     pile = own_deposit(last.reshape(128), last, skey, schg)
-    here, vrow, pay_lo, pay_hi = edge_deposit(meta, pile, recv_lo, recv_hi, ucol)
+    share, vrow, pay_lo, pay_hi = edge_deposit(meta, pile, recv_lo, recv_hi, ucol)
     got_lo = shift(pay_hi, "gy", 1)
     got_hi = shift(pay_lo, "gy", -1)
-    mid, mpart, share = heat_one(meta, thermal_excess, here, urow, recv_lo, recv_hi, vrow)
+    mid, mpart, here = heat_one(meta, thermal_excess, pltpu.with_memory_space_constraint(share, pltpu.HBM), urow, recv_lo, recv_hi, vrow)
     final = heat_two(meta, mid, here, mpart, recv_lo, recv_hi, vrow, pay_lo, pay_hi, got_lo, got_hi)
     return nloc, nvel, share, final
 

time: 85.2 us -> 82.2 us (0.965)
  the two profiles are of different devices: /device:TPU:17 before, /device:TPU:15 now
where the time goes in v6:
time: 82.2 us; the launch traced here: 81.9 us
  Pallas kernels  47.6 us (58%)
  starting transfers between devices  23.9 us (29%)
  waiting for transfers between devices  5.46 us (7%)
  local copies, waits for them, and re-layouts  2.22 us (3%)
  between operations  1.72 us (2%)
  other arithmetic  1.03 us (1%)
    ppermute x6, starting transfers between devices, shift(): lax.ppermute(value, axis, [(i, i + steps) for i in range(first, stop)])  23.9 us
    pallas_call x1, Pallas kernels, particles(): pl.pallas_call(particle_kernel, out_shape=(sd((3, NPART), F32), sd((3, NP...  11.5 us
    pallas_call x1, Pallas kernels, heat_two(): pl.pallas_call(heat_two_kernel, out_shape=jax.ShapeDtypeStruct((DEPTH, CX...  10.4 us
    pallas_call x1, Pallas kernels, heat_one(): pl.pallas_call(heat_one_kernel, out_shape=(sd((DEPTH, CX, CY), F32), sd((...  9.93 us
    pallas_call x1, Pallas kernels, edge_deposit(): pl.pallas_call(edge_deposit_kernel, out_shape=(sd((DEPTH, CX, CY), F32),...  7.76 us
    pallas_call x1, Pallas kernels, own_deposit(): pl.pallas_call(own_deposit_kernel, out_shape=sd((XW, DEPTH, CY), F32), in...  6.15 us
    ppermute x6, waiting for transfers between devices, shift(): lax.ppermute(value, axis, [(i, i + steps) for i in range(first, stop)])  5.46 us
    unnamed x20, local copies, waits for them, and re-layouts  2.22 us
  transfers between devices with their start and end apart: 6, of which 1 were waited for; matrix products, arithmetic and copies ran while one was open for 0% of the time, Pallas kernels for 22%

profile of v6, /device:TPU:15, one launch (start us, length us, event | category | flops | bytes accessed | tf_op | source)
XLA Modules:
  0.0 81.9 jit_solution(18166462363181228982)
XLA Ops:
  0.6 0.0 copy-start.3
  0.6 0.0 copy-start.2
  0.7 0.0 copy-start.8
  0.7 0.0 copy-start.7
  0.7 0.0 copy-start.9
  0.7 0.8 pad_maximum_fusion
  1.5 2.4 %collective-permute-start.1 = (f32[6,256]{1,0:T(8,128)S(1)}, f32[6,256]{1,0:T(8,128)S(1)}, u32[]{:S(2)}, u32[]{:S(2)}) collective-permute-start(f32[6,256]{1,0:T(8,128)S(1)} %get-tuple-element.36), channel_id=1, source_target_pairs={{1,0},{2,1},{3,2},{4,3},{5,4},{6,5},{7,6},{8,7},{9,8},{10,9},{11,1... | collective-permute-start | bytes 18440 | tf_op jit(solution)/shard_map/ppermute | solution.py:843
  3.9 6.4 %collective-permute-start = (f32[6,256]{1,0:T(8,128)S(1)}, f32[6,256]{1,0:T(8,128)S(1)}, u32[]{:S(2)}, u32[]{:S(2)}) collective-permute-start(f32[6,256]{1,0:T(8,128)S(1)} %get-tuple-element.37), channel_id=1, source_target_pairs={{0,1},{1,2},{2,3},{3,4},{4,5},{5,6},{6,7},{7,8},{8,9},{9,10},{10,1... | collective-permute-start | bytes 18440 | tf_op jit(solution)/shard_map/ppermute | solution.py:843
  10.4 0.1 pad_add_fusion.origin
  11.1 0.0 copy-start
  11.1 2.2 %copy-done = f32[64,32,512]{2,1,0:T(8,128)S(1)} copy-done((f32[64,32,512]{2,1,0:T(8,128)S(1)}, f32[64,32,512]{2,1,0:T(8,128)}, u32[]{:S(2)}) %copy-start) | copy-done | bytes 4194328
  13.3 0.0 copy-start.4
  13.3 0.0 copy-start.5
  13.3 0.0 copy-start.6
  13.3 1.9 %temperature_edges.1 = (f32[4,64,512]{2,1,0:T(8,128)S(1)}, f32[4,32,128]{2,1,0:T(8,128)S(1)}) custom-call(f32[64,32,512]{2,1,0:T(8,128)S(1)} %copy-done), custom_call_target="tpu_custom_call" | custom-call | tf_op jit(solution)/shard_map/temperature_edges/pallas_call | solution.py:533
  15.2 0.0 collective-permute-done.1.halo_hi
  15.2 0.0 collective-permute-done.halo_lo
  15.2 0.0 copy-done.3
  15.2 0.0 copy-done.2
  15.2 0.0 copy-done.8
  15.2 0.0 copy-done.7
  15.2 0.0 copy-done.4
  15.3 0.0 copy-done.5
  15.3 0.0 copy-done.6
  15.3 11.5 %particle_step.1 = (f32[3,16384]{1,0:T(4,128)}, f32[3,16384]{1,0:T(4,128)}, s32[128,128]{1,0:T(8,128)S(1)}, f32[128,128]{1,0:T(8,128)S(1)}, s32[1,128]{1,0:T(1,1...) custom-call(s32[256]{0:T(256)S(1)} %copy-done.7, s32[256]{0:T(256)S(1)} %copy-done.8, s32[1]{0:T(128)S(6)} %copy.14.cnt, ...), custom_call_target="tpu_custom_call" | custom-call | tf_op jit(solution)/shard_map/particle_step/pallas_call | solution.py:324
  26.8 3.8 %collective-permute-start.2 = (f32[1160,128]{1,0:T(8,128)S(1)}, f32[1160,128]{1,0:T(8,128)S(1)}, u32[]{:S(2)}, u32[]{:S(2)}) collective-permute-start(f32[1160,128]{1,0:T(8,128)S(1)} %get-tuple-element.26), channel_id=1, source_target_pairs={{0,8},{8,16},{16,24},{24,32},{32,40},{40,48},{48,56},{56,64},{64,7... | collective-permute-start | bytes 1781768 | tf_op jit(solution)/shard_map/ppermute | solution.py:843
  30.6 2.1 %collective-permute-start.3 = (f32[1160,128]{1,0:T(8,128)S(1)}, f32[1160,128]{1,0:T(8,128)S(1)}, u32[]{:S(2)}, u32[]{:S(2)}) collective-permute-start(f32[1160,128]{1,0:T(8,128)S(1)} %get-tuple-element.27), channel_id=1, source_target_pairs={{8,0},{16,8},{24,16},{32,24},{40,32},{48,40},{56,48},{64,56},{72,6... | collective-permute-start | bytes 1781768 | tf_op jit(solution)/shard_map/ppermute | solution.py:843
  32.8 0.1 add_convert_fusion
  32.8 0.0 copy-done.9
  32.8 0.1 pad_maximum_fusion.2.meta
  32.9 6.1 %own_deposit.1.pile_in = f32[36,64,512]{2,1,0:T(8,128)S(1)} custom-call(s32[128]{0:T(128)S(1)} %bitcast.11, s32[1,128]{1,0:T(1,128)S(1)} %get-tuple-element.23.last_v, s32[128,128]{1,0:T(8,128)S(1)} %get-tuple-element.24.skey, f32[128,128]{1,0:T(8,128)S(1)} %get-tuple-element.25.schg), custom_call_target="tpu_custom_call" | custom-call | tf_op jit(solution)/shard_map/own_deposit/pallas_call | solution.py:377
  39.1 0.0 copy-start.1
  39.1 0.0 collective-permute-done.2.recv_lo
  39.1 5.4 %collective-permute-done.3.recv_hi = f32[1160,128]{1,0:T(8,128)S(1)} collective-permute-done((f32[1160,128]{1,0:T(8,128)S(1)}, f32[1160,128]{1,0:T(8,128)S(1)}, u32[]{:S(2)}, u32[]{:S(2)}) %collective-permute-start.3) | collective-permute-done | bytes 593952 | tf_op jit(solution)/shard_map/ppermute | solution.py:843
  44.5 7.8 %edge_deposit.1 = (f32[64,32,512]{2,1,0:T(8,128)}, f32[6,64,512]{2,1,0:T(8,128)S(1)}, f32[80,128]{1,0:T(8,128)S(1)}, f32[80,128]{1,0:T(8,128)S(1)}) custom-call(f32[6]{0:T(128)S(1)} %pad_maximum_fusion.2.meta, f32[36,64,512]{2,1,0:T(8,128)S(1)} %own_deposit.1.pile_in, f32[1160,128]{1,0:T(8,128)S(1)} %collective-permute-done.2.recv_lo, ...), custom_call_target="tpu_custom_call" | custom-call | tf_op jit(solution)/shard_map/edge_deposit/pallas_call | solution.py:483
  52.3 1.9 %collective-permute-start.5 = (f32[80,128]{1,0:T(8,128)S(1)}, f32[80,128]{1,0:T(8,128)S(1)}, u32[]{:S(2)}, u32[]{:S(2)}) collective-permute-start(f32[80,128]{1,0:T(8,128)S(1)} %get-tuple-element.34.pay_lo), channel_id=1, source_target_pairs={{1,0},{2,1},{3,2},{4,3},{5,4},{6,5},{7,6},{9,8},{10,9},{11,10},{12... | collective-permute-start | bytes 122888 | tf_op jit(solution)/shard_map/ppermute | solution.py:843
  54.2 7.2 %collective-permute-start.4 = (f32[80,128]{1,0:T(8,128)S(1)}, f32[80,128]{1,0:T(8,128)S(1)}, u32[]{:S(2)}, u32[]{:S(2)}) collective-permute-start(f32[80,128]{1,0:T(8,128)S(1)} %get-tuple-element.35.pay_hi), channel_id=1, source_target_pairs={{0,1},{1,2},{2,3},{3,4},{4,5},{5,6},{6,7},{8,9},{9,10},{10,11},{11... | collective-permute-start | bytes 122888 | tf_op jit(solution)/shard_map/ppermute | solution.py:843
  61.4 0.0 copy-done.1
  61.4 9.9 %heat_step_one.1 = (f32[64,32,512]{2,1,0:T(8,128)S(1)}, f32[2,64,512]{2,1,0:T(8,128)S(1)}, f32[64,32,512]{2,1,0:T(8,128)S(1)}) custom-call(f32[6]{0:T(128)S(1)} %pad_maximum_fusion.2.meta, f32[64,32,512]{2,1,0:T(8,128)S(1)} %copy-done.1, f32[64,32,512]{2,1,0:T(8,128)} %get-tuple-element.18.share, f32[4,64,512]{2,1,0:T(8,128)S(1)} %get-tuple-element.20.urow, ...), custom_call_target="tpu_custom_call" | custom-call | flops 33554432 | bytes 16777216 | tf_op jit(solution)/shard_map/heat_step_one/pallas_call | solution.py:711
  71.3 0.0 collective-permute-done.5.got_hi
  71.4 0.0 collective-permute-done.4.got_lo
  71.4 10.4 %heat_step_two.1 = f32[64,32,512]{2,1,0:T(8,128)} custom-call(f32[6]{0:T(128)S(1)} %pad_maximum_fusion.2.meta, f32[64,32,512]{2,1,0:T(8,128)S(1)} %get-tuple-element.31.mid, f32[64,32,512]{2,1,0:T(8,128)S(1)} %get-tuple-element.32.vs, f32[2,64,512]{2,1,0:T(8,128)S(1)} %get-tuple-element.33.mpart, f32[1160,128]{1,0:T(8,128)S(1)} %collective-permute-done.2.recv_lo, ...), custom_call_target="tpu_custom_call" | custom-call | tf_op jit(solution)/shard_map/heat_step_two/pallas_call | solution.py:823
  (1 shorter events, 0.0 us)
Async XLA Ops:
  0.6 14.6 %copy-start.3 = (f32[3,16384]{1,0:T(4,128)S(1)}, f32[3,16384]{1,0:T(4,128)}, u32[]{:S(2)}) copy-start(f32[3,16384]{1,0:T(4,128)} %vel.1) | copy-start | bytes 589828
  0.6 14.6 %copy-start.2 = (f32[3,16384]{1,0:T(4,128)S(1)}, f32[3,16384]{1,0:T(4,128)}, u32[]{:S(2)}) copy-start(f32[3,16384]{1,0:T(4,128)} %loc.1) | copy-start | bytes 589828
  0.7 14.6 %copy-start.8 = (s32[256]{0:T(256)S(1)}, s32[256]{0:T(256)}, u32[]{:S(2)}) copy-start(s32[256]{0:T(256)} %src.1) | copy-start | bytes 3076
  0.7 14.6 %copy-start.7 = (s32[256]{0:T(256)S(1)}, s32[256]{0:T(256)}, u32[]{:S(2)}) copy-start(s32[256]{0:T(256)} %tgt.1) | copy-start | bytes 3076
  0.7 32.2 %copy-start.9 = (s32[2]{0:T(128)S(1)}, s32[2]{0:T(128)}, u32[]{:S(2)}) copy-start(s32[2]{0:T(128)} %param.19) | copy-start | bytes 28
  1.5 13.7 %collective-permute-start.1 = (f32[6,256]{1,0:T(8,128)S(1)}, f32[6,256]{1,0:T(8,128)S(1)}, u32[]{:S(2)}, u32[]{:S(2)}) collective-permute-start(f32[6,256]{1,0:T(8,128)S(1)} %get-tuple-element.36), channel_id=1, source_target_pairs={{1,0},{2,1},{3,2},{4,3},{5,4},{6,5},{7,6},{8,7},{9,8},{10,9},{11,1... | collective-permute-start | bytes 18440 | tf_op jit(solution)/shard_map/ppermute | solution.py:843
  3.9 11.3 %collective-permute-start = (f32[6,256]{1,0:T(8,128)S(1)}, f32[6,256]{1,0:T(8,128)S(1)}, u32[]{:S(2)}, u32[]{:S(2)}) collective-permute-start(f32[6,256]{1,0:T(8,128)S(1)} %get-tuple-element.37), channel_id=1, source_target_pairs={{0,1},{1,2},{2,3},{3,4},{4,5},{5,6},{6,7},{7,8},{8,9},{9,10},{10,1... | collective-permute-start | bytes 18440 | tf_op jit(solution)/shard_map/ppermute | solution.py:843
  11.1 2.2 %copy-start = (f32[64,32,512]{2,1,0:T(8,128)S(1)}, f32[64,32,512]{2,1,0:T(8,128)}, u32[]{:S(2)}) copy-start(f32[64,32,512]{2,1,0:T(8,128)} %us.1) | copy-start | bytes 12582916
  13.3 1.9 %copy-start.4 = (s32[3,16384]{1,0:T(4,128)S(1)}, s32[3,16384]{1,0:T(4,128)}, u32[]{:S(2)}) copy-start(s32[3,16384]{1,0:T(4,128)} %site.1) | copy-start | bytes 589828
  13.3 1.9 %copy-start.5 = (f32[16384]{0:T(1024)S(1)}, f32[16384]{0:T(1024)}, u32[]{:S(2)}) copy-start(f32[16384]{0:T(1024)} %param.12) | copy-start | bytes 196612
  13.3 2.0 %copy-start.6 = (s32[16384]{0:T(1024)S(1)}, s32[16384]{0:T(1024)}, u32[]{:S(2)}) copy-start(s32[16384]{0:T(1024)} %param.17) | copy-start | bytes 196612
  26.8 12.3 %collective-permute-start.2 = (f32[1160,128]{1,0:T(8,128)S(1)}, f32[1160,128]{1,0:T(8,128)S(1)}, u32[]{:S(2)}, u32[]{:S(2)}) collective-permute-start(f32[1160,128]{1,0:T(8,128)S(1)} %get-tuple-element.26), channel_id=1, source_target_pairs={{0,8},{8,16},{16,24},{24,32},{32,40},{40,48},{48,56},{56,64},{64,7... | collective-permute-start | bytes 1781768 | tf_op jit(solution)/shard_map/ppermute | solution.py:843
  30.6 13.9 %collective-permute-start.3 = (f32[1160,128]{1,0:T(8,128)S(1)}, f32[1160,128]{1,0:T(8,128)S(1)}, u32[]{:S(2)}, u32[]{:S(2)}) collective-permute-start(f32[1160,128]{1,0:T(8,128)S(1)} %get-tuple-element.27), channel_id=1, source_target_pairs={{8,0},{16,8},{24,16},{32,24},{40,32},{48,40},{56,48},{64,56},{72,6... | collective-permute-start | bytes 1781768 | tf_op jit(solution)/shard_map/ppermute | solution.py:843
  39.1 22.3 %copy-start.1 = (f32[64,32,512]{2,1,0:T(8,128)S(1)}, f32[64,32,512]{2,1,0:T(8,128)}, u32[]{:S(2)}) copy-start(f32[64,32,512]{2,1,0:T(8,128)} %us.1) | copy-start | bytes 12582916
  52.3 19.0 %collective-permute-start.5 = (f32[80,128]{1,0:T(8,128)S(1)}, f32[80,128]{1,0:T(8,128)S(1)}, u32[]{:S(2)}, u32[]{:S(2)}) collective-permute-start(f32[80,128]{1,0:T(8,128)S(1)} %get-tuple-element.34.pay_lo), channel_id=1, source_target_pairs={{1,0},{2,1},{3,2},{4,3},{5,4},{6,5},{7,6},{9,8},{10,9},{11,10},{12... | collective-permute-start | bytes 122888 | tf_op jit(solution)/shard_map/ppermute | solution.py:843
  54.2 17.1 %collective-permute-start.4 = (f32[80,128]{1,0:T(8,128)S(1)}, f32[80,128]{1,0:T(8,128)S(1)}, u32[]{:S(2)}, u32[]{:S(2)}) collective-permute-start(f32[80,128]{1,0:T(8,128)S(1)} %get-tuple-element.35.pay_hi), channel_id=1, source_target_pairs={{0,1},{1,2},{2,3},{3,4},{4,5},{5,6},{6,7},{8,9},{9,10},{10,11},{11... | collective-permute-start | bytes 122888 | tf_op jit(solution)/shard_map/ppermute | solution.py:843

commit v7 on v6

--- a/solution.py
+++ b/solution.py
@@ -24,11 +24,12 @@
 BIN = 256
 LOG2E = 1.4426950408889634
 VMEM_LIMIT = 30 * 1024 * 1024
-TILE_UNROLL = 32
+TILE_UNROLL = 64
 WALK_UNROLL = 32
 ROW_UNROLL = 16
 PLANES = 8
 CHUNK = 8
+AHEAD = 5
 XW = CX + 4
 BINS = 2 * XW
 PART = 128 + 8 * DEPTH
@@ -504,20 +505,24 @@
 
 def edges_kernel(cells, urow, ucol, left, right, sems):
     rows = [
-        pltpu.make_async_copy(cells.at[:, x, :], urow.at[r], sems.at[2 + r])
+        pltpu.make_async_copy(cells.at[:, x, :], urow.at[r], sems.at[r])
         for r, x in enumerate((0, 1, CX - 2, CX - 1))
     ]
     cols = [
-        pltpu.make_async_copy(cells.at[:, :, pl.ds(at, 128)], ref, sems.at[n])
+        pltpu.make_async_copy(
+            cells.at[pl.ds(z, 16), :, pl.ds(at, 128)], ref.at[pl.ds(z, 16)], sems.at[4 + n + z // 8]
+        )
+        for z in range(0, DEPTH, 16)
         for n, (ref, at) in enumerate(((left, 0), (right, CY - 128)))
     ]
     for copy in cols + rows:
         copy.start()
-    for copy in cols:
-        copy.wait()
     lane = iota((CX, 128), 1)
     acc = [jnp.zeros((CX, 128), F32)] * 4
     for z in range(DEPTH):
+        if z % 16 == 0:
+            for copy in cols[z // 8 : z // 8 + 2]:
+                copy.wait()
         for n, (ref, by) in enumerate(((left, z), (left, z + 127), (right, z + 2), (right, z + 1))):
             by = by & 127
             a = ref[z] if by == 0 else pltpu.roll(ref[z], by, 1)
@@ -538,7 +543,7 @@
         scratch_shapes=[
             pltpu.VMEM((DEPTH, CX, 128), F32),
             pltpu.VMEM((DEPTH, CX, 128), F32),
-            pltpu.SemaphoreType.DMA((6,)),
+            pltpu.SemaphoreType.DMA((12,)),
         ],
         compiler_params=pltpu.CompilerParams(vmem_limit_bytes=VMEM_LIMIT),
         name="temperature_edges",
@@ -657,7 +662,7 @@
         at = pl.ds(pl.multiple_of(c * CHUNK, CHUNK), CHUNK)
         return pltpu.make_async_copy(share.at[at], vs.at[at], sems.at[c])
 
-    for c in range(2):
+    for c in range(AHEAD):
         bring(c).start()
     lane_w = iota((DEPTH, CY), 1)
     sub_w = iota((DEPTH, CY), 0)
@@ -698,9 +703,9 @@
             c = (g + 1) // per
             bring(c).wait()
 
-            @pl.when(c + 1 < DEPTH // CHUNK)
+            @pl.when(c + AHEAD - 1 < DEPTH // CHUNK)
             def _():
-                bring(c + 1).start()
+                bring(c + AHEAD - 1).start()
 
     bring(0).wait()
     heat_planes(us, mid, vs, kz, fz, row1, None, None, glow, before, lambda g: None)
@@ -859,7 +864,7 @@
     width = HB * 128
     halo_lo = shift(states[:, NPART - width :], ("gx", "gy"), 1)
     halo_hi = shift(states[:, :width], ("gx", "gy"), -1)
-    urow, ucol = edges(thermal_excess)
+    urow, ucol = edges(pltpu.with_memory_space_constraint(thermal_excess, pltpu.HBM))
 
     gx, gy = lax.axis_index("gx"), lax.axis_index("gy")
     row_start, col_start = gx * CX, gy * CY

time: 82.2 us -> 79.5 us (0.967)
  the two profiles are of different devices: /device:TPU:15 before, /device:TPU:97 now
where the time goes in v7:
time: 79.5 us; the launch traced here: 78.5 us
  Pallas kernels  48.5 us (61%)
  starting transfers between devices  19.3 us (24%)
  waiting for transfers between devices  7.97 us (10%)
  between operations  1.7 us (2%)
  other arithmetic  1.02 us (1%)
    ppermute x6, starting transfers between devices, shift(): lax.ppermute(value, axis, [(i, i + steps) for i in range(first, stop)])  19.3 us
    pallas_call x1, Pallas kernels, particles(): pl.pallas_call(particle_kernel, out_shape=(sd((3, NPART), F32), sd((3, NP...  11.8 us
    pallas_call x1, Pallas kernels, heat_two(): pl.pallas_call(heat_two_kernel, out_shape=jax.ShapeDtypeStruct((DEPTH, CX...  10.4 us
    pallas_call x1, Pallas kernels, heat_one(): pl.pallas_call(heat_one_kernel, out_shape=(sd((DEPTH, CX, CY), F32), sd((...  9.22 us
    ppermute x6, waiting for transfers between devices, shift(): lax.ppermute(value, axis, [(i, i + steps) for i in range(first, stop)])  7.97 us
    pallas_call x1, Pallas kernels, edge_deposit(): pl.pallas_call(edge_deposit_kernel, out_shape=(sd((DEPTH, CX, CY), F32),...  7.77 us
    pallas_call x1, Pallas kernels, own_deposit(): pl.pallas_call(own_deposit_kernel, out_shape=sd((XW, DEPTH, CY), F32), in...  6.88 us
    pallas_call x1, Pallas kernels, edges(): pl.pallas_call(edges_kernel, out_shape=(sd((4, DEPTH, CY), F32), sd((4, C...  2.49 us
  transfers between devices with their start and end apart: 6, of which 2 were waited for; matrix products, arithmetic and copies ran while one was open for 0% of the time, Pallas kernels for 24%

profile of v7, /device:TPU:97, one launch (start us, length us, event | category | flops | bytes accessed | tf_op | source)
XLA Modules:
  0.0 78.5 jit_solution(3864443819077203315)
XLA Ops:
  0.6 0.0 copy-start.2
  0.6 0.0 copy-start.1
  0.7 0.0 copy-start.5
  0.7 0.0 copy-start.3
  0.7 0.0 copy-start.7
  0.7 0.0 copy-start.6
  0.7 0.0 copy-start.4
  0.7 0.0 copy-start.8
  0.7 0.8 pad_maximum_fusion
  1.5 7.6 %collective-permute-start.1 = (f32[6,256]{1,0:T(8,128)S(1)}, f32[6,256]{1,0:T(8,128)S(1)}, u32[]{:S(2)}, u32[]{:S(2)}) collective-permute-start(f32[6,256]{1,0:T(8,128)S(1)} %get-tuple-element.36), channel_id=1, source_target_pairs={{1,0},{2,1},{3,2},{4,3},{5,4},{6,5},{7,6},{8,7},{9,8},{10,9},{11,1... | collective-permute-start | bytes 18440 | tf_op jit(solution)/shard_map/ppermute | solution.py:848
  9.1 1.9 %collective-permute-start = (f32[6,256]{1,0:T(8,128)S(1)}, f32[6,256]{1,0:T(8,128)S(1)}, u32[]{:S(2)}, u32[]{:S(2)}) collective-permute-start(f32[6,256]{1,0:T(8,128)S(1)} %get-tuple-element.37), channel_id=1, source_target_pairs={{0,1},{1,2},{2,3},{3,4},{4,5},{5,6},{6,7},{7,8},{8,9},{9,10},{10,1... | collective-permute-start | bytes 18440 | tf_op jit(solution)/shard_map/ppermute | solution.py:848
  11.0 0.1 pad_add_fusion.origin
  11.7 2.5 %temperature_edges.1 = (f32[4,64,512]{2,1,0:T(8,128)S(1)}, f32[4,32,128]{2,1,0:T(8,128)S(1)}) custom-call(f32[64,32,512]{2,1,0:T(8,128)} %us.1), custom_call_target="tpu_custom_call" | custom-call | tf_op jit(solution)/shard_map/temperature_edges/pallas_call | solution.py:538
  14.2 0.0 collective-permute-done.1.halo_hi
  14.3 3.6 %collective-permute-done.halo_lo = f32[6,256]{1,0:T(8,128)S(1)} collective-permute-done((f32[6,256]{1,0:T(8,128)S(1)}, f32[6,256]{1,0:T(8,128)S(1)}, u32[]{:S(2)}, u32[]{:S(2)}) %collective-permute-start) | collective-permute-done | bytes 6176 | tf_op jit(solution)/shard_map/ppermute | solution.py:848
  17.9 0.0 copy-done.2
  17.9 0.0 copy-done.1
  17.9 0.0 copy-done.5
  17.9 0.0 copy-done.3
  17.9 0.0 copy-done.7
  17.9 0.0 copy-done.6
  17.9 0.0 copy-done.4
  17.9 11.8 %particle_step.1 = (f32[3,16384]{1,0:T(4,128)}, f32[3,16384]{1,0:T(4,128)}, s32[128,128]{1,0:T(8,128)S(1)}, f32[128,128]{1,0:T(8,128)S(1)}, s32[1,128]{1,0:T(1,1...) custom-call(s32[256]{0:T(256)S(1)} %copy-done.6, s32[256]{0:T(256)S(1)} %copy-done.7, s32[1]{0:T(128)S(6)} %copy.14.cnt, ...), custom_call_target="tpu_custom_call" | custom-call | tf_op jit(solution)/shard_map/particle_step/pallas_call | solution.py:325
  29.7 2.4 %collective-permute-start.2 = (f32[1160,128]{1,0:T(8,128)S(1)}, f32[1160,128]{1,0:T(8,128)S(1)}, u32[]{:S(2)}, u32[]{:S(2)}) collective-permute-start(f32[1160,128]{1,0:T(8,128)S(1)} %get-tuple-element.26), channel_id=1, source_target_pairs={{0,8},{8,16},{16,24},{24,32},{32,40},{40,48},{48,56},{56,64},{64,7... | collective-permute-start | bytes 1781768 | tf_op jit(solution)/shard_map/ppermute | solution.py:848
  32.1 1.9 %collective-permute-start.3 = (f32[1160,128]{1,0:T(8,128)S(1)}, f32[1160,128]{1,0:T(8,128)S(1)}, u32[]{:S(2)}, u32[]{:S(2)}) collective-permute-start(f32[1160,128]{1,0:T(8,128)S(1)} %get-tuple-element.27), channel_id=1, source_target_pairs={{8,0},{16,8},{24,16},{32,24},{40,32},{48,40},{56,48},{64,56},{72,6... | collective-permute-start | bytes 1781768 | tf_op jit(solution)/shard_map/ppermute | solution.py:848
  34.1 0.1 add_convert_fusion
  34.1 0.0 copy-done.8
  34.1 0.1 pad_maximum_fusion.2.meta
  34.2 6.9 %own_deposit.1.pile_in = f32[36,64,512]{2,1,0:T(8,128)S(1)} custom-call(s32[128]{0:T(128)S(1)} %bitcast.11, s32[1,128]{1,0:T(1,128)S(1)} %get-tuple-element.23.last_v, s32[128,128]{1,0:T(8,128)S(1)} %get-tuple-element.24.skey, f32[128,128]{1,0:T(8,128)S(1)} %get-tuple-element.25.schg), custom_call_target="tpu_custom_call" | custom-call | tf_op jit(solution)/shard_map/own_deposit/pallas_call | solution.py:378
  41.1 0.0 copy-start
  41.1 0.0 collective-permute-done.2.recv_lo
  41.1 4.3 %collective-permute-done.3.recv_hi = f32[1160,128]{1,0:T(8,128)S(1)} collective-permute-done((f32[1160,128]{1,0:T(8,128)S(1)}, f32[1160,128]{1,0:T(8,128)S(1)}, u32[]{:S(2)}, u32[]{:S(2)}) %collective-permute-start.3) | collective-permute-done | bytes 593952 | tf_op jit(solution)/shard_map/ppermute | solution.py:848
  45.5 7.8 %edge_deposit.1 = (f32[64,32,512]{2,1,0:T(8,128)}, f32[6,64,512]{2,1,0:T(8,128)S(1)}, f32[80,128]{1,0:T(8,128)S(1)}, f32[80,128]{1,0:T(8,128)S(1)}) custom-call(f32[6]{0:T(128)S(1)} %pad_maximum_fusion.2.meta, f32[36,64,512]{2,1,0:T(8,128)S(1)} %own_deposit.1.pile_in, f32[1160,128]{1,0:T(8,128)S(1)} %collective-permute-done.2.recv_lo, ...), custom_call_target="tpu_custom_call" | custom-call | tf_op jit(solution)/shard_map/edge_deposit/pallas_call | solution.py:484
  53.2 1.3 %collective-permute-start.5 = (f32[80,128]{1,0:T(8,128)S(1)}, f32[80,128]{1,0:T(8,128)S(1)}, u32[]{:S(2)}, u32[]{:S(2)}) collective-permute-start(f32[80,128]{1,0:T(8,128)S(1)} %get-tuple-element.34.pay_lo), channel_id=1, source_target_pairs={{1,0},{2,1},{3,2},{4,3},{5,4},{6,5},{7,6},{9,8},{10,9},{11,10},{12... | collective-permute-start | bytes 122888 | tf_op jit(solution)/shard_map/ppermute | solution.py:848
  54.5 4.2 %collective-permute-start.4 = (f32[80,128]{1,0:T(8,128)S(1)}, f32[80,128]{1,0:T(8,128)S(1)}, u32[]{:S(2)}, u32[]{:S(2)}) collective-permute-start(f32[80,128]{1,0:T(8,128)S(1)} %get-tuple-element.35.pay_hi), channel_id=1, source_target_pairs={{0,1},{1,2},{2,3},{3,4},{4,5},{5,6},{6,7},{8,9},{9,10},{10,11},{11... | collective-permute-start | bytes 122888 | tf_op jit(solution)/shard_map/ppermute | solution.py:848
  58.7 0.0 copy-done
  58.7 9.2 %heat_step_one.1 = (f32[64,32,512]{2,1,0:T(8,128)S(1)}, f32[2,64,512]{2,1,0:T(8,128)S(1)}, f32[64,32,512]{2,1,0:T(8,128)S(1)}) custom-call(f32[6]{0:T(128)S(1)} %pad_maximum_fusion.2.meta, f32[64,32,512]{2,1,0:T(8,128)S(1)} %copy-done, f32[64,32,512]{2,1,0:T(8,128)} %get-tuple-element.18.share, f32[4,64,512]{2,1,0:T(8,128)S(1)} %get-tuple-element.20.urow, ...), custom_call_target="tpu_custom_call" | custom-call | flops 33554432 | bytes 16777216 | tf_op jit(solution)/shard_map/heat_step_one/pallas_call | solution.py:716
  67.9 0.0 collective-permute-done.5.got_hi
  68.0 0.0 collective-permute-done.4.got_lo
  68.0 10.4 %heat_step_two.1 = f32[64,32,512]{2,1,0:T(8,128)} custom-call(f32[6]{0:T(128)S(1)} %pad_maximum_fusion.2.meta, f32[64,32,512]{2,1,0:T(8,128)S(1)} %get-tuple-element.31.mid, f32[64,32,512]{2,1,0:T(8,128)S(1)} %get-tuple-element.32.vs, f32[2,64,512]{2,1,0:T(8,128)S(1)} %get-tuple-element.33.mpart, f32[1160,128]{1,0:T(8,128)S(1)} %collective-permute-done.2.recv_lo, ...), custom_call_target="tpu_custom_call" | custom-call | tf_op jit(solution)/shard_map/heat_step_two/pallas_call | solution.py:828
  (1 shorter events, 0.0 us)
Async XLA Ops:
  0.6 17.3 %copy-start.2 = (f32[3,16384]{1,0:T(4,128)S(1)}, f32[3,16384]{1,0:T(4,128)}, u32[]{:S(2)}) copy-start(f32[3,16384]{1,0:T(4,128)} %vel.1) | copy-start | bytes 589828
  0.6 17.3 %copy-start.1 = (f32[3,16384]{1,0:T(4,128)S(1)}, f32[3,16384]{1,0:T(4,128)}, u32[]{:S(2)}) copy-start(f32[3,16384]{1,0:T(4,128)} %loc.1) | copy-start | bytes 589828
  0.7 17.2 %copy-start.5 = (s32[16384]{0:T(1024)S(1)}, s32[16384]{0:T(1024)}, u32[]{:S(2)}) copy-start(s32[16384]{0:T(1024)} %param.17) | copy-start | bytes 196612
  0.7 17.2 %copy-start.3 = (s32[3,16384]{1,0:T(4,128)S(1)}, s32[3,16384]{1,0:T(4,128)}, u32[]{:S(2)}) copy-start(s32[3,16384]{1,0:T(4,128)} %site.1) | copy-start | bytes 589828
  0.7 17.2 %copy-start.7 = (s32[256]{0:T(256)S(1)}, s32[256]{0:T(256)}, u32[]{:S(2)}) copy-start(s32[256]{0:T(256)} %src.1) | copy-start | bytes 3076
  0.7 17.2 %copy-start.6 = (s32[256]{0:T(256)S(1)}, s32[256]{0:T(256)}, u32[]{:S(2)}) copy-start(s32[256]{0:T(256)} %tgt.1) | copy-start | bytes 3076
  0.7 17.2 %copy-start.4 = (f32[16384]{0:T(1024)S(1)}, f32[16384]{0:T(1024)}, u32[]{:S(2)}) copy-start(f32[16384]{0:T(1024)} %param.12) | copy-start | bytes 196612
  0.7 33.4 %copy-start.8 = (s32[2]{0:T(128)S(1)}, s32[2]{0:T(128)}, u32[]{:S(2)}) copy-start(s32[2]{0:T(128)} %param.19) | copy-start | bytes 28
  1.5 12.8 %collective-permute-start.1 = (f32[6,256]{1,0:T(8,128)S(1)}, f32[6,256]{1,0:T(8,128)S(1)}, u32[]{:S(2)}, u32[]{:S(2)}) collective-permute-start(f32[6,256]{1,0:T(8,128)S(1)} %get-tuple-element.36), channel_id=1, source_target_pairs={{1,0},{2,1},{3,2},{4,3},{5,4},{6,5},{7,6},{8,7},{9,8},{10,9},{11,1... | collective-permute-start | bytes 18440 | tf_op jit(solution)/shard_map/ppermute | solution.py:848
  9.1 8.8 %collective-permute-start = (f32[6,256]{1,0:T(8,128)S(1)}, f32[6,256]{1,0:T(8,128)S(1)}, u32[]{:S(2)}, u32[]{:S(2)}) collective-permute-start(f32[6,256]{1,0:T(8,128)S(1)} %get-tuple-element.37), channel_id=1, source_target_pairs={{0,1},{1,2},{2,3},{3,4},{4,5},{5,6},{6,7},{7,8},{8,9},{9,10},{10,1... | collective-permute-start | bytes 18440 | tf_op jit(solution)/shard_map/ppermute | solution.py:848
  29.7 11.4 %collective-permute-start.2 = (f32[1160,128]{1,0:T(8,128)S(1)}, f32[1160,128]{1,0:T(8,128)S(1)}, u32[]{:S(2)}, u32[]{:S(2)}) collective-permute-start(f32[1160,128]{1,0:T(8,128)S(1)} %get-tuple-element.26), channel_id=1, source_target_pairs={{0,8},{8,16},{16,24},{24,32},{32,40},{40,48},{48,56},{56,64},{64,7... | collective-permute-start | bytes 1781768 | tf_op jit(solution)/shard_map/ppermute | solution.py:848
  32.1 13.4 %collective-permute-start.3 = (f32[1160,128]{1,0:T(8,128)S(1)}, f32[1160,128]{1,0:T(8,128)S(1)}, u32[]{:S(2)}, u32[]{:S(2)}) collective-permute-start(f32[1160,128]{1,0:T(8,128)S(1)} %get-tuple-element.27), channel_id=1, source_target_pairs={{8,0},{16,8},{24,16},{32,24},{40,32},{48,40},{56,48},{64,56},{72,6... | collective-permute-start | bytes 1781768 | tf_op jit(solution)/shard_map/ppermute | solution.py:848
  41.1 17.6 %copy-start = (f32[64,32,512]{2,1,0:T(8,128)S(1)}, f32[64,32,512]{2,1,0:T(8,128)}, u32[]{:S(2)}) copy-start(f32[64,32,512]{2,1,0:T(8,128)} %us.1) | copy-start | bytes 12582916
  53.2 14.7 %collective-permute-start.5 = (f32[80,128]{1,0:T(8,128)S(1)}, f32[80,128]{1,0:T(8,128)S(1)}, u32[]{:S(2)}, u32[]{:S(2)}) collective-permute-start(f32[80,128]{1,0:T(8,128)S(1)} %get-tuple-element.34.pay_lo), channel_id=1, source_target_pairs={{1,0},{2,1},{3,2},{4,3},{5,4},{6,5},{7,6},{9,8},{10,9},{11,10},{12... | collective-permute-start | bytes 122888 | tf_op jit(solution)/shard_map/ppermute | solution.py:848
  54.5 13.4 %collective-permute-start.4 = (f32[80,128]{1,0:T(8,128)S(1)}, f32[80,128]{1,0:T(8,128)S(1)}, u32[]{:S(2)}, u32[]{:S(2)}) collective-permute-start(f32[80,128]{1,0:T(8,128)S(1)} %get-tuple-element.35.pay_hi), channel_id=1, source_target_pairs={{0,1},{1,2},{2,3},{3,4},{4,5},{5,6},{6,7},{8,9},{9,10},{10,11},{11... | collective-permute-start | bytes 122888 | tf_op jit(solution)/shard_map/ppermute | solution.py:848

commit v8 on v7

--- a/solution.py
+++ b/solution.py
@@ -29,7 +29,7 @@
 ROW_UNROLL = 16
 PLANES = 8
 CHUNK = 8
-AHEAD = 5
+AHEAD = 8
 XW = CX + 4
 BINS = 2 * XW
 PART = 128 + 8 * DEPTH
@@ -739,8 +739,8 @@
     side = jnp.where(lo_half, meta[4], meta[5])
     glow1 = glow_of(sub.astype(F32) + meta[0])
 
-    def stacks(a, b, at, size):
-        p, q = a[at : at + size], b[at : at + size]
+    def stacks(a, b, at, size, fa=1.0, fb=1.0):
+        p, q = a[at : at + size] * fa, b[at : at + size] * fb
         low = iota((size, 128), 1) < DEPTH
         return jnp.where(low, p, pltpu.roll(q, DEPTH, 1)), jnp.where(low, pltpu.roll(p, DEPTH, 1), q)
 
@@ -761,11 +761,11 @@
             total = total + flux(kh, kn, uh, un)
         return uh + total + glow1 * vh
 
-    outer = stacks(got_lo, got_hi, 40, CX)
-    here = stacks(got_lo, got_hi, 0, CX)
+    outer = stacks(got_lo, got_hi, 40, CX, meta[4], meta[5])
+    here = stacks(got_lo, got_hi, 0, CX, meta[4], meta[5])
     inner = stacks(pay_lo, pay_hi, 0, CX)
     next_in = stacks(pay_lo, pay_hi, 40, CX)
-    mid_out = column_step(outer, here, inner, stacks(got_lo, got_hi, CX, 8)) * side
+    mid_out = column_step(outer, here, inner, stacks(got_lo, got_hi, CX, 8, meta[4], meta[5])) * side
     mid_in = column_step(here, inner, next_in, stacks(pay_lo, pay_hi, CX, 8))
     sign = jnp.where(lo_half, 1.0, -1.0)
     lane8 = iota((8, 128), 1)
@@ -779,7 +779,10 @@
     weave(fix, mid_in)
     weave(col2, sign * flux(half_kappa(mid_out, here[1]), half_kappa(mid_in, inner[1]), mid_out, mid_in))
 
-    tail = [jnp.transpose(jnp.concatenate([g[CX : CX + 8]] * 16, axis=0)) for g in (got_lo, got_hi)]
+    tail = [
+        jnp.transpose(jnp.concatenate([g[CX : CX + 8] * meta[4 + i]] * 16, axis=0))
+        for i, g in enumerate((got_lo, got_hi))
+    ]
     ends = jnp.transpose(jnp.concatenate([mid_in] * 4, axis=0))
     lane_t = iota((DEPTH, 128), 1)
 
@@ -848,6 +851,11 @@
     return lax.ppermute(value, axis, [(i, i + steps) for i in range(first, stop)])
 
 
+def ring(value, axis, steps):
+    count = lax.axis_size(axis)
+    return lax.ppermute(value, axis, [(i, (i + steps) % count) for i in range(count)])
+
+
 def body(
     particle_locations,
     particle_speeds,
@@ -862,8 +870,8 @@
 ):
     states = jnp.concatenate([particle_locations, particle_speeds], axis=0)
     width = HB * 128
-    halo_lo = shift(states[:, NPART - width :], ("gx", "gy"), 1)
-    halo_hi = shift(states[:, :width], ("gx", "gy"), -1)
+    halo_lo = ring(states[:, NPART - width :], ("gx", "gy"), 1)
+    halo_hi = ring(states[:, :width], ("gx", "gy"), -1)
     urow, ucol = edges(pltpu.with_memory_space_constraint(thermal_excess, pltpu.HBM))
 
     gx, gy = lax.axis_index("gx"), lax.axis_index("gy")
@@ -882,8 +890,8 @@
     recv_hi = shift(send_lo, "gx", -1)
     pile = own_deposit(last.reshape(128), last, skey, schg)
     share, vrow, pay_lo, pay_hi = edge_deposit(meta, pile, recv_lo, recv_hi, ucol)
-    got_lo = shift(pay_hi, "gy", 1)
-    got_hi = shift(pay_lo, "gy", -1)
+    got_lo = ring(pay_hi, "gy", 1)
+    got_hi = ring(pay_lo, "gy", -1)
     mid, mpart, here = heat_one(meta, thermal_excess, pltpu.with_memory_space_constraint(share, pltpu.HBM), urow, recv_lo, recv_hi, vrow)
     final = heat_two(meta, mid, here, mpart, recv_lo, recv_hi, vrow, pay_lo, pay_hi, got_lo, got_hi)
     return nloc, nvel, share, final

time: 79.5 us -> 71.4 us (0.90)
  starting transfers between devices: 19.3 us -> 13 us
  Pallas kernels: 48.5 us -> 45.9 us
    ppermute x6 -> x2, starting transfers between devices: 19.3 us -> 5.74 us  [shift(): lax.ppermute(value, axis, [(i, i + steps) for i in range(first, stop)])]
    ppermute x0 -> x4, starting transfers between devices: none -> 7.28 us  [ring(): lax.ppermute(value, axis, [(i, (i + steps) % count) for i in range(count)])]
    ppermute x0 -> x4, waiting for transfers between devices: none -> 3.68 us  [ring(): lax.ppermute(value, axis, [(i, (i + steps) % count) for i in range(count)])]
    ppermute x6 -> x2, waiting for transfers between devices: 7.97 us -> 5.08 us  [shift(): lax.ppermute(value, axis, [(i, i + steps) for i in range(first, stop)])]
    pallas_call x1, Pallas kernels: 11.8 us -> 10.3 us  [particles(): pl.pallas_call(particle_kernel, out_shape=(sd((3, NPART), F32), sd((3, NP...]
  transfers between devices with their start and end apart: 6 -> 6, of which waited for: 2 -> 2; matrix products, arithmetic and copies ran while one was open for 0% -> 0% of each run, Pallas kernels for 24% -> 25%
where the time goes in v8:
time: 71.4 us; the launch traced here: 70.4 us
  Pallas kernels  45.9 us (64%)
  starting transfers between devices  13 us (18%)
  waiting for transfers between devices  8.76 us (12%)
  between operations  1.66 us (2%)
  other arithmetic  1.02 us (1%)
    pallas_call x1, Pallas kernels, heat_two(): pl.pallas_call(heat_two_kernel, out_shape=jax.ShapeDtypeStruct((DEPTH, CX...  10.4 us
    pallas_call x1, Pallas kernels, particles(): pl.pallas_call(particle_kernel, out_shape=(sd((3, NPART), F32), sd((3, NP...  10.3 us
    pallas_call x1, Pallas kernels, heat_one(): pl.pallas_call(heat_one_kernel, out_shape=(sd((DEPTH, CX, CY), F32), sd((...  8.83 us
    pallas_call x1, Pallas kernels, edge_deposit(): pl.pallas_call(edge_deposit_kernel, out_shape=(sd((DEPTH, CX, CY), F32),...  7.77 us
    ppermute x4, starting transfers between devices, ring(): lax.ppermute(value, axis, [(i, (i + steps) % count) for i in range(count)])  7.28 us
    pallas_call x1, Pallas kernels, own_deposit(): pl.pallas_call(own_deposit_kernel, out_shape=sd((XW, DEPTH, CY), F32), in...  6.15 us
    ppermute x2, starting transfers between devices, shift(): lax.ppermute(value, axis, [(i, i + steps) for i in range(first, stop)])  5.74 us
    ppermute x2, waiting for transfers between devices, shift(): lax.ppermute(value, axis, [(i, i + steps) for i in range(first, stop)])  5.08 us
  transfers between devices with their start and end apart: 6, of which 2 were waited for; matrix products, arithmetic and copies ran while one was open for 0% of the time, Pallas kernels for 25%

profile of v8, /device:TPU:97, one launch (start us, length us, event | category | flops | bytes accessed | tf_op | source)
XLA Modules:
  0.0 70.4 jit_solution(18324512159018907240)
XLA Ops:
  0.6 0.0 copy-start.2
  0.6 0.0 copy-start.1
  0.7 0.0 copy-start.5
  0.7 0.0 copy-start.3
  0.7 0.0 copy-start.7
  0.7 0.0 copy-start.6
  0.7 0.0 copy-start.4
  0.7 0.0 copy-start.8
  0.7 0.8 %pad_maximum_fusion = (f32[6,256]{1,0:T(8,128)S(1)}, f32[6,256]{1,0:T(8,128)S(1)}) fusion(f32[3,16384]{1,0:T(4,128)} %vel.1, f32[3,16384]{1,0:T(4,128)} %loc.1), kind=kLoop, calls=%fused_computation | loop fusion | flops 3072 | bytes 405504 | tf_op jit(solution)/shard_map/concatenate | solution.py:871
  1.5 5.7 %collective-permute-start.1 = (f32[6,256]{1,0:T(8,128)S(1)}, f32[6,256]{1,0:T(8,128)S(1)}, u32[]{:S(2)}, u32[]{:S(2)}) collective-permute-start(f32[6,256]{1,0:T(8,128)S(1)} %get-tuple-element.36), channel_id=1, source_target_pairs={{0,127},{1,0},{2,1},{3,2},{4,3},{5,4},{6,5},{7,6},{8,7},{9,8},{10,... | collective-permute-start | bytes 18440 | tf_op jit(solution)/shard_map/ppermute | solution.py:856
  7.2 0.0 collective-permute-start
  7.2 0.1 pad_add_fusion.origin
  8.0 2.5 %temperature_edges.1 = (f32[4,64,512]{2,1,0:T(8,128)S(1)}, f32[4,32,128]{2,1,0:T(8,128)S(1)}) custom-call(f32[64,32,512]{2,1,0:T(8,128)} %us.1), custom_call_target="tpu_custom_call" | custom-call | tf_op jit(solution)/shard_map/temperature_edges/pallas_call | solution.py:538
  10.5 0.0 collective-permute-done.1.halo_hi
  10.5 3.7 %collective-permute-done.halo_lo = f32[6,256]{1,0:T(8,128)S(1)} collective-permute-done((f32[6,256]{1,0:T(8,128)S(1)}, f32[6,256]{1,0:T(8,128)S(1)}, u32[]{:S(2)}, u32[]{:S(2)}) %collective-permute-start) | collective-permute-done | bytes 6176 | tf_op jit(solution)/shard_map/ppermute | solution.py:856
  14.2 0.0 copy-done.2
  14.2 0.0 copy-done.1
  14.2 0.0 copy-done.5
  14.2 0.0 copy-done.3
  14.2 0.0 copy-done.7
  14.2 0.0 copy-done.6
  14.2 0.0 copy-done.4
  14.2 10.3 %particle_step.1 = (f32[3,16384]{1,0:T(4,128)}, f32[3,16384]{1,0:T(4,128)}, s32[128,128]{1,0:T(8,128)S(1)}, f32[128,128]{1,0:T(8,128)S(1)}, s32[1,128]{1,0:T(1,1...) custom-call(s32[256]{0:T(256)S(1)} %copy-done.6, s32[256]{0:T(256)S(1)} %copy-done.7, s32[1]{0:T(128)S(6)} %copy.14.cnt, ...), custom_call_target="tpu_custom_call" | custom-call | tf_op jit(solution)/shard_map/particle_step/pallas_call | solution.py:325
  24.6 3.8 %collective-permute-start.2 = (f32[1160,128]{1,0:T(8,128)S(1)}, f32[1160,128]{1,0:T(8,128)S(1)}, u32[]{:S(2)}, u32[]{:S(2)}) collective-permute-start(f32[1160,128]{1,0:T(8,128)S(1)} %get-tuple-element.26), channel_id=1, source_target_pairs={{0,8},{8,16},{16,24},{24,32},{32,40},{40,48},{48,56},{56,64},{64,7... | collective-permute-start | bytes 1781768 | tf_op jit(solution)/shard_map/ppermute | solution.py:851
  28.4 1.9 %collective-permute-start.3 = (f32[1160,128]{1,0:T(8,128)S(1)}, f32[1160,128]{1,0:T(8,128)S(1)}, u32[]{:S(2)}, u32[]{:S(2)}) collective-permute-start(f32[1160,128]{1,0:T(8,128)S(1)} %get-tuple-element.27), channel_id=1, source_target_pairs={{8,0},{16,8},{24,16},{32,24},{40,32},{48,40},{56,48},{64,56},{72,6... | collective-permute-start | bytes 1781768 | tf_op jit(solution)/shard_map/ppermute | solution.py:851
  30.3 0.1 add_convert_fusion
  30.4 0.0 copy-done.8
  30.4 0.1 pad_maximum_fusion.2.meta
  30.5 6.1 %own_deposit.1.pile_in = f32[36,64,512]{2,1,0:T(8,128)S(1)} custom-call(s32[128]{0:T(128)S(1)} %bitcast.11, s32[1,128]{1,0:T(1,128)S(1)} %get-tuple-element.23.last_v, s32[128,128]{1,0:T(8,128)S(1)} %get-tuple-element.24.skey, f32[128,128]{1,0:T(8,128)S(1)} %get-tuple-element.25.schg), custom_call_target="tpu_custom_call" | custom-call | tf_op jit(solution)/shard_map/own_deposit/pallas_call | solution.py:378
  36.6 0.0 copy-start
  36.6 0.0 collective-permute-done.2.recv_lo
  36.7 5.1 %collective-permute-done.3.recv_hi = f32[1160,128]{1,0:T(8,128)S(1)} collective-permute-done((f32[1160,128]{1,0:T(8,128)S(1)}, f32[1160,128]{1,0:T(8,128)S(1)}, u32[]{:S(2)}, u32[]{:S(2)}) %collective-permute-start.3) | collective-permute-done | bytes 593952 | tf_op jit(solution)/shard_map/ppermute | solution.py:851
  41.7 7.8 %edge_deposit.1 = (f32[64,32,512]{2,1,0:T(8,128)}, f32[6,64,512]{2,1,0:T(8,128)S(1)}, f32[80,128]{1,0:T(8,128)S(1)}, f32[80,128]{1,0:T(8,128)S(1)}) custom-call(f32[6]{0:T(128)S(1)} %pad_maximum_fusion.2.meta, f32[36,64,512]{2,1,0:T(8,128)S(1)} %own_deposit.1.pile_in, f32[1160,128]{1,0:T(8,128)S(1)} %collective-permute-done.2.recv_lo, ...), custom_call_target="tpu_custom_call" | custom-call | tf_op jit(solution)/shard_map/edge_deposit/pallas_call | solution.py:484
  49.5 1.3 %collective-permute-start.5 = (f32[80,128]{1,0:T(8,128)S(1)}, f32[80,128]{1,0:T(8,128)S(1)}, u32[]{:S(2)}, u32[]{:S(2)}) collective-permute-start(f32[80,128]{1,0:T(8,128)S(1)} %get-tuple-element.34.pay_lo), channel_id=1, source_target_pairs={{0,7},{1,0},{2,1},{3,2},{4,3},{5,4},{6,5},{7,6},{8,15},{9,8},{10,9... | collective-permute-start | bytes 122888 | tf_op jit(solution)/shard_map/ppermute | solution.py:856
  50.9 0.2 collective-permute-start.4
  51.0 0.0 copy-done
  51.0 8.8 %heat_step_one.1 = (f32[64,32,512]{2,1,0:T(8,128)S(1)}, f32[2,64,512]{2,1,0:T(8,128)S(1)}, f32[64,32,512]{2,1,0:T(8,128)S(1)}) custom-call(f32[6]{0:T(128)S(1)} %pad_maximum_fusion.2.meta, f32[64,32,512]{2,1,0:T(8,128)S(1)} %copy-done, f32[64,32,512]{2,1,0:T(8,128)} %get-tuple-element.18.share, f32[4,64,512]{2,1,0:T(8,128)S(1)} %get-tuple-element.20.urow, ...), custom_call_target="tpu_custom_call" | custom-call | flops 33554432 | bytes 16777216 | tf_op jit(solution)/shard_map/heat_step_one/pallas_call | solution.py:716
  59.9 0.0 collective-permute-done.5.got_hi
  59.9 0.0 collective-permute-done.4.got_lo
  59.9 10.4 %heat_step_two.1 = f32[64,32,512]{2,1,0:T(8,128)} custom-call(f32[6]{0:T(128)S(1)} %pad_maximum_fusion.2.meta, f32[64,32,512]{2,1,0:T(8,128)S(1)} %get-tuple-element.31.mid, f32[64,32,512]{2,1,0:T(8,128)S(1)} %get-tuple-element.32.vs, f32[2,64,512]{2,1,0:T(8,128)S(1)} %get-tuple-element.33.mpart, f32[1160,128]{1,0:T(8,128)S(1)} %collective-permute-done.2.recv_lo, ...), custom_call_target="tpu_custom_call" | custom-call | tf_op jit(solution)/shard_map/heat_step_two/pallas_call | solution.py:831
  (1 shorter events, 0.0 us)
Async XLA Ops:
  0.6 13.5 %copy-start.2 = (f32[3,16384]{1,0:T(4,128)S(1)}, f32[3,16384]{1,0:T(4,128)}, u32[]{:S(2)}) copy-start(f32[3,16384]{1,0:T(4,128)} %vel.1) | copy-start | bytes 589828
  0.6 13.5 %copy-start.1 = (f32[3,16384]{1,0:T(4,128)S(1)}, f32[3,16384]{1,0:T(4,128)}, u32[]{:S(2)}) copy-start(f32[3,16384]{1,0:T(4,128)} %loc.1) | copy-start | bytes 589828
  0.7 13.5 %copy-start.5 = (s32[16384]{0:T(1024)S(1)}, s32[16384]{0:T(1024)}, u32[]{:S(2)}) copy-start(s32[16384]{0:T(1024)} %param.17) | copy-start | bytes 196612
  0.7 13.5 %copy-start.3 = (s32[3,16384]{1,0:T(4,128)S(1)}, s32[3,16384]{1,0:T(4,128)}, u32[]{:S(2)}) copy-start(s32[3,16384]{1,0:T(4,128)} %site.1) | copy-start | bytes 589828
  0.7 13.5 %copy-start.7 = (s32[256]{0:T(256)S(1)}, s32[256]{0:T(256)}, u32[]{:S(2)}) copy-start(s32[256]{0:T(256)} %src.1) | copy-start | bytes 3076
  0.7 13.5 %copy-start.6 = (s32[256]{0:T(256)S(1)}, s32[256]{0:T(256)}, u32[]{:S(2)}) copy-start(s32[256]{0:T(256)} %tgt.1) | copy-start | bytes 3076
  0.7 13.5 %copy-start.4 = (f32[16384]{0:T(1024)S(1)}, f32[16384]{0:T(1024)}, u32[]{:S(2)}) copy-start(f32[16384]{0:T(1024)} %param.12) | copy-start | bytes 196612
  0.7 29.7 %copy-start.8 = (s32[2]{0:T(128)S(1)}, s32[2]{0:T(128)}, u32[]{:S(2)}) copy-start(s32[2]{0:T(128)} %param.19) | copy-start | bytes 28
  1.5 9.0 %collective-permute-start.1 = (f32[6,256]{1,0:T(8,128)S(1)}, f32[6,256]{1,0:T(8,128)S(1)}, u32[]{:S(2)}, u32[]{:S(2)}) collective-permute-start(f32[6,256]{1,0:T(8,128)S(1)} %get-tuple-element.36), channel_id=1, source_target_pairs={{0,127},{1,0},{2,1},{3,2},{4,3},{5,4},{6,5},{7,6},{8,7},{9,8},{10,... | collective-permute-start | bytes 18440 | tf_op jit(solution)/shard_map/ppermute | solution.py:856
  7.2 6.9 %collective-permute-start = (f32[6,256]{1,0:T(8,128)S(1)}, f32[6,256]{1,0:T(8,128)S(1)}, u32[]{:S(2)}, u32[]{:S(2)}) collective-permute-start(f32[6,256]{1,0:T(8,128)S(1)} %get-tuple-element.37), channel_id=1, source_target_pairs={{0,1},{1,2},{2,3},{3,4},{4,5},{5,6},{6,7},{7,8},{8,9},{9,10},{10,1... | collective-permute-start | bytes 18440 | tf_op jit(solution)/shard_map/ppermute | solution.py:856
  24.6 12.1 %collective-permute-start.2 = (f32[1160,128]{1,0:T(8,128)S(1)}, f32[1160,128]{1,0:T(8,128)S(1)}, u32[]{:S(2)}, u32[]{:S(2)}) collective-permute-start(f32[1160,128]{1,0:T(8,128)S(1)} %get-tuple-element.26), channel_id=1, source_target_pairs={{0,8},{8,16},{16,24},{24,32},{32,40},{40,48},{48,56},{56,64},{64,7... | collective-permute-start | bytes 1781768 | tf_op jit(solution)/shard_map/ppermute | solution.py:851
  28.4 13.4 %collective-permute-start.3 = (f32[1160,128]{1,0:T(8,128)S(1)}, f32[1160,128]{1,0:T(8,128)S(1)}, u32[]{:S(2)}, u32[]{:S(2)}) collective-permute-start(f32[1160,128]{1,0:T(8,128)S(1)} %get-tuple-element.27), channel_id=1, source_target_pairs={{8,0},{16,8},{24,16},{32,24},{40,32},{48,40},{56,48},{64,56},{72,6... | collective-permute-start | bytes 1781768 | tf_op jit(solution)/shard_map/ppermute | solution.py:851
  36.6 14.4 %copy-start = (f32[64,32,512]{2,1,0:T(8,128)S(1)}, f32[64,32,512]{2,1,0:T(8,128)}, u32[]{:S(2)}) copy-start(f32[64,32,512]{2,1,0:T(8,128)} %us.1) | copy-start | bytes 12582916
  49.5 10.4 %collective-permute-start.5 = (f32[80,128]{1,0:T(8,128)S(1)}, f32[80,128]{1,0:T(8,128)S(1)}, u32[]{:S(2)}, u32[]{:S(2)}) collective-permute-start(f32[80,128]{1,0:T(8,128)S(1)} %get-tuple-element.34.pay_lo), channel_id=1, source_target_pairs={{0,7},{1,0},{2,1},{3,2},{4,3},{5,4},{6,5},{7,6},{8,15},{9,8},{10,9... | collective-permute-start | bytes 122888 | tf_op jit(solution)/shard_map/ppermute | solution.py:856
  50.9 9.0 %collective-permute-start.4 = (f32[80,128]{1,0:T(8,128)S(1)}, f32[80,128]{1,0:T(8,128)S(1)}, u32[]{:S(2)}, u32[]{:S(2)}) collective-permute-start(f32[80,128]{1,0:T(8,128)S(1)} %get-tuple-element.35.pay_hi), channel_id=1, source_target_pairs={{0,1},{1,2},{2,3},{3,4},{4,5},{5,6},{6,7},{7,0},{8,9},{9,10},{10,1... | collective-permute-start | bytes 122888 | tf_op jit(solution)/shard_map/ppermute | solution.py:856

commit v9 on v8

--- a/solution.py
+++ b/solution.py
@@ -405,10 +405,10 @@
         cells[at : at + RECV] = x * CY + ref[32:64].astype(I32)
 
     def profiles(i, carry):
-        for ref, at in ((recv_lo, 0), (recv_hi, RECV)):
+        for ref, at, flag in ((recv_lo, 0, meta[2]), (recv_hi, RECV, meta[3])):
             for u in range(4):
                 b = i * 4 + u
-                prof[at + b] = profile(ref[pl.ds(64 + b, 1), :], ref[pl.ds(96 + b, 1), :])
+                prof[at + b] = profile(ref[pl.ds(64 + b, 1), :], flag * ref[pl.ds(96 + b, 1), :])
         return carry
 
     lax.fori_loop(0, RECV // 4, profiles, 0)
@@ -460,8 +460,8 @@
     pick(CX + 2, CX + 1)
     base = 128 + 4 * DEPTH
     for pay, recv_col, near, far in ((pay_lo, 0, 0, 1), (pay_hi, 3, 3, 2)):
-        lo = recv_lo[base + recv_col * DEPTH : base + recv_col * DEPTH + DEPTH]
-        hi = recv_hi[128 + recv_col * DEPTH : 128 + recv_col * DEPTH + DEPTH]
+        lo = meta[2] * recv_lo[base + recv_col * DEPTH : base + recv_col * DEPTH + DEPTH]
+        hi = meta[3] * recv_hi[128 + recv_col * DEPTH : 128 + recv_col * DEPTH + DEPTH]
         by = 0 if recv_col == 0 else 1
         corner = jnp.where(lane == CX, pltpu.roll(lo, CX + by, 1), 0.0)
         corner = jnp.where(lane == CX + 1, pltpu.roll(hi, CX + 1 + by, 1), corner)
@@ -671,7 +671,8 @@
 
         def got_row(r):
             base = 128 + r * 4 * DEPTH
-            return jnp.concatenate([recv[base + c * DEPTH : base + (c + 1) * DEPTH] for c in range(4)], axis=1)
+            got = [recv[base + c * DEPTH : base + (c + 1) * DEPTH] for c in range(4)]
+            return meta[2 + n] * jnp.concatenate(got, axis=1)
 
         uo, uh = (got_row(0), got_row(1)) if n == 0 else (got_row(1), got_row(0))
         ui = urow[0] if n == 0 else urow[3]
@@ -796,7 +797,7 @@
         mi = [mid[:, x, tile(c)] for c in TILES]
         for c, at, half, g, e in ((0, 0, 0, 0, 0), (3, 127, DEPTH, 1, 127)):
             base = 128 + (r * 4 + c) * DEPTH
-            uc = recv[base : base + DEPTH]
+            uc = meta[2 + n] * recv[base : base + DEPTH]
             kc = half_kappa(uc, vh[:, tile(c)])
             ue = turned(tail[g][:DEPTH], e - n)
             ke = half_kappa(ue, turned(tail[g][DEPTH:], e - n))
@@ -843,12 +844,6 @@
         compiler_params=pltpu.CompilerParams(vmem_limit_bytes=VMEM_LIMIT),
         name="heat_step_two",
     )(meta, mid, v, mpart, recv_lo, recv_hi, vrow, pay_lo, pay_hi, got_lo, got_hi)
-
-
-def shift(value, axis, steps):
-    count = lax.axis_size(axis)
-    first, stop = max(0, -steps), min(count, count - steps)
-    return lax.ppermute(value, axis, [(i, i + steps) for i in range(first, stop)])
 
 
 def ring(value, axis, steps):
@@ -886,8 +881,8 @@
         particle_locations, particle_speeds, halo_lo, halo_hi, landing_site_triple,
         particle_bulk.reshape(128, 128), landing_weight_octants.reshape(128, 128), urow,
     )
-    recv_lo = shift(send_hi, "gx", 1)
-    recv_hi = shift(send_lo, "gx", -1)
+    recv_lo = ring(send_hi, "gx", 1)
+    recv_hi = ring(send_lo, "gx", -1)
     pile = own_deposit(last.reshape(128), last, skey, schg)
     share, vrow, pay_lo, pay_hi = edge_deposit(meta, pile, recv_lo, recv_hi, ucol)
     got_lo = ring(pay_hi, "gy", 1)

time: 71.4 us -> 69.6 us (0.975)
  the two profiles are of different devices: /device:TPU:97 before, /device:TPU:0 now
where the time goes in v9:
time: 69.6 us; the launch traced here: 69.4 us
  Pallas kernels  46.6 us (67%)
  starting transfers between devices  14.3 us (21%)
  waiting for transfers between devices  5.82 us (8%)
  between operations  1.64 us (2%)
  other arithmetic  1.02 us (1%)
    ppermute x6, starting transfers between devices, ring(): lax.ppermute(value, axis, [(i, (i + steps) % count) for i in range(count)])  14.3 us
    pallas_call x1, Pallas kernels, particles(): pl.pallas_call(particle_kernel, out_shape=(sd((3, NPART), F32), sd((3, NP...  11.8 us
    pallas_call x1, Pallas kernels, heat_two(): pl.pallas_call(heat_two_kernel, out_shape=jax.ShapeDtypeStruct((DEPTH, CX...  10.4 us
    pallas_call x1, Pallas kernels, heat_one(): pl.pallas_call(heat_one_kernel, out_shape=(sd((DEPTH, CX, CY), F32), sd((...  8.81 us
    pallas_call x1, Pallas kernels, own_deposit(): pl.pallas_call(own_deposit_kernel, out_shape=sd((XW, DEPTH, CY), F32), in...  6.87 us
    pallas_call x1, Pallas kernels, edge_deposit(): pl.pallas_call(edge_deposit_kernel, out_shape=(sd((DEPTH, CX, CY), F32),...  6.31 us
    ppermute x6, waiting for transfers between devices, ring(): lax.ppermute(value, axis, [(i, (i + steps) % count) for i in range(count)])  5.82 us
    pallas_call x1, Pallas kernels, edges(): pl.pallas_call(edges_kernel, out_shape=(sd((4, DEPTH, CY), F32), sd((4, C...  2.49 us
  transfers between devices with their start and end apart: 6, of which 2 were waited for; matrix products, arithmetic and copies ran while one was open for 0% of the time, Pallas kernels for 26%

profile of v9, /device:TPU:0, one launch (start us, length us, event | category | flops | bytes accessed | tf_op | source)
XLA Modules:
  0.0 69.4 jit_solution(18389612467879578370)
XLA Ops:
  0.6 0.0 copy-start.2
  0.6 0.0 copy-start.1
  0.7 0.0 copy-start.5
  0.7 0.0 copy-start.3
  0.7 0.0 copy-start.7
  0.7 0.0 copy-start.6
  0.7 0.0 copy-start.4
  0.7 0.0 copy-start.8
  0.7 0.8 %pad_maximum_fusion = (f32[6,256]{1,0:T(8,128)S(1)}, f32[6,256]{1,0:T(8,128)S(1)}) fusion(f32[3,16384]{1,0:T(4,128)} %vel.1, f32[3,16384]{1,0:T(4,128)} %loc.1), kind=kLoop, calls=%fused_computation | loop fusion | flops 3072 | bytes 405504 | tf_op jit(solution)/shard_map/concatenate | solution.py:866
  1.5 8.3 %collective-permute-start.1 = (f32[6,256]{1,0:T(8,128)S(1)}, f32[6,256]{1,0:T(8,128)S(1)}, u32[]{:S(2)}, u32[]{:S(2)}) collective-permute-start(f32[6,256]{1,0:T(8,128)S(1)} %get-tuple-element.36), channel_id=1, source_target_pairs={{0,127},{1,0},{2,1},{3,2},{4,3},{5,4},{6,5},{7,6},{8,7},{9,8},{10,... | collective-permute-start | bytes 18440 | tf_op jit(solution)/shard_map/ppermute | solution.py:851
  9.8 0.0 collective-permute-start
  9.8 0.1 pad_add_fusion.origin
  10.5 2.5 %temperature_edges.1 = (f32[4,64,512]{2,1,0:T(8,128)S(1)}, f32[4,32,128]{2,1,0:T(8,128)S(1)}) custom-call(f32[64,32,512]{2,1,0:T(8,128)} %us.1), custom_call_target="tpu_custom_call" | custom-call | tf_op jit(solution)/shard_map/temperature_edges/pallas_call | solution.py:538
  13.0 0.0 collective-permute-done.1.halo_hi
  13.0 5.3 %collective-permute-done.halo_lo = f32[6,256]{1,0:T(8,128)S(1)} collective-permute-done((f32[6,256]{1,0:T(8,128)S(1)}, f32[6,256]{1,0:T(8,128)S(1)}, u32[]{:S(2)}, u32[]{:S(2)}) %collective-permute-start) | collective-permute-done | bytes 6176 | tf_op jit(solution)/shard_map/ppermute | solution.py:851
  18.3 0.0 copy-done.2
  18.3 0.0 copy-done.1
  18.3 0.0 copy-done.5
  18.3 0.0 copy-done.3
  18.3 0.0 copy-done.7
  18.3 0.0 copy-done.6
  18.3 0.0 copy-done.4
  18.3 11.8 %particle_step.1 = (f32[3,16384]{1,0:T(4,128)}, f32[3,16384]{1,0:T(4,128)}, s32[128,128]{1,0:T(8,128)S(1)}, f32[128,128]{1,0:T(8,128)S(1)}, s32[1,128]{1,0:T(1,1...) custom-call(s32[256]{0:T(256)S(1)} %copy-done.6, s32[256]{0:T(256)S(1)} %copy-done.7, s32[1]{0:T(128)S(6)} %copy.14.cnt, ...), custom_call_target="tpu_custom_call" | custom-call | tf_op jit(solution)/shard_map/particle_step/pallas_call | solution.py:325
  30.1 0.1 collective-permute-start.2
  30.2 3.8 %collective-permute-start.3 = (f32[1160,128]{1,0:T(8,128)S(1)}, f32[1160,128]{1,0:T(8,128)S(1)}, u32[]{:S(2)}, u32[]{:S(2)}) collective-permute-start(f32[1160,128]{1,0:T(8,128)S(1)} %get-tuple-element.27), channel_id=1, source_target_pairs={{0,120},{8,0},{16,8},{24,16},{32,24},{40,32},{48,40},{56,48},{64,5... | collective-permute-start | bytes 1781768 | tf_op jit(solution)/shard_map/ppermute | solution.py:851
  34.0 0.1 add_convert_fusion
  34.1 0.0 copy-done.8
  34.1 0.1 pad_maximum_fusion.2.meta
  34.2 6.9 %own_deposit.1.pile_in = f32[36,64,512]{2,1,0:T(8,128)S(1)} custom-call(s32[128]{0:T(128)S(1)} %bitcast.11, s32[1,128]{1,0:T(1,128)S(1)} %get-tuple-element.23.last_v, s32[128,128]{1,0:T(8,128)S(1)} %get-tuple-element.24.skey, f32[128,128]{1,0:T(8,128)S(1)} %get-tuple-element.25.schg), custom_call_target="tpu_custom_call" | custom-call | tf_op jit(solution)/shard_map/own_deposit/pallas_call | solution.py:378
  41.1 0.0 copy-start
  41.1 0.5 collective-permute-done.2.recv_lo
  41.6 0.0 collective-permute-done.3.recv_hi
  41.6 6.3 %edge_deposit.1 = (f32[64,32,512]{2,1,0:T(8,128)}, f32[6,64,512]{2,1,0:T(8,128)S(1)}, f32[80,128]{1,0:T(8,128)S(1)}, f32[80,128]{1,0:T(8,128)S(1)}) custom-call(f32[6]{0:T(128)S(1)} %pad_maximum_fusion.2.meta, f32[36,64,512]{2,1,0:T(8,128)S(1)} %own_deposit.1.pile_in, f32[1160,128]{1,0:T(8,128)S(1)} %collective-permute-done.2.recv_lo, ...), custom_call_target="tpu_custom_call" | custom-call | tf_op jit(solution)/shard_map/edge_deposit/pallas_call | solution.py:484
  47.9 0.1 collective-permute-start.5
  48.0 2.0 %collective-permute-start.4 = (f32[80,128]{1,0:T(8,128)S(1)}, f32[80,128]{1,0:T(8,128)S(1)}, u32[]{:S(2)}, u32[]{:S(2)}) collective-permute-start(f32[80,128]{1,0:T(8,128)S(1)} %get-tuple-element.35.pay_hi), channel_id=1, source_target_pairs={{0,1},{1,2},{2,3},{3,4},{4,5},{5,6},{6,7},{7,0},{8,9},{9,10},{10,1... | collective-permute-start | bytes 122888 | tf_op jit(solution)/shard_map/ppermute | solution.py:851
  50.0 0.0 copy-done
  50.0 8.8 %heat_step_one.1 = (f32[64,32,512]{2,1,0:T(8,128)S(1)}, f32[2,64,512]{2,1,0:T(8,128)S(1)}, f32[64,32,512]{2,1,0:T(8,128)S(1)}) custom-call(f32[6]{0:T(128)S(1)} %pad_maximum_fusion.2.meta, f32[64,32,512]{2,1,0:T(8,128)S(1)} %copy-done, f32[64,32,512]{2,1,0:T(8,128)} %get-tuple-element.18.share, f32[4,64,512]{2,1,0:T(8,128)S(1)} %get-tuple-element.20.urow, ...), custom_call_target="tpu_custom_call" | custom-call | flops 33554432 | bytes 16777216 | tf_op jit(solution)/shard_map/heat_step_one/pallas_call | solution.py:717
  58.9 0.0 collective-permute-done.5.got_hi
  58.9 0.0 collective-permute-done.4.got_lo
  58.9 10.4 %heat_step_two.1 = f32[64,32,512]{2,1,0:T(8,128)} custom-call(f32[6]{0:T(128)S(1)} %pad_maximum_fusion.2.meta, f32[64,32,512]{2,1,0:T(8,128)S(1)} %get-tuple-element.31.mid, f32[64,32,512]{2,1,0:T(8,128)S(1)} %get-tuple-element.32.vs, f32[2,64,512]{2,1,0:T(8,128)S(1)} %get-tuple-element.33.mpart, f32[1160,128]{1,0:T(8,128)S(1)} %collective-permute-done.2.recv_lo, ...), custom_call_target="tpu_custom_call" | custom-call | tf_op jit(solution)/shard_map/heat_step_two/pallas_call | solution.py:832
  (1 shorter events, 0.0 us)
Async XLA Ops:
  0.6 17.7 %copy-start.2 = (f32[3,16384]{1,0:T(4,128)S(1)}, f32[3,16384]{1,0:T(4,128)}, u32[]{:S(2)}) copy-start(f32[3,16384]{1,0:T(4,128)} %vel.1) | copy-start | bytes 589828
  0.6 17.6 %copy-start.1 = (f32[3,16384]{1,0:T(4,128)S(1)}, f32[3,16384]{1,0:T(4,128)}, u32[]{:S(2)}) copy-start(f32[3,16384]{1,0:T(4,128)} %loc.1) | copy-start | bytes 589828
  0.7 17.6 %copy-start.5 = (s32[16384]{0:T(1024)S(1)}, s32[16384]{0:T(1024)}, u32[]{:S(2)}) copy-start(s32[16384]{0:T(1024)} %param.17) | copy-start | bytes 196612
  0.7 17.6 %copy-start.3 = (s32[3,16384]{1,0:T(4,128)S(1)}, s32[3,16384]{1,0:T(4,128)}, u32[]{:S(2)}) copy-start(s32[3,16384]{1,0:T(4,128)} %site.1) | copy-start | bytes 589828
  0.7 17.6 %copy-start.7 = (s32[256]{0:T(256)S(1)}, s32[256]{0:T(256)}, u32[]{:S(2)}) copy-start(s32[256]{0:T(256)} %src.1) | copy-start | bytes 3076
  0.7 17.6 %copy-start.6 = (s32[256]{0:T(256)S(1)}, s32[256]{0:T(256)}, u32[]{:S(2)}) copy-start(s32[256]{0:T(256)} %tgt.1) | copy-start | bytes 3076
  0.7 17.6 %copy-start.4 = (f32[16384]{0:T(1024)S(1)}, f32[16384]{0:T(1024)}, u32[]{:S(2)}) copy-start(f32[16384]{0:T(1024)} %param.12) | copy-start | bytes 196612
  0.7 33.4 %copy-start.8 = (s32[2]{0:T(128)S(1)}, s32[2]{0:T(128)}, u32[]{:S(2)}) copy-start(s32[2]{0:T(128)} %param.19) | copy-start | bytes 28
  1.5 11.5 %collective-permute-start.1 = (f32[6,256]{1,0:T(8,128)S(1)}, f32[6,256]{1,0:T(8,128)S(1)}, u32[]{:S(2)}, u32[]{:S(2)}) collective-permute-start(f32[6,256]{1,0:T(8,128)S(1)} %get-tuple-element.36), channel_id=1, source_target_pairs={{0,127},{1,0},{2,1},{3,2},{4,3},{5,4},{6,5},{7,6},{8,7},{9,8},{10,... | collective-permute-start | bytes 18440 | tf_op jit(solution)/shard_map/ppermute | solution.py:851
  9.8 8.5 %collective-permute-start = (f32[6,256]{1,0:T(8,128)S(1)}, f32[6,256]{1,0:T(8,128)S(1)}, u32[]{:S(2)}, u32[]{:S(2)}) collective-permute-start(f32[6,256]{1,0:T(8,128)S(1)} %get-tuple-element.37), channel_id=1, source_target_pairs={{0,1},{1,2},{2,3},{3,4},{4,5},{5,6},{6,7},{7,8},{8,9},{9,10},{10,1... | collective-permute-start | bytes 18440 | tf_op jit(solution)/shard_map/ppermute | solution.py:851
  30.1 11.5 %collective-permute-start.2 = (f32[1160,128]{1,0:T(8,128)S(1)}, f32[1160,128]{1,0:T(8,128)S(1)}, u32[]{:S(2)}, u32[]{:S(2)}) collective-permute-start(f32[1160,128]{1,0:T(8,128)S(1)} %get-tuple-element.26), channel_id=1, source_target_pairs={{0,8},{8,16},{16,24},{24,32},{32,40},{40,48},{48,56},{56,64},{64,7... | collective-permute-start | bytes 1781768 | tf_op jit(solution)/shard_map/ppermute | solution.py:851
  30.2 11.5 %collective-permute-start.3 = (f32[1160,128]{1,0:T(8,128)S(1)}, f32[1160,128]{1,0:T(8,128)S(1)}, u32[]{:S(2)}, u32[]{:S(2)}) collective-permute-start(f32[1160,128]{1,0:T(8,128)S(1)} %get-tuple-element.27), channel_id=1, source_target_pairs={{0,120},{8,0},{16,8},{24,16},{32,24},{40,32},{48,40},{56,48},{64,5... | collective-permute-start | bytes 1781768 | tf_op jit(solution)/shard_map/ppermute | solution.py:851
  41.1 9.0 %copy-start = (f32[64,32,512]{2,1,0:T(8,128)S(1)}, f32[64,32,512]{2,1,0:T(8,128)}, u32[]{:S(2)}) copy-start(f32[64,32,512]{2,1,0:T(8,128)} %us.1) | copy-start | bytes 12582916
  47.9 10.9 %collective-permute-start.5 = (f32[80,128]{1,0:T(8,128)S(1)}, f32[80,128]{1,0:T(8,128)S(1)}, u32[]{:S(2)}, u32[]{:S(2)}) collective-permute-start(f32[80,128]{1,0:T(8,128)S(1)} %get-tuple-element.34.pay_lo), channel_id=1, source_target_pairs={{0,7},{1,0},{2,1},{3,2},{4,3},{5,4},{6,5},{7,6},{8,15},{9,8},{10,9... | collective-permute-start | bytes 122888 | tf_op jit(solution)/shard_map/ppermute | solution.py:851
  48.0 10.8 %collective-permute-start.4 = (f32[80,128]{1,0:T(8,128)S(1)}, f32[80,128]{1,0:T(8,128)S(1)}, u32[]{:S(2)}, u32[]{:S(2)}) collective-permute-start(f32[80,128]{1,0:T(8,128)S(1)} %get-tuple-element.35.pay_hi), channel_id=1, source_target_pairs={{0,1},{1,2},{2,3},{3,4},{4,5},{5,6},{6,7},{7,0},{8,9},{9,10},{10,1... | collective-permute-start | bytes 122888 | tf_op jit(solution)/shard_map/ppermute | solution.py:851
